TPU v7x, 32 devices: a whole 2x2x4 slice. The times are simulated.
32 devices in a mesh: tile: 8 (over y, x, core), fsdp: 4 (over z).
Axes of the slice: x: 2, y: 2, z: 4, core: 2. Of those that a mesh axis runs over, the one named last changes fastest.
Arguments:
- tiles_in: bfloat16 [64, 32, 32, 256], P(('tile', 'fsdp')), may hold values from -6 to 6
- first_weight: bfloat16 [512, 2304], P('fsdp'), may hold values from -0.125 to 0.125
- first_bias: float32 [512], replicated, may hold values from -3 to 3
- second_weight: bfloat16 [512, 4608], P('fsdp'), may hold values from -0.09375 to 0.09375
- second_bias: float32 [512], replicated, may hold values from -3 to 3
- side_links: int32 [64, 4, 3], P(('tile', 'fsdp')), may hold values from 0 to 63, as said below
- corner_links: int32 [64, 4, 3], P(('tile', 'fsdp')), may hold values from 0 to 63, as said below
Outputs:
- pooled: bfloat16 [64, 16, 16, 512], P(('tile', 'fsdp'))
Inputs may be any that keep to these rules, and one draw needn't show every extreme that they name: `side_links`: the tile across side s (0 north, 1 east, 2 south, 3 west) of a tile lies on the device one step in that direction, with wrap, in the grid whose rows are the tile index and whose columns are the fsdp index; a tile id g lies on the device numbered g // 2 with the fsdp index fastest. The second entry is a side 0..3, the third a flag 0 or 1. `corner_links`: the tile at corner c (0 north-west, 1 north-east, 2 south-east, 3 south-west) lies on the diagonal device in that direction, with wrap, in the same grid; the second entry is a corner 0..3, the third is 1 where four or five tiles meet and 0 where three meet.
All inputs are finite; a program needn't handle non-finite values.
Results may differ from a plain program's by a relative error of at most 0.0031.
Values may be sent and summed in bfloat16 or wider, within the bound.
No kernel may reach another device: no remote copies, remote signals or barrier semaphores. Data moves between devices by JAX's collectives and lax.ppermute only.
A program may use at most 384 MiB of HBM per device.

v0:
```python
import functools

import jax
import jax.numpy as jnp
from jax import lax
from jax.experimental import pallas as pl
from jax.experimental.pallas import tpu as pltpu
from jax.sharding import PartitionSpec as P


AXES = ("tile", "fsdp")
PAD = 16


def move(x, target):
    rows, cols = (lax.axis_size("tile"), lax.axis_size("fsdp"))
    pairs = []
    for t in range(rows):
        for f in range(cols):
            there_t, there_f = target(t, f)
            pairs.append((t * cols + f, (there_t % rows) * cols + there_f % cols))
    return lax.ppermute(x, AXES, pairs)


def shift(x, rows, cols):
    return move(x, lambda t, f: (t + rows, f + cols))


def gather_rows(weight):
    rows, cols = (lax.axis_size("tile"), lax.axis_size("fsdp"))
    tall = rows // 4
    share = weight.shape[0] // rows
    width = weight.shape[1]
    parts = weight.reshape(rows, share, width)
    mine = lax.dynamic_index_in_dim(parts, lax.axis_index("tile"), 0, keepdims=True)
    unit = jnp.concatenate([shift(mine, 0, k) for k in range(1, cols)], axis=0)
    near = [unit]
    for step in range(1, 2 * tall):
        dy, dx = divmod(step, 2)
        near.append(
            move(
                unit, lambda t, f: (((t // 4 + dy) % tall) * 4 + ((t // 2 % 2) ^ dx) * 2 + t % 2, f)
            )
        )
    other = [move(x, lambda t, f: (t ^ 1, f)) for x in near]
    return near + other


def place(weight, pieces):
    rows, cols = (lax.axis_size("tile"), lax.axis_size("fsdp"))
    tall = rows // 4
    share, width = pieces[0].shape[1:]
    t, f = (lax.axis_index("tile"), lax.axis_index("fsdp"))
    pieces = jnp.concatenate(pieces, axis=0)
    source_f = jnp.arange(cols)[:, None]
    source_t = jnp.arange(rows)[None, :]
    core = (source_t ^ t) & 1
    dx = ((source_t ^ t) >> 1) & 1
    dy = (t // 4 - source_t // 4) % tall
    hop = (f - source_f) % cols
    index = (core * 2 * tall + dy * 2 + dx) * (cols - 1) + hop - 1
    index = jnp.where(hop == 0, 0, index)
    whole = jnp.take(pieces, index.reshape(-1), axis=0).reshape(cols, rows * share, width)
    whole = lax.dynamic_update_index_in_dim(whole, weight, f, 0)
    return whole.reshape(-1, width)


def gelu(x):
    return 0.5 * x * (1.0 + lax.erf(x * (0.5**0.5)))


def one_hot(rows, width, target):
    n = lax.broadcasted_iota(jnp.int32, (rows, width), 0)
    return jnp.where(lax.broadcasted_iota(jnp.int32, (rows, width), 1) == target(n), 1.0, 0.0).astype(
        jnp.bfloat16
    )


def select(picker, values):
    return jnp.dot(picker, values, preferred_element_type=jnp.float32)


def put_borders(bundle, tile, half, chunk, edge):
    rows = edge // 2
    sides = one_hot(
        edge, rows * edge, lambda n: jnp.where(n < rows, n * edge, (n - rows) * edge + edge - 1)
    )
    sides = select(sides, chunk).astype(jnp.bfloat16)
    start = tile * 4 * edge
    bundle[pl.ds(start + 3 * edge + half * rows, rows), :] = sides[:rows]
    bundle[pl.ds(start + edge + half * rows, rows), :] = sides[rows:]
    if half == 0:
        bundle[pl.ds(start, edge), :] = chunk[:edge]
    else:
        bundle[pl.ds(start + 2 * edge, edge), :] = chunk[-edge:]


def put_corners(bundle, tiles, edge):
    def source(n):
        corner = n & 3
        across = jnp.where((corner == 1) | (corner == 2), edge - 1, 0)
        return (n >> 2) * 4 * edge + jnp.where(corner >= 2, 2 * edge, 0) + across

    strips = tiles * 4 * edge
    cells = select(one_hot(PAD, strips, source), bundle[:strips, :])
    bundle[strips:, :] = cells.astype(jnp.bfloat16)


def borders_kernel(field, bundle):
    tiles, edge, _, channels = field.shape
    for tile in range(tiles):
        for half in range(2):
            rows = edge // 2
            chunk = field[tile, half * rows : (half + 1) * rows].reshape(rows * edge, channels)
            put_borders(bundle, tile, half, chunk, edge)
    put_corners(bundle, tiles, edge)


def borders(field):
    tiles, edge, _, channels = field.shape
    return pl.pallas_call(
        borders_kernel,
        out_shape=jax.ShapeDtypeStruct((tiles * 4 * edge + PAD, channels), jnp.bfloat16),
        name="borders",
    )(field)


def surround(field, near, side_links, corner_links, halos, wide):
    tiles, edge, _, channels = field.shape
    strips = tiles * 4 * edge
    column = lax.broadcasted_iota(jnp.int32, (edge, channels), 0)

    def put(tile, row, middle, before, after):
        spread = middle.astype(jnp.float32)
        left = jnp.where(column == 0, before, pltpu.roll(spread, 1, 0))
        right = jnp.where(column == edge - 1, after, pltpu.roll(spread, edge - 1, 0))
        wide[tile, row, :, :channels] = left.astype(jnp.bfloat16)
        wide[tile, row, :, channels : 2 * channels] = middle.astype(jnp.bfloat16)
        wide[tile, row, :, 2 * channels :] = right.astype(jnp.bfloat16)

    for tile in range(tiles):
        for side in range(4):
            link = (tile * 4 + side) * 3
            home = lax.rem(side_links[link], tiles) * 4 + side_links[link + 1]
            turns = (
                (1 if side >= 2 else 0)
                + jnp.where(side_links[link + 1] >= 2, 1, 0)
                + jnp.where(side_links[link + 2] == 1, 0, 1)
            )
            forward = lax.rem(turns, 2) == 0
            first = home * edge + jnp.where(forward, 0, edge - 1)
            step = jnp.where(forward, 1, -1)
            picker = one_hot(edge, strips, lambda n: first + step * n)
            halos[tile, side] = select(picker, near[side][:strips, :])
        cells = []
        for corner, (source, low) in enumerate(((3, 0), (1, 0), (1, PAD), (3, PAD))):
            link = (tile * 4 + corner) * 3
            pick = lax.rem(corner_links[link], tiles) * 4 + corner_links[link + 1]
            pick = jnp.where(corner_links[link + 2] == 1, pick, -1)
            picker = one_hot(8, PAD, lambda n: pick)
            cells.append(select(picker, near[source][strips + low : strips + low + PAD, :])[:1])
        put(tile, 0, halos[tile, 0], cells[0], cells[1])
        put(tile, edge + 1, halos[tile, 2], cells[3], cells[2])

        @pl.loop(0, edge // 4)
        def _(block):
            for offset in range(4):
                row = block * 4 + offset
                before = halos[tile, 3, pl.ds(row, 1), :]
                after = halos[tile, 1, pl.ds(row, 1), :]
                put(tile, row + 1, field[tile, row], before, after)


def fetch_weight(sources, whole, place_of, sems):
    copies = []
    if len(sources) == 1:
        copies.append(pltpu.make_async_copy(sources[0], whole, sems.at[0]))
    else:
        own, *pieces = sources
        hops, share, _ = pieces[0].shape
        steps = len(pieces) // 2
        cols = hops + 1
        rows = own.shape[0] // share
        t, f = (place_of[0], place_of[1])
        tall = steps // 2
        copies.append(
            pltpu.make_async_copy(
                own, whole.at[pl.ds(pl.multiple_of(f * rows * share, share), rows * share)], sems.at[0]
            )
        )
        for core in range(2):
            for step in range(steps):
                dy, dx = divmod(step, 2)
                far_y = lax.rem(t // 4 + tall - dy, tall)
                far_x = lax.rem(t // 2 + dx, 2)
                far = far_y * 4 + far_x * 2 + lax.rem(t + core, 2)
                for hop in range(1, cols):
                    far_f = lax.rem(f + cols - hop, cols)
                    start = pl.multiple_of((far_f * rows + far) * share, share)
                    copies.append(
                        pltpu.make_async_copy(
                            pieces[core * steps + step].at[hop - 1], whole.at[pl.ds(start, share)], sems.at[len(copies)]
                        )
                    )
    for copy in copies:
        copy.start()
    return copies


def conv_kernel(count, pooling, *refs):
    place_of, side_links, corner_links, field, north, east, south, west, bias = refs[:9]
    sources = refs[9 : 9 + count]
    outs = refs[9 + count : -5]
    halos, wide, whole, sems, total = refs[-5:]
    tiles, edge, _, channels = field.shape
    copies = fetch_weight(sources, whole, place_of, sems)
    surround(field, (north, east, south, west), side_links, corner_links, halos, wide)
    for copy in copies:
        copy.wait()
    rows = edge // 2
    depth = 3 * channels
    for tile in range(tiles):
        for half in range(2):
            low = half * rows
            summed = bias[...]
            for tap in range(3):
                window = wide[tile, low + tap : low + tap + rows].reshape(rows * edge, depth)
                summed = summed + lax.dot_general(
                    window,
                    whole[:, tap * depth : (tap + 1) * depth],
                    (((1,), (1,)), ((), ())),
                    preferred_element_type=jnp.float32,
                )
            act = gelu(summed)
            if pooling:
                width = act.shape[1]
                act = act.reshape(rows // 2, 2, edge, width)
                act = (act[:, 0] + act[:, 1]).reshape(rows // 2 * edge, width)
                mean = []
                for lanes in range(0, width, 128):
                    total[...] = act[:, lanes : lanes + 128]
                    even = total[pl.ds(0, rows * edge // 4, stride=2), :]
                    odd = total[pl.ds(1, rows * edge // 4, stride=2), :]
                    mean.append(((even + odd) * 0.25).astype(jnp.bfloat16))
                mean = jnp.concatenate(mean, axis=1)
                outs[0][tile, low // 2 : (low + rows) // 2] = mean.reshape(rows // 2, edge // 2, width)
            else:
                hidden = act.astype(jnp.bfloat16)
                outs[0][tile, low : low + rows] = hidden.reshape(rows, edge, act.shape[1])
                put_borders(outs[1], tile, half, hidden, edge)
    if not pooling:
        put_corners(outs[1], tiles, edge)


def conv(field, near, place_of, side_links, corner_links, bias, sources, pooling):
    tiles, edge, _, channels = field.shape
    width = bias.shape[0]
    if pooling:
        outs = (jax.ShapeDtypeStruct((tiles, edge // 2, edge // 2, width), jnp.bfloat16),)
    else:
        outs = (
            jax.ShapeDtypeStruct((tiles, edge, edge, width), jnp.bfloat16),
            jax.ShapeDtypeStruct((tiles * 4 * edge + PAD, width), jnp.bfloat16),
        )
    vmem = pl.BlockSpec(memory_space=pltpu.VMEM)
    smem = pl.BlockSpec(memory_space=pltpu.SMEM)
    anywhere = pl.BlockSpec(memory_space=pl.ANY)
    copies = 1 + sum(piece.shape[0] for piece in sources[1:])
    flops = 2 * tiles * edge * edge * 9 * channels * width
    return pl.pallas_call(
        functools.partial(conv_kernel, len(sources), pooling),
        out_shape=outs,
        in_specs=[smem] * 3 + [vmem] * 6 + [anywhere] * len(sources),
        out_specs=[vmem] * len(outs),
        scratch_shapes=[
            pltpu.VMEM((tiles, 4, edge, channels), jnp.float32),
            pltpu.VMEM((tiles, edge + 2, edge, 3 * channels), jnp.bfloat16),
            pltpu.VMEM((width, 9 * channels), jnp.bfloat16),
            pltpu.SemaphoreType.DMA((copies,)),
            pltpu.VMEM((edge * edge // 4, 128), jnp.float32),
        ],
        cost_estimate=pl.CostEstimate(flops=flops, bytes_accessed=8 << 20, transcendentals=0),
        name="second" if pooling else "first",
    )(
        place_of,
        side_links.reshape(-1),
        corner_links.reshape(-1),
        field,
        *near,
        bias.reshape(1, width),
        *sources,
    )


def exchange(bundle):
    north = shift(bundle, 1, 0)
    south = shift(bundle, -1, 0)
    strips = bundle.shape[0] - PAD
    bundle = jnp.concatenate([bundle[:strips], north[strips:], south[strips:]], axis=0)
    west = shift(bundle, 0, 1)
    east = shift(bundle, 0, -1)
    return north, east, south, west


def sources_of(weight):
    pieces = gather_rows(weight)
    if pieces[0].shape[1] % 16 == 0:
        return (weight, *pieces)
    return (place(weight, pieces),)


def shards(
    tiles_in, first_weight, first_bias, second_weight, second_bias, side_links, corner_links
):
    place_of = jnp.stack([lax.axis_index("tile"), lax.axis_index("fsdp")])
    first = sources_of(first_weight)
    second = sources_of(second_weight)
    links = (place_of, side_links, corner_links)
    bundle = borders(tiles_in)
    near = exchange(bundle)
    hidden, bundle = conv(tiles_in, near, *links, first_bias, first, False)
    near = exchange(bundle)
    return conv(hidden, near, *links, second_bias, second, True)[0]


def solution(mesh):
    placed = (
        P(AXES, None, None, None),
        P("fsdp", None),
        P(),
        P("fsdp", None),
        P(),
        P(AXES, None, None),
        P(AXES, None, None),
    )
    return jax.shard_map(
        shards,
        mesh=mesh,
        in_specs=placed,
        out_specs=P(AXES, None, None, None),
        check_vma=False,
    )
```

profile of v0, /device:TPU:0, one launch (start us, length us, event | category | flops | bytes accessed | tf_op | source)
XLA Modules:
  0.0 106.8 jit_solution(15497778590188836478)
XLA Ops:
  0.0 0.9 constant_dynamic-slice_fusion.1
  0.9 5.1 %collective-permute-start.6 = (bf16[1,16,2304]{2,1,0:T(8,128)(2,1)S(1)}, bf16[1,16,2304]{2,1,0:T(8,128)(2,1)S(1)}, u32[]{:S(2)}, u32[]{:S(2)}) collective-permute-start(bf16[1,16,2304]{2,1,0:T(8,128)(2,1)S(1)} %constant_dynamic-slice_fusion.1), channel_id=1, source_target_pairs={{0,3},{1,0},{2,1},{3,2},{4,7},{5,4},{6,5},{7,6},{8,11},{9,8},{10,9... | collective-permute-start | bytes 221192 | tf_op jit(solution)/shard_map/ppermute | solution.py:22
  6.0 0.0 collective-permute-start.5
  6.0 1.0 collective-permute-start.4
  7.0 2.3 %borders.1 = bf16[272,256]{1,0:T(8,128)(2,1)} custom-call(bf16[2,32,32,256]{3,2,1,0:T(8,128)(2,1)} %refs_3_.1), custom_call_target="tpu_custom_call" | custom-call | tf_op jit(solution)/shard_map/borders/pallas_call | solution.py:121
  9.3 1.0 collective-permute-start.1
  10.4 0.0 collective-permute-start
  10.4 0.9 slice.24
  11.3 0.1 copy.10
  11.4 0.6 reshape.20.refs_1_
  12.0 0.1 copy.11
  12.1 0.7 reshape.21.refs_2_
  12.8 0.9 constant_dynamic-slice_fusion
  13.7 0.6 pad_add_fusion.refs_0_
  14.3 0.0 collective-permute-done.4
  14.3 3.1 %collective-permute-start.20 = (bf16[1,16,4608]{2,1,0:T(8,128)(2,1)S(1)}, bf16[1,16,4608]{2,1,0:T(8,128)(2,1)S(1)}, u32[]{:S(2)}, u32[]{:S(2)}) collective-permute-start(bf16[1,16,4608]{2,1,0:T(8,128)(2,1)S(1)} %constant_dynamic-slice_fusion), channel_id=1, source_target_pairs={{0,3},{1,0},{2,1},{3,2},{4,7},{5,4},{6,5},{7,6},{8,11},{9,8},{10,9... | collective-permute-start | bytes 442376 | tf_op jit(solution)/shard_map/ppermute | solution.py:22
  17.4 0.0 collective-permute-done.5
  17.4 0.9 collective-permute-start.19
  18.3 0.0 collective-permute-done.6
  18.4 0.3 collective-permute-start.18
  18.7 0.0 collective-permute-done.1.refs_6_
  18.7 1.7 %collective-permute-start.9 = (bf16[3,16,2304]{2,1,0:T(8,128)(2,1)S(1)}, bf16[3,16,2304]{2,1,0:T(8,128)(2,1)S(1)}, u32[]{:S(2)}, u32[]{:S(2)}) collective-permute-start(bf16[3,16,2304]{2,1,0:T(8,128)(2,1)S(1)} %constant_dynamic-update-slice_fusion.refs_10_), channel_id=1, source_target_pairs={{0,24},{1,25},{2,26},{3,27},{4,28},{5,29},{6,30},{7,31},{8,16},{9,... | collective-permute-start | bytes 663560 | tf_op jit(solution)/shard_map/ppermute | solution.py:22
  20.4 0.0 collective-permute-done.refs_4_
  20.4 0.5 collective-permute-start.8
  20.9 7.5 %collective-permute-done.18 = bf16[1,16,4608]{2,1,0:T(8,128)(2,1)S(1)} collective-permute-done((bf16[1,16,4608]{2,1,0:T(8,128)(2,1)S(1)}, bf16[1,16,4608]{2,1,0:T(8,128)(2,1)S(1)}, u32[]{:S(2)}, u32[]{:S(2)}) %collective-permute-start.18) | collective-permute-done | bytes 147488 | tf_op jit(solution)/shard_map/ppermute | solution.py:22
  28.4 0.9 collective-permute-start.7
  29.3 2.8 %collective-permute-done.19 = bf16[1,16,4608]{2,1,0:T(8,128)(2,1)S(1)} collective-permute-done((bf16[1,16,4608]{2,1,0:T(8,128)(2,1)S(1)}, bf16[1,16,4608]{2,1,0:T(8,128)(2,1)S(1)}, u32[]{:S(2)}, u32[]{:S(2)}) %collective-permute-start.19) | collective-permute-done | bytes 147488 | tf_op jit(solution)/shard_map/ppermute | solution.py:22
  32.0 0.9 collective-permute-start.3
  32.9 0.0 collective-permute-done.20
  32.9 0.1 collective-permute-start.10
  33.0 6.3 %collective-permute-done.3.refs_7_ = bf16[288,256]{1,0:T(8,128)(2,1)S(1)} collective-permute-done((bf16[288,256]{1,0:T(8,128)(2,1)S(1)}, bf16[288,256]{1,0:T(8,128)(2,1)S(1)}, u32[]{:S(2)}, u32[]{:S(2)}) %collective-permute-start.3) | collective-permute-done | bytes 147488 | tf_op jit(solution)/shard_map/ppermute | solution.py:22
  39.3 1.0 collective-permute-start.2
  40.3 0.0 collective-permute-done.9.refs_13_
  40.3 0.0 collective-permute-start.13
  40.3 0.0 collective-permute-done.8.refs_12_
  40.4 0.5 collective-permute-start.12
  40.9 0.0 collective-permute-done.7.refs_11_
  40.9 0.1 collective-permute-start.11
  41.0 3.4 %collective-permute-done.2.refs_5_ = bf16[288,256]{1,0:T(8,128)(2,1)S(1)} collective-permute-done((bf16[288,256]{1,0:T(8,128)(2,1)S(1)}, bf16[288,256]{1,0:T(8,128)(2,1)S(1)}, u32[]{:S(2)}, u32[]{:S(2)}) %collective-permute-start.2) | collective-permute-done | bytes 147488 | tf_op jit(solution)/shard_map/ppermute | solution.py:22
  44.4 0.0 collective-permute-done.10.refs_14_
  44.4 2.6 %collective-permute-start.23 = (bf16[3,16,4608]{2,1,0:T(8,128)(2,1)S(1)}, bf16[3,16,4608]{2,1,0:T(8,128)(2,1)S(1)}, u32[]{:S(2)}, u32[]{:S(2)}) collective-permute-start(bf16[3,16,4608]{2,1,0:T(8,128)(2,1)S(1)} %constant_dynamic-update-slice_fusion.3.refs_10_), channel_id=1, source_target_pairs={{0,24},{1,25},{2,26},{3,27},{4,28},{5,29},{6,30},{7,31},{8,16},{9,... | collective-permute-start | bytes 1327112 | tf_op jit(solution)/shard_map/ppermute | solution.py:22
  47.0 0.5 collective-permute-start.22
  47.5 0.0 collective-permute-done.12.refs_16_
  47.5 0.5 collective-permute-start.21
  48.0 0.0 collective-permute-done.11.refs_15_
  48.0 0.7 copy-done.20
  48.8 10.9 %first.1 = (bf16[2,32,32,512]{3,2,1,0:T(8,128)(2,1)}, bf16[272,512]{1,0:T(8,128)(2,1)}) custom-call(s32[2]{0:T(128)} %pad_add_fusion.refs_0_, s32[24]{0:T(128)} %reshape.20.refs_1_, s32[24]{0:T(128)} %reshape.21.refs_2_, bf16[2,32,32,256]{3,2,1,0:T(8,128)(2,1)} %refs_3_.1, bf16[272,256]{1,0:T(8,128)(2,1)} %copy-done.7, bf16[288,256]{1,0:T(8,128)(2,1)} %copy-done.22, ...), custom_call_target="tpu_custom_call" | custom-call | flops 4831838208 | bytes 8388608 | tf_op jit(solution)/shard_map/first/pallas_call | solution.py:270
  59.7 1.8 %collective-permute-start.15 = (bf16[272,512]{1,0:T(8,128)(2,1)}, bf16[272,512]{1,0:T(8,128)(2,1)S(1)}, u32[]{:S(2)}, u32[]{:S(2)}) collective-permute-start(bf16[272,512]{1,0:T(8,128)(2,1)} %get-tuple-element.8), channel_id=1, source_target_pairs={{0,28},{1,29},{2,30},{3,31},{4,0},{5,1},{6,2},{7,3},{8,4},{9,5},{1... | collective-permute-start | bytes 835592 | tf_op jit(solution)/shard_map/ppermute | solution.py:22
  61.5 6.4 %collective-permute-done.22.refs_12_ = bf16[3,16,4608]{2,1,0:T(8,128)(2,1)S(1)} collective-permute-done((bf16[3,16,4608]{2,1,0:T(8,128)(2,1)S(1)}, bf16[3,16,4608]{2,1,0:T(8,128)(2,1)S(1)}, u32[]{:S(2)}, u32[]{:S(2)}) %collective-permute-start.22) | collective-permute-done | bytes 442400 | tf_op jit(solution)/shard_map/ppermute | solution.py:22
  67.9 0.0 collective-permute-start.27
  67.9 0.2 collective-permute-done.21.refs_11_
  68.1 0.3 collective-permute-start.26
  68.4 4.3 %collective-permute-done.15.refs_6_ = bf16[272,512]{1,0:T(8,128)(2,1)S(1)} collective-permute-done((bf16[272,512]{1,0:T(8,128)(2,1)}, bf16[272,512]{1,0:T(8,128)(2,1)S(1)}, u32[]{:S(2)}, u32[]{:S(2)}) %collective-permute-start.15) | collective-permute-done | bytes 278560 | tf_op jit(solution)/shard_map/ppermute | solution.py:22
  72.7 0.7 collective-permute-start.25
  73.4 1.0 slice.21
  74.4 0.0 collective-permute-done.14.refs_4_
  74.4 0.1 collective-permute-start.17
  74.5 3.8 %collective-permute-start.16 = (bf16[288,512]{1,0:T(8,128)(2,1)S(1)}, bf16[288,512]{1,0:T(8,128)(2,1)S(1)}, u32[]{:S(2)}, u32[]{:S(2)}) collective-permute-start(bf16[288,512]{1,0:T(8,128)(2,1)S(1)} %pad_maximum_fusion), channel_id=1, source_target_pairs={{0,3},{1,0},{2,1},{3,2},{4,7},{5,4},{6,5},{7,6},{8,11},{9,8},{10,9... | collective-permute-start | bytes 884744 | tf_op jit(solution)/shard_map/ppermute | solution.py:22
  78.3 0.0 collective-permute-done.27.refs_17_
  78.3 0.0 collective-permute-done.26.refs_16_
  78.3 7.9 %collective-permute-done.17.refs_7_ = bf16[288,512]{1,0:T(8,128)(2,1)S(1)} collective-permute-done((bf16[288,512]{1,0:T(8,128)(2,1)S(1)}, bf16[288,512]{1,0:T(8,128)(2,1)S(1)}, u32[]{:S(2)}, u32[]{:S(2)}) %collective-permute-start.17) | collective-permute-done | bytes 294944 | tf_op jit(solution)/shard_map/ppermute | solution.py:22
  86.2 3.9 %collective-permute-done.16.refs_5_ = bf16[288,512]{1,0:T(8,128)(2,1)S(1)} collective-permute-done((bf16[288,512]{1,0:T(8,128)(2,1)S(1)}, bf16[288,512]{1,0:T(8,128)(2,1)S(1)}, u32[]{:S(2)}, u32[]{:S(2)}) %collective-permute-start.16) | collective-permute-done | bytes 294944 | tf_op jit(solution)/shard_map/ppermute | solution.py:22
  90.2 0.6 copy-done.16
  90.8 15.8 %second.1 = bf16[2,16,16,512]{3,2,1,0:T(8,128)(2,1)} custom-call(s32[2]{0:T(128)} %pad_add_fusion.refs_0_, s32[24]{0:T(128)} %reshape.20.refs_1_, s32[24]{0:T(128)} %reshape.21.refs_2_, bf16[2,32,32,512]{3,2,1,0:T(8,128)(2,1)} %get-tuple-element.7.refs_3_, bf16[272,512]{1,0:T(8,128)(2,1)} %copy-done.5, bf16[288,512]{1,0:T(8,128)(2,1)} %copy-done.16, ...), custom_call_target="tpu_custom_call" | custom-call | flops 9663676416 | bytes 8388608 | tf_op jit(solution)/shard_map/second/pallas_call | solution.py:270
  (62 shorter events, 0.2 us)
Async XLA Ops:
  0.0 11.3 %copy-start.2 = (s32[2,4,3]{1,0,2:T(2,128)S(1)}, s32[2,4,3]{1,0,2:T(2,128)}, u32[]{:S(2)}) copy-start(s32[2,4,3]{1,0,2:T(2,128)} %param.12) | copy-start | bytes 292
  0.0 12.0 %copy-start.3 = (s32[2,4,3]{1,0,2:T(2,128)S(1)}, s32[2,4,3]{1,0,2:T(2,128)}, u32[]{:S(2)}) copy-start(s32[2,4,3]{1,0,2:T(2,128)} %param.13) | copy-start | bytes 292
  0.9 17.4 %collective-permute-start.6 = (bf16[1,16,2304]{2,1,0:T(8,128)(2,1)S(1)}, bf16[1,16,2304]{2,1,0:T(8,128)(2,1)S(1)}, u32[]{:S(2)}, u32[]{:S(2)}) collective-permute-start(bf16[1,16,2304]{2,1,0:T(8,128)(2,1)S(1)} %constant_dynamic-slice_fusion.1), channel_id=1, source_target_pairs={{0,3},{1,0},{2,1},{3,2},{4,7},{5,4},{6,5},{7,6},{8,11},{9,8},{10,9... | collective-permute-start | bytes 221192 | tf_op jit(solution)/shard_map/ppermute | solution.py:22
  6.0 11.4 %collective-permute-start.5 = (bf16[1,16,2304]{2,1,0:T(8,128)(2,1)S(1)}, bf16[1,16,2304]{2,1,0:T(8,128)(2,1)S(1)}, u32[]{:S(2)}, u32[]{:S(2)}) collective-permute-start(bf16[1,16,2304]{2,1,0:T(8,128)(2,1)S(1)} %constant_dynamic-slice_fusion.1), channel_id=1, source_target_pairs={{0,2},{1,3},{2,0},{3,1},{4,6},{5,7},{6,4},{7,5},{8,10},{9,11},{10,... | collective-permute-start | bytes 221192 | tf_op jit(solution)/shard_map/ppermute | solution.py:22
  6.0 8.3 %collective-permute-start.4 = (bf16[1,16,2304]{2,1,0:T(8,128)(2,1)S(1)}, bf16[1,16,2304]{2,1,0:T(8,128)(2,1)S(1)}, u32[]{:S(2)}, u32[]{:S(2)}) collective-permute-start(bf16[1,16,2304]{2,1,0:T(8,128)(2,1)S(1)} %constant_dynamic-slice_fusion.1), channel_id=1, source_target_pairs={{0,1},{1,2},{2,3},{3,0},{4,5},{5,6},{6,7},{7,4},{8,9},{9,10},{10,1... | collective-permute-start | bytes 221192 | tf_op jit(solution)/shard_map/ppermute | solution.py:22
  9.3 9.4 %collective-permute-start.1 = (bf16[272,256]{1,0:T(8,128)(2,1)}, bf16[272,256]{1,0:T(8,128)(2,1)S(1)}, u32[]{:S(2)}, u32[]{:S(2)}) collective-permute-start(bf16[272,256]{1,0:T(8,128)(2,1)} %borders.1), channel_id=1, source_target_pairs={{0,28},{1,29},{2,30},{3,31},{4,0},{5,1},{6,2},{7,3},{8,4},{9,5},{1... | collective-permute-start | bytes 417800 | tf_op jit(solution)/shard_map/ppermute | solution.py:22
  10.4 10.1 %collective-permute-start = (bf16[272,256]{1,0:T(8,128)(2,1)}, bf16[272,256]{1,0:T(8,128)(2,1)S(1)}, u32[]{:S(2)}, u32[]{:S(2)}) collective-permute-start(bf16[272,256]{1,0:T(8,128)(2,1)} %borders.1), channel_id=1, source_target_pairs={{0,4},{1,5},{2,6},{3,7},{4,8},{5,9},{6,10},{7,11},{8,12},{9,13},{1... | collective-permute-start | bytes 417800 | tf_op jit(solution)/shard_map/ppermute | solution.py:22
  14.3 18.6 %collective-permute-start.20 = (bf16[1,16,4608]{2,1,0:T(8,128)(2,1)S(1)}, bf16[1,16,4608]{2,1,0:T(8,128)(2,1)S(1)}, u32[]{:S(2)}, u32[]{:S(2)}) collective-permute-start(bf16[1,16,4608]{2,1,0:T(8,128)(2,1)S(1)} %constant_dynamic-slice_fusion), channel_id=1, source_target_pairs={{0,3},{1,0},{2,1},{3,2},{4,7},{5,4},{6,5},{7,6},{8,11},{9,8},{10,9... | collective-permute-start | bytes 442376 | tf_op jit(solution)/shard_map/ppermute | solution.py:22
  17.4 14.6 %collective-permute-start.19 = (bf16[1,16,4608]{2,1,0:T(8,128)(2,1)S(1)}, bf16[1,16,4608]{2,1,0:T(8,128)(2,1)S(1)}, u32[]{:S(2)}, u32[]{:S(2)}) collective-permute-start(bf16[1,16,4608]{2,1,0:T(8,128)(2,1)S(1)} %constant_dynamic-slice_fusion), channel_id=1, source_target_pairs={{0,2},{1,3},{2,0},{3,1},{4,6},{5,7},{6,4},{7,5},{8,10},{9,11},{10,... | collective-permute-start | bytes 442376 | tf_op jit(solution)/shard_map/ppermute | solution.py:22
  18.4 10.1 %collective-permute-start.18 = (bf16[1,16,4608]{2,1,0:T(8,128)(2,1)S(1)}, bf16[1,16,4608]{2,1,0:T(8,128)(2,1)S(1)}, u32[]{:S(2)}, u32[]{:S(2)}) collective-permute-start(bf16[1,16,4608]{2,1,0:T(8,128)(2,1)S(1)} %constant_dynamic-slice_fusion), channel_id=1, source_target_pairs={{0,1},{1,2},{2,3},{3,0},{4,5},{5,6},{6,7},{7,4},{8,9},{9,10},{10,1... | collective-permute-start | bytes 442376 | tf_op jit(solution)/shard_map/ppermute | solution.py:22
  18.7 30.0 %copy-start.1 = (bf16[3,16,2304]{2,1,0:T(8,128)(2,1)}, bf16[3,16,2304]{2,1,0:T(8,128)(2,1)S(1)}, u32[]{:S(2)}) copy-start(bf16[3,16,2304]{2,1,0:T(8,128)(2,1)S(1)} %constant_dynamic-update-slice_fusion.refs_10_) | copy-start | bytes 663556
  18.7 30.0 %copy-start.6 = (bf16[272,256]{1,0:T(8,128)(2,1)}, bf16[272,256]{1,0:T(8,128)(2,1)S(1)}, u32[]{:S(2)}) copy-start(bf16[272,256]{1,0:T(8,128)(2,1)S(1)} %collective-permute-done.1.refs_6_) | copy-start | bytes 417796
  18.7 21.6 %collective-permute-start.9 = (bf16[3,16,2304]{2,1,0:T(8,128)(2,1)S(1)}, bf16[3,16,2304]{2,1,0:T(8,128)(2,1)S(1)}, u32[]{:S(2)}, u32[]{:S(2)}) collective-permute-start(bf16[3,16,2304]{2,1,0:T(8,128)(2,1)S(1)} %constant_dynamic-update-slice_fusion.refs_10_), channel_id=1, source_target_pairs={{0,24},{1,25},{2,26},{3,27},{4,28},{5,29},{6,30},{7,31},{8,16},{9,... | collective-permute-start | bytes 663560 | tf_op jit(solution)/shard_map/ppermute | solution.py:22
  20.4 28.3 %copy-start.7 = (bf16[272,256]{1,0:T(8,128)(2,1)}, bf16[272,256]{1,0:T(8,128)(2,1)S(1)}, u32[]{:S(2)}) copy-start(bf16[272,256]{1,0:T(8,128)(2,1)S(1)} %collective-permute-done.refs_4_) | copy-start | bytes 417796
  20.4 19.9 %collective-permute-start.8 = (bf16[3,16,2304]{2,1,0:T(8,128)(2,1)S(1)}, bf16[3,16,2304]{2,1,0:T(8,128)(2,1)S(1)}, u32[]{:S(2)}, u32[]{:S(2)}) collective-permute-start(bf16[3,16,2304]{2,1,0:T(8,128)(2,1)S(1)} %constant_dynamic-update-slice_fusion.refs_10_), channel_id=1, source_target_pairs={{0,16},{1,17},{2,18},{3,19},{4,20},{5,21},{6,22},{7,23},{8,24},{9,... | collective-permute-start | bytes 663560 | tf_op jit(solution)/shard_map/ppermute | solution.py:22
  28.4 12.5 %collective-permute-start.7 = (bf16[3,16,2304]{2,1,0:T(8,128)(2,1)S(1)}, bf16[3,16,2304]{2,1,0:T(8,128)(2,1)S(1)}, u32[]{:S(2)}, u32[]{:S(2)}) collective-permute-start(bf16[3,16,2304]{2,1,0:T(8,128)(2,1)S(1)} %constant_dynamic-update-slice_fusion.refs_10_), channel_id=1, source_target_pairs={{0,8},{1,9},{2,10},{3,11},{4,12},{5,13},{6,14},{7,15},{8,0},{9,1},... | collective-permute-start | bytes 663560 | tf_op jit(solution)/shard_map/ppermute | solution.py:22
  32.0 7.3 %collective-permute-start.3 = (bf16[288,256]{1,0:T(8,128)(2,1)S(1)}, bf16[288,256]{1,0:T(8,128)(2,1)S(1)}, u32[]{:S(2)}, u32[]{:S(2)}) collective-permute-start(bf16[288,256]{1,0:T(8,128)(2,1)S(1)} %pad_maximum_fusion.1), channel_id=1, source_target_pairs={{0,1},{1,2},{2,3},{3,0},{4,5},{5,6},{6,7},{7,4},{8,9},{9,10},{10,1... | collective-permute-start | bytes 442376 | tf_op jit(solution)/shard_map/ppermute | solution.py:22
  32.9 11.5 %collective-permute-start.10 = (bf16[3,16,2304]{2,1,0:T(8,128)(2,1)S(1)}, bf16[3,16,2304]{2,1,0:T(8,128)(2,1)}, u32[]{:S(2)}, u32[]{:S(2)}) collective-permute-start(bf16[3,16,2304]{2,1,0:T(8,128)(2,1)S(1)} %constant_dynamic-update-slice_fusion.refs_10_), channel_id=1, source_target_pairs={{0,4},{1,5},{2,6},{3,7},{4,0},{5,1},{6,2},{7,3},{8,12},{9,13},{10,... | collective-permute-start | bytes 663560 | tf_op jit(solution)/shard_map/ppermute | solution.py:22
  39.3 1.7 %copy-start.21 = (bf16[288,256]{1,0:T(8,128)(2,1)}, bf16[288,256]{1,0:T(8,128)(2,1)S(1)}, u32[]{:S(2)}) copy-start(bf16[288,256]{1,0:T(8,128)(2,1)S(1)} %collective-permute-done.3.refs_7_) | copy-start | bytes 442372
  39.3 5.1 %collective-permute-start.2 = (bf16[288,256]{1,0:T(8,128)(2,1)S(1)}, bf16[288,256]{1,0:T(8,128)(2,1)S(1)}, u32[]{:S(2)}, u32[]{:S(2)}) collective-permute-start(bf16[288,256]{1,0:T(8,128)(2,1)S(1)} %pad_maximum_fusion.1), channel_id=1, source_target_pairs={{0,3},{1,0},{2,1},{3,2},{4,7},{5,4},{6,5},{7,6},{8,11},{9,8},{10,9... | collective-permute-start | bytes 442376 | tf_op jit(solution)/shard_map/ppermute | solution.py:22
  40.3 8.4 %copy-start.17 = (bf16[3,16,2304]{2,1,0:T(8,128)(2,1)}, bf16[3,16,2304]{2,1,0:T(8,128)(2,1)S(1)}, u32[]{:S(2)}) copy-start(bf16[3,16,2304]{2,1,0:T(8,128)(2,1)S(1)} %collective-permute-done.9.refs_13_) | copy-start | bytes 663556
  40.3 6.7 %collective-permute-start.13 = (bf16[3,16,2304]{2,1,0:T(8,128)(2,1)S(1)}, bf16[3,16,2304]{2,1,0:T(8,128)(2,1)}, u32[]{:S(2)}, u32[]{:S(2)}) collective-permute-start(bf16[3,16,2304]{2,1,0:T(8,128)(2,1)S(1)} %collective-permute-done.9.refs_13_), channel_id=1, source_target_pairs={{0,4},{1,5},{2,6},{3,7},{4,0},{5,1},{6,2},{7,3},{8,12},{9,13},{10,... | collective-permute-start | bytes 663560 | tf_op jit(solution)/shard_map/ppermute | solution.py:22
  40.4 8.4 %copy-start.18 = (bf16[3,16,2304]{2,1,0:T(8,128)(2,1)}, bf16[3,16,2304]{2,1,0:T(8,128)(2,1)S(1)}, u32[]{:S(2)}) copy-start(bf16[3,16,2304]{2,1,0:T(8,128)(2,1)S(1)} %collective-permute-done.8.refs_12_) | copy-start | bytes 663556
  40.4 7.2 %collective-permute-start.12 = (bf16[3,16,2304]{2,1,0:T(8,128)(2,1)S(1)}, bf16[3,16,2304]{2,1,0:T(8,128)(2,1)}, u32[]{:S(2)}, u32[]{:S(2)}) collective-permute-start(bf16[3,16,2304]{2,1,0:T(8,128)(2,1)S(1)} %collective-permute-done.8.refs_12_), channel_id=1, source_target_pairs={{0,4},{1,5},{2,6},{3,7},{4,0},{5,1},{6,2},{7,3},{8,12},{9,13},{10,... | collective-permute-start | bytes 663560 | tf_op jit(solution)/shard_map/ppermute | solution.py:22
  40.9 7.9 %copy-start.19 = (bf16[3,16,2304]{2,1,0:T(8,128)(2,1)}, bf16[3,16,2304]{2,1,0:T(8,128)(2,1)S(1)}, u32[]{:S(2)}) copy-start(bf16[3,16,2304]{2,1,0:T(8,128)(2,1)S(1)} %collective-permute-done.7.refs_11_) | copy-start | bytes 663556
  40.9 7.1 %collective-permute-start.11 = (bf16[3,16,2304]{2,1,0:T(8,128)(2,1)S(1)}, bf16[3,16,2304]{2,1,0:T(8,128)(2,1)S(1)}, u32[]{:S(2)}, u32[]{:S(2)}) collective-permute-start(bf16[3,16,2304]{2,1,0:T(8,128)(2,1)S(1)} %collective-permute-done.7.refs_11_), channel_id=1, source_target_pairs={{0,4},{1,5},{2,6},{3,7},{4,0},{5,1},{6,2},{7,3},{8,12},{9,13},{10,... | collective-permute-start | bytes 663560 | tf_op jit(solution)/shard_map/ppermute | solution.py:22
  41.0 18.7 %copy-start = (bf16[3,16,4608]{2,1,0:T(8,128)(2,1)}, bf16[3,16,4608]{2,1,0:T(8,128)(2,1)S(1)}, u32[]{:S(2)}) copy-start(bf16[3,16,4608]{2,1,0:T(8,128)(2,1)S(1)} %constant_dynamic-update-slice_fusion.3.refs_10_) | copy-start | bytes 1327108
  44.4 3.6 %copy-start.22 = (bf16[288,256]{1,0:T(8,128)(2,1)}, bf16[288,256]{1,0:T(8,128)(2,1)S(1)}, u32[]{:S(2)}) copy-start(bf16[288,256]{1,0:T(8,128)(2,1)S(1)} %collective-permute-done.2.refs_5_) | copy-start | bytes 442372
  44.4 30.1 %collective-permute-start.24 = (bf16[3,16,4608]{2,1,0:T(8,128)(2,1)S(1)}, bf16[3,16,4608]{2,1,0:T(8,128)(2,1)S(1)}, u32[]{:S(2)}, u32[]{:S(2)}) collective-permute-start(bf16[3,16,4608]{2,1,0:T(8,128)(2,1)S(1)} %constant_dynamic-update-slice_fusion.3.refs_10_), channel_id=1, source_target_pairs={{0,4},{1,5},{2,6},{3,7},{4,0},{5,1},{6,2},{7,3},{8,12},{9,13},{10,... | collective-permute-start | bytes 1327112 | tf_op jit(solution)/shard_map/ppermute | solution.py:22
  44.4 17.0 %collective-permute-start.23 = (bf16[3,16,4608]{2,1,0:T(8,128)(2,1)S(1)}, bf16[3,16,4608]{2,1,0:T(8,128)(2,1)S(1)}, u32[]{:S(2)}, u32[]{:S(2)}) collective-permute-start(bf16[3,16,4608]{2,1,0:T(8,128)(2,1)S(1)} %constant_dynamic-update-slice_fusion.3.refs_10_), channel_id=1, source_target_pairs={{0,24},{1,25},{2,26},{3,27},{4,28},{5,29},{6,30},{7,31},{8,16},{9,... | collective-permute-start | bytes 1327112 | tf_op jit(solution)/shard_map/ppermute | solution.py:22
  47.0 20.9 %collective-permute-start.22 = (bf16[3,16,4608]{2,1,0:T(8,128)(2,1)S(1)}, bf16[3,16,4608]{2,1,0:T(8,128)(2,1)S(1)}, u32[]{:S(2)}, u32[]{:S(2)}) collective-permute-start(bf16[3,16,4608]{2,1,0:T(8,128)(2,1)S(1)} %constant_dynamic-update-slice_fusion.3.refs_10_), channel_id=1, source_target_pairs={{0,16},{1,17},{2,18},{3,19},{4,20},{5,21},{6,22},{7,23},{8,24},{9,... | collective-permute-start | bytes 1327112 | tf_op jit(solution)/shard_map/ppermute | solution.py:22
  47.5 20.6 %collective-permute-start.21 = (bf16[3,16,4608]{2,1,0:T(8,128)(2,1)S(1)}, bf16[3,16,4608]{2,1,0:T(8,128)(2,1)S(1)}, u32[]{:S(2)}, u32[]{:S(2)}) collective-permute-start(bf16[3,16,4608]{2,1,0:T(8,128)(2,1)S(1)} %constant_dynamic-update-slice_fusion.3.refs_10_), channel_id=1, source_target_pairs={{0,8},{1,9},{2,10},{3,11},{4,12},{5,13},{6,14},{7,15},{8,0},{9,1},... | collective-permute-start | bytes 1327112 | tf_op jit(solution)/shard_map/ppermute | solution.py:22
  48.0 0.7 copy-start.20
  59.7 13.0 %collective-permute-start.15 = (bf16[272,512]{1,0:T(8,128)(2,1)}, bf16[272,512]{1,0:T(8,128)(2,1)S(1)}, u32[]{:S(2)}, u32[]{:S(2)}) collective-permute-start(bf16[272,512]{1,0:T(8,128)(2,1)} %get-tuple-element.8), channel_id=1, source_target_pairs={{0,28},{1,29},{2,30},{3,31},{4,0},{5,1},{6,2},{7,3},{8,4},{9,5},{1... | collective-permute-start | bytes 835592 | tf_op jit(solution)/shard_map/ppermute | solution.py:22
  61.5 28.6 %copy-start.9 = (bf16[3,16,4608]{2,1,0:T(8,128)(2,1)}, bf16[3,16,4608]{2,1,0:T(8,128)(2,1)S(1)}, u32[]{:S(2)}) copy-start(bf16[3,16,4608]{2,1,0:T(8,128)(2,1)S(1)} %collective-permute-done.23.refs_13_) | copy-start | bytes 1327108
  61.5 12.9 %collective-permute-start.14 = (bf16[272,512]{1,0:T(8,128)(2,1)}, bf16[272,512]{1,0:T(8,128)(2,1)S(1)}, u32[]{:S(2)}, u32[]{:S(2)}) collective-permute-start(bf16[272,512]{1,0:T(8,128)(2,1)} %get-tuple-element.8), channel_id=1, source_target_pairs={{0,4},{1,5},{2,6},{3,7},{4,8},{5,9},{6,10},{7,11},{8,12},{9,13},{1... | collective-permute-start | bytes 835592 | tf_op jit(solution)/shard_map/ppermute | solution.py:22
  67.9 22.2 %copy-start.10 = (bf16[3,16,4608]{2,1,0:T(8,128)(2,1)}, bf16[3,16,4608]{2,1,0:T(8,128)(2,1)S(1)}, u32[]{:S(2)}) copy-start(bf16[3,16,4608]{2,1,0:T(8,128)(2,1)S(1)} %collective-permute-done.22.refs_12_) | copy-start | bytes 1327108
  67.9 10.4 %collective-permute-start.27 = (bf16[3,16,4608]{2,1,0:T(8,128)(2,1)S(1)}, bf16[3,16,4608]{2,1,0:T(8,128)(2,1)S(1)}, u32[]{:S(2)}, u32[]{:S(2)}) collective-permute-start(bf16[3,16,4608]{2,1,0:T(8,128)(2,1)S(1)} %collective-permute-done.23.refs_13_), channel_id=1, source_target_pairs={{0,4},{1,5},{2,6},{3,7},{4,0},{5,1},{6,2},{7,3},{8,12},{9,13},{10,... | collective-permute-start | bytes 1327112 | tf_op jit(solution)/shard_map/ppermute | solution.py:22
  68.1 22.0 %copy-start.11 = (bf16[3,16,4608]{2,1,0:T(8,128)(2,1)}, bf16[3,16,4608]{2,1,0:T(8,128)(2,1)S(1)}, u32[]{:S(2)}) copy-start(bf16[3,16,4608]{2,1,0:T(8,128)(2,1)S(1)} %collective-permute-done.21.refs_11_) | copy-start | bytes 1327108
  68.1 10.2 %collective-permute-start.26 = (bf16[3,16,4608]{2,1,0:T(8,128)(2,1)S(1)}, bf16[3,16,4608]{2,1,0:T(8,128)(2,1)S(1)}, u32[]{:S(2)}, u32[]{:S(2)}) collective-permute-start(bf16[3,16,4608]{2,1,0:T(8,128)(2,1)S(1)} %collective-permute-done.22.refs_12_), channel_id=1, source_target_pairs={{0,4},{1,5},{2,6},{3,7},{4,0},{5,1},{6,2},{7,3},{8,12},{9,13},{10,... | collective-permute-start | bytes 1327112 | tf_op jit(solution)/shard_map/ppermute | solution.py:22
  72.7 17.5 %copy-start.4 = (bf16[272,512]{1,0:T(8,128)(2,1)}, bf16[272,512]{1,0:T(8,128)(2,1)S(1)}, u32[]{:S(2)}) copy-start(bf16[272,512]{1,0:T(8,128)(2,1)S(1)} %collective-permute-done.15.refs_6_) | copy-start | bytes 835588
  72.7 5.7 %collective-permute-start.25 = (bf16[3,16,4608]{2,1,0:T(8,128)(2,1)S(1)}, bf16[3,16,4608]{2,1,0:T(8,128)(2,1)S(1)}, u32[]{:S(2)}, u32[]{:S(2)}) collective-permute-start(bf16[3,16,4608]{2,1,0:T(8,128)(2,1)S(1)} %collective-permute-done.21.refs_11_), channel_id=1, source_target_pairs={{0,4},{1,5},{2,6},{3,7},{4,0},{5,1},{6,2},{7,3},{8,12},{9,13},{10,... | collective-permute-start | bytes 1327112 | tf_op jit(solution)/shard_map/ppermute | solution.py:22
  74.4 15.8 %copy-start.5 = (bf16[272,512]{1,0:T(8,128)(2,1)}, bf16[272,512]{1,0:T(8,128)(2,1)S(1)}, u32[]{:S(2)}) copy-start(bf16[272,512]{1,0:T(8,128)(2,1)S(1)} %collective-permute-done.14.refs_4_) | copy-start | bytes 835588
  74.4 11.8 %collective-permute-start.17 = (bf16[288,512]{1,0:T(8,128)(2,1)S(1)}, bf16[288,512]{1,0:T(8,128)(2,1)S(1)}, u32[]{:S(2)}, u32[]{:S(2)}) collective-permute-start(bf16[288,512]{1,0:T(8,128)(2,1)S(1)} %pad_maximum_fusion), channel_id=1, source_target_pairs={{0,1},{1,2},{2,3},{3,0},{4,5},{5,6},{6,7},{7,4},{8,9},{9,10},{10,1... | collective-permute-start | bytes 884744 | tf_op jit(solution)/shard_map/ppermute | solution.py:22
  74.5 15.6 %copy-start.8 = (bf16[3,16,4608]{2,1,0:T(8,128)(2,1)}, bf16[3,16,4608]{2,1,0:T(8,128)(2,1)S(1)}, u32[]{:S(2)}) copy-start(bf16[3,16,4608]{2,1,0:T(8,128)(2,1)S(1)} %collective-permute-done.24.refs_14_) | copy-start | bytes 1327108
  74.5 15.6 %collective-permute-start.16 = (bf16[288,512]{1,0:T(8,128)(2,1)S(1)}, bf16[288,512]{1,0:T(8,128)(2,1)S(1)}, u32[]{:S(2)}, u32[]{:S(2)}) collective-permute-start(bf16[288,512]{1,0:T(8,128)(2,1)S(1)} %pad_maximum_fusion), channel_id=1, source_target_pairs={{0,3},{1,0},{2,1},{3,2},{4,7},{5,4},{6,5},{7,6},{8,11},{9,8},{10,9... | collective-permute-start | bytes 884744 | tf_op jit(solution)/shard_map/ppermute | solution.py:22
  78.3 11.8 %copy-start.12 = (bf16[3,16,4608]{2,1,0:T(8,128)(2,1)}, bf16[3,16,4608]{2,1,0:T(8,128)(2,1)S(1)}, u32[]{:S(2)}) copy-start(bf16[3,16,4608]{2,1,0:T(8,128)(2,1)S(1)} %collective-permute-done.27.refs_17_) | copy-start | bytes 1327108
  78.3 11.8 %copy-start.13 = (bf16[3,16,4608]{2,1,0:T(8,128)(2,1)}, bf16[3,16,4608]{2,1,0:T(8,128)(2,1)S(1)}, u32[]{:S(2)}) copy-start(bf16[3,16,4608]{2,1,0:T(8,128)(2,1)S(1)} %collective-permute-done.26.refs_16_) | copy-start | bytes 1327108
  78.3 11.8 %copy-start.14 = (bf16[3,16,4608]{2,1,0:T(8,128)(2,1)}, bf16[3,16,4608]{2,1,0:T(8,128)(2,1)S(1)}, u32[]{:S(2)}) copy-start(bf16[3,16,4608]{2,1,0:T(8,128)(2,1)S(1)} %collective-permute-done.25.refs_15_) | copy-start | bytes 1327108
  86.2 4.0 %copy-start.15 = (bf16[288,512]{1,0:T(8,128)(2,1)}, bf16[288,512]{1,0:T(8,128)(2,1)S(1)}, u32[]{:S(2)}) copy-start(bf16[288,512]{1,0:T(8,128)(2,1)S(1)} %collective-permute-done.17.refs_7_) | copy-start | bytes 884740
  90.1 0.7 copy-start.16
where the time goes:
time: 107 us
  waiting for transfers between devices  42.6 us (40%)
  Pallas kernels  29.1 us (27%)
  starting transfers between devices  27.3 us (26%)
  local copies, waits for them, and re-layouts  6.68 us (6%)
    ppermute x28, waiting for transfers between devices, move(): return lax.ppermute(x, AXES, pairs)  42.6 us
    ppermute x28, starting transfers between devices, move(): return lax.ppermute(x, AXES, pairs)  27.3 us
    pallas_call x2, Pallas kernels, conv(): pl.pallas_call(functools.partial(conv_kernel, len(sources), pooling), out...  26.8 us
    pallas_call x1, Pallas kernels, borders(): pl.pallas_call(borders_kernel, out_shape=jax.ShapeDtypeStruct((tiles * 4...  2.3 us
  transfers between devices with their start and end apart: 28, of which 9 were waited for; matrix products, arithmetic and copies ran while one was open for 5% of the time, Pallas kernels for 12%

commit v1 on v0

--- a/solution.py
+++ b/solution.py
@@ -10,6 +10,7 @@
 
 AXES = ("tile", "fsdp")
 PAD = 16
+GRANT = 36 << 20
 
 
 def move(x, target):
@@ -26,6 +27,11 @@
     return move(x, lambda t, f: (t + rows, f + cols))
 
 
+def doublings(cols):
+    bits = [1 << k for k in range(cols.bit_length() - 1)]
+    return bits[::-1]
+
+
 def gather_rows(weight):
     rows, cols = (lax.axis_size("tile"), lax.axis_size("fsdp"))
     tall = rows // 4
@@ -33,15 +39,16 @@
     width = weight.shape[1]
     parts = weight.reshape(rows, share, width)
     mine = lax.dynamic_index_in_dim(parts, lax.axis_index("tile"), 0, keepdims=True)
-    unit = jnp.concatenate([shift(mine, 0, k) for k in range(1, cols)], axis=0)
+    held = {0: mine}
+    for bit in doublings(cols):
+        there = jnp.concatenate([held[h] for h in sorted(held)], axis=0)
+        there = move(there, lambda t, f: (t, f ^ bit))
+        held.update({h ^ bit: there[i : i + 1] for i, h in enumerate(sorted(held))})
+    unit = jnp.concatenate([held[h] for h in range(1, cols)], axis=0)
     near = [unit]
     for step in range(1, 2 * tall):
         dy, dx = divmod(step, 2)
-        near.append(
-            move(
-                unit, lambda t, f: (((t // 4 + dy) % tall) * 4 + ((t // 2 % 2) ^ dx) * 2 + t % 2, f)
-            )
-        )
+        near.append(move(unit, lambda t, f: (((t // 4 + dy) % tall) * 4 + ((t // 2 % 2) ^ dx) * 2 + t % 2, f)))
     other = [move(x, lambda t, f: (t ^ 1, f)) for x in near]
     return near + other
 
@@ -57,7 +64,7 @@
     core = (source_t ^ t) & 1
     dx = ((source_t ^ t) >> 1) & 1
     dy = (t // 4 - source_t // 4) % tall
-    hop = (f - source_f) % cols
+    hop = f ^ source_f
     index = (core * 2 * tall + dy * 2 + dx) * (cols - 1) + hop - 1
     index = jnp.where(hop == 0, 0, index)
     whole = jnp.take(pieces, index.reshape(-1), axis=0).reshape(cols, rows * share, width)
@@ -95,7 +102,14 @@
         bundle[pl.ds(start + 2 * edge, edge), :] = chunk[-edge:]
 
 
-def put_corners(bundle, tiles, edge):
+def request_of(links, link, tiles, edge, turned):
+    home = lax.rem(links[link], tiles) * 4 + links[link + 1]
+    turns = turned + jnp.where(links[link + 1] >= 2, 1, 0) + jnp.where(links[link + 2] == 1, 0, 1)
+    forward = lax.rem(turns, 2) == 0
+    return home * edge + jnp.where(forward, 0, edge - 1), jnp.where(forward, 1, -1)
+
+
+def put_corners(bundle, tiles, edge, links=None):
     def source(n):
         corner = n & 3
         across = jnp.where((corner == 1) | (corner == 2), edge - 1, 0)
@@ -103,31 +117,57 @@
 
     strips = tiles * 4 * edge
     cells = select(one_hot(PAD, strips, source), bundle[:strips, :])
+    if links is not None:
+        row = lax.broadcasted_iota(jnp.int32, cells.shape, 0)
+        lane = lax.broadcasted_iota(jnp.int32, cells.shape, 1)
+        for side in range(tiles * 4):
+            first, step = request_of(links, 2 + side * 3, tiles, edge, 1 if side % 4 >= 2 else 0)
+            asked = jnp.where(lane < 128, first, step).astype(jnp.float32)
+            cells = jnp.where(row == tiles * 4 + side, asked, cells)
     bundle[strips:, :] = cells.astype(jnp.bfloat16)
 
 
-def borders_kernel(field, bundle):
+def answer(out, bundle, near, side, tiles, edge):
+    strips = tiles * 4 * edge
+    asked = near[strips : strips + PAD, :256].astype(jnp.float32)
+    n = lax.broadcasted_iota(jnp.int32, (edge, strips), 0).astype(jnp.float32)
+    column = lax.broadcasted_iota(jnp.int32, (edge, strips), 1).astype(jnp.float32)
+    for tile in range(tiles):
+        row = tiles * 4 + tile * 4 + side
+        first, step = (
+            jnp.concatenate([asked[row : row + 1, low : low + 128]] * (strips // 128), axis=1)
+            for low in (0, 128)
+        )
+        picker = jnp.where(column == first + step * n, 1.0, 0.0).astype(jnp.bfloat16)
+        out[tile * edge : (tile + 1) * edge, :] = select(picker, bundle[:strips, :]).astype(jnp.bfloat16)
+
+
+def borders_kernel(links, field, bundle):
     tiles, edge, _, channels = field.shape
     for tile in range(tiles):
         for half in range(2):
             rows = edge // 2
             chunk = field[tile, half * rows : (half + 1) * rows].reshape(rows * edge, channels)
             put_borders(bundle, tile, half, chunk, edge)
-    put_corners(bundle, tiles, edge)
-
-
-def borders(field):
+    put_corners(bundle, tiles, edge, links)
+
+
+def borders(field, links):
     tiles, edge, _, channels = field.shape
     return pl.pallas_call(
         borders_kernel,
         out_shape=jax.ShapeDtypeStruct((tiles * 4 * edge + PAD, channels), jnp.bfloat16),
+        in_specs=[pl.BlockSpec(memory_space=pltpu.SMEM), pl.BlockSpec(memory_space=pltpu.VMEM)],
+        out_specs=pl.BlockSpec(memory_space=pltpu.VMEM),
+        compiler_params=pltpu.CompilerParams(vmem_limit_bytes=16 << 20),
         name="borders",
-    )(field)
-
-
-def surround(field, near, side_links, corner_links, halos, wide):
-    tiles, edge, _, channels = field.shape
-    strips = tiles * 4 * edge
+    )(links, field)
+
+
+def surround(field, near, links, chosen, halos, wide):
+    tiles, edge, _, channels = field.shape
+    strips = tiles * edge if chosen else tiles * 4 * edge
+    cells_at = strips if chosen else strips + PAD
     column = lax.broadcasted_iota(jnp.int32, (edge, channels), 0)
 
     def put(tile, row, middle, before, after):
@@ -140,25 +180,21 @@
 
     for tile in range(tiles):
         for side in range(4):
-            link = (tile * 4 + side) * 3
-            home = lax.rem(side_links[link], tiles) * 4 + side_links[link + 1]
-            turns = (
-                (1 if side >= 2 else 0)
-                + jnp.where(side_links[link + 1] >= 2, 1, 0)
-                + jnp.where(side_links[link + 2] == 1, 0, 1)
+            if chosen:
+                halos[tile, side] = near[side][tile * edge : (tile + 1) * edge, :].astype(jnp.float32)
+                continue
+            first, step = request_of(
+                links, 2 + (tile * 4 + side) * 3, tiles, edge, 1 if side >= 2 else 0
             )
-            forward = lax.rem(turns, 2) == 0
-            first = home * edge + jnp.where(forward, 0, edge - 1)
-            step = jnp.where(forward, 1, -1)
             picker = one_hot(edge, strips, lambda n: first + step * n)
             halos[tile, side] = select(picker, near[side][:strips, :])
         cells = []
         for corner, (source, low) in enumerate(((3, 0), (1, 0), (1, PAD), (3, PAD))):
-            link = (tile * 4 + corner) * 3
-            pick = lax.rem(corner_links[link], tiles) * 4 + corner_links[link + 1]
-            pick = jnp.where(corner_links[link + 2] == 1, pick, -1)
+            link = 2 + (tiles * 4 + tile * 4 + corner) * 3
+            pick = lax.rem(links[link], tiles) * 4 + links[link + 1]
+            pick = jnp.where(links[link + 2] == 1, pick, -1)
             picker = one_hot(8, PAD, lambda n: pick)
-            cells.append(select(picker, near[source][strips + low : strips + low + PAD, :])[:1])
+            cells.append(select(picker, near[source][cells_at + low : cells_at + low + PAD, :])[:1])
         put(tile, 0, halos[tile, 0], cells[0], cells[1])
         put(tile, edge + 1, halos[tile, 2], cells[3], cells[2])
 
@@ -171,7 +207,7 @@
                 put(tile, row + 1, field[tile, row], before, after)
 
 
-def fetch_weight(sources, whole, place_of, sems):
+def fetch_weight(sources, whole, links, sems):
     copies = []
     if len(sources) == 1:
         copies.append(pltpu.make_async_copy(sources[0], whole, sems.at[0]))
@@ -181,7 +217,7 @@
         steps = len(pieces) // 2
         cols = hops + 1
         rows = own.shape[0] // share
-        t, f = (place_of[0], place_of[1])
+        t, f = (links[0], links[1])
         tall = steps // 2
         copies.append(
             pltpu.make_async_copy(
@@ -195,7 +231,7 @@
                 far_x = lax.rem(t // 2 + dx, 2)
                 far = far_y * 4 + far_x * 2 + lax.rem(t + core, 2)
                 for hop in range(1, cols):
-                    far_f = lax.rem(f + cols - hop, cols)
+                    far_f = f ^ hop
                     start = pl.multiple_of((far_f * rows + far) * share, share)
                     copies.append(
                         pltpu.make_async_copy(
@@ -208,13 +244,14 @@
 
 
 def conv_kernel(count, pooling, *refs):
-    place_of, side_links, corner_links, field, north, east, south, west, bias = refs[:9]
-    sources = refs[9 : 9 + count]
-    outs = refs[9 + count : -5]
-    halos, wide, whole, sems, total = refs[-5:]
-    tiles, edge, _, channels = field.shape
-    copies = fetch_weight(sources, whole, place_of, sems)
-    surround(field, (north, east, south, west), side_links, corner_links, halos, wide)
+    links, field, north, east, south, west, bias = refs[:7]
+    near = (north, east, south, west)
+    sources = refs[7 : 7 + count]
+    outs = refs[7 + count : -6]
+    halos, wide, whole, sems, total, bundle = refs[-6:]
+    tiles, edge, _, channels = field.shape
+    copies = fetch_weight(sources, whole, links, sems)
+    surround(field, near, links, pooling, halos, wide)
     for copy in copies:
         copy.wait()
     rows = edge // 2
@@ -247,20 +284,23 @@
             else:
                 hidden = act.astype(jnp.bfloat16)
                 outs[0][tile, low : low + rows] = hidden.reshape(rows, edge, act.shape[1])
-                put_borders(outs[1], tile, half, hidden, edge)
+                put_borders(bundle, tile, half, hidden, edge)
     if not pooling:
-        put_corners(outs[1], tiles, edge)
-
-
-def conv(field, near, place_of, side_links, corner_links, bias, sources, pooling):
+        put_corners(bundle, tiles, edge)
+        for side, out in enumerate(outs[1:]):
+            answer(out, bundle, near[side], (side + 2) % 4, tiles, edge)
+            if side in (0, 2):
+                out[tiles * edge :, :] = bundle[tiles * 4 * edge :, :]
+
+
+def conv(field, near, links, bias, sources, pooling):
     tiles, edge, _, channels = field.shape
     width = bias.shape[0]
     if pooling:
         outs = (jax.ShapeDtypeStruct((tiles, edge // 2, edge // 2, width), jnp.bfloat16),)
     else:
-        outs = (
-            jax.ShapeDtypeStruct((tiles, edge, edge, width), jnp.bfloat16),
-            jax.ShapeDtypeStruct((tiles * 4 * edge + PAD, width), jnp.bfloat16),
+        outs = (jax.ShapeDtypeStruct((tiles, edge, edge, width), jnp.bfloat16),) + tuple(
+            jax.ShapeDtypeStruct((tiles * edge + extra, width), jnp.bfloat16) for extra in (PAD, 0, PAD, 0)
         )
     vmem = pl.BlockSpec(memory_space=pltpu.VMEM)
     smem = pl.BlockSpec(memory_space=pltpu.SMEM)
@@ -270,7 +310,7 @@
     return pl.pallas_call(
         functools.partial(conv_kernel, len(sources), pooling),
         out_shape=outs,
-        in_specs=[smem] * 3 + [vmem] * 6 + [anywhere] * len(sources),
+        in_specs=[smem] + [vmem] * 6 + [anywhere] * len(sources),
         out_specs=[vmem] * len(outs),
         scratch_shapes=[
             pltpu.VMEM((tiles, 4, edge, channels), jnp.float32),
@@ -278,13 +318,13 @@
             pltpu.VMEM((width, 9 * channels), jnp.bfloat16),
             pltpu.SemaphoreType.DMA((copies,)),
             pltpu.VMEM((edge * edge // 4, 128), jnp.float32),
+            pltpu.VMEM((tiles * 4 * edge + PAD, width), jnp.bfloat16),
         ],
         cost_estimate=pl.CostEstimate(flops=flops, bytes_accessed=8 << 20, transcendentals=0),
+        compiler_params=pltpu.CompilerParams(vmem_limit_bytes=GRANT),
         name="second" if pooling else "first",
     )(
-        place_of,
-        side_links.reshape(-1),
-        corner_links.reshape(-1),
+        links,
         field,
         *near,
         bias.reshape(1, width),
@@ -292,13 +332,12 @@
     )
 
 
-def exchange(bundle):
-    north = shift(bundle, 1, 0)
-    south = shift(bundle, -1, 0)
-    strips = bundle.shape[0] - PAD
-    bundle = jnp.concatenate([bundle[:strips], north[strips:], south[strips:]], axis=0)
-    west = shift(bundle, 0, 1)
-    east = shift(bundle, 0, -1)
+def exchange(to_north, to_east, to_south, to_west):
+    north = shift(to_south, 1, 0)
+    south = shift(to_north, -1, 0)
+    cells = [north[-PAD:], south[-PAD:]]
+    west = shift(jnp.concatenate([to_east, *cells], axis=0), 0, 1)
+    east = shift(jnp.concatenate([to_west, *cells], axis=0), 0, -1)
     return north, east, south, west
 
 
@@ -312,15 +351,21 @@
 def shards(
     tiles_in, first_weight, first_bias, second_weight, second_bias, side_links, corner_links
 ):
-    place_of = jnp.stack([lax.axis_index("tile"), lax.axis_index("fsdp")])
+    links = jnp.concatenate(
+        [
+            lax.axis_index("tile").reshape(1),
+            lax.axis_index("fsdp").reshape(1),
+            side_links.reshape(-1),
+            corner_links.reshape(-1),
+        ]
+    )
     first = sources_of(first_weight)
     second = sources_of(second_weight)
-    links = (place_of, side_links, corner_links)
-    bundle = borders(tiles_in)
-    near = exchange(bundle)
-    hidden, bundle = conv(tiles_in, near, *links, first_bias, first, False)
-    near = exchange(bundle)
-    return conv(hidden, near, *links, second_bias, second, True)[0]
+    bundle = borders(tiles_in, links)
+    near = exchange(bundle, bundle, bundle, bundle)
+    hidden, *strips = conv(tiles_in, near, links, first_bias, first, False)
+    near = exchange(*strips)
+    return conv(hidden, near, links, second_bias, second, True)[0]
 
 
 def solution(mesh):

time: 107 us -> 103 us (0.963)
  starting transfers between devices: 27.3 us -> 22.1 us
  local copies, waits for them, and re-layouts: 6.68 us -> 3.92 us
  Pallas kernels: 29.1 us -> 31.5 us
  waiting for transfers between devices: 42.6 us -> 45 us
    ppermute x28 -> x26, starting transfers between devices: 27.3 us -> 22.1 us  [move(): return lax.ppermute(x, AXES, pairs)]
    pallas_call x2, Pallas kernels: 26.8 us -> 30.6 us  [conv(): pl.pallas_call(functools.partial(conv_kernel, len(sources), pooling), out...]
    ppermute x28 -> x26, waiting for transfers between devices: 42.6 us -> 45 us  [move(): return lax.ppermute(x, AXES, pairs)]
    slice x6, local copies, waits for them, and re-layouts: 1.92 us -> 0.04 us  [the longest x2 0.03 us: gather_rows(): held.update({h ^ bit: there[i:i + 1] for i, h in enumerate(sorted(held))})]
    pallas_call x1, Pallas kernels: 2.3 us -> 0.95 us  [borders(): pl.pallas_call(borders_kernel, out_shape=jax.ShapeDtypeStruct((tiles * 4...]
    unnamed x52 -> x14, local copies, waits for them, and re-layouts: 1.64 us -> 2.81 us
    reshape x2, local copies, waits for them, and re-layouts: 1.26 us -> 0.17 us  [the longest x1 0.09 us: shards(): side_links.reshape(-1)]
  transfers between devices with their start and end apart: 28 -> 26, of which waited for: 9 -> 9; matrix products, arithmetic and copies ran while one was open for 5% -> 1% of each run, Pallas kernels for 12% -> 11%
where the time goes in v1:
time: 103 us
  waiting for transfers between devices  45 us (44%)
  Pallas kernels  31.5 us (31%)
  starting transfers between devices  22.1 us (21%)
  local copies, waits for them, and re-layouts  3.92 us (4%)
    ppermute x26, waiting for transfers between devices, move(): return lax.ppermute(x, AXES, pairs)  45 us
    pallas_call x2, Pallas kernels, conv(): pl.pallas_call(functools.partial(conv_kernel, len(sources), pooling), out...  30.6 us
    ppermute x26, starting transfers between devices, move(): return lax.ppermute(x, AXES, pairs)  22.1 us
    unnamed x14, local copies, waits for them, and re-layouts  2.81 us
  transfers between devices with their start and end apart: 26, of which 9 were waited for; matrix products, arithmetic and copies ran while one was open for 1% of the time, Pallas kernels for 11%

profile of v1, /device:TPU:0, one launch (start us, length us, event | category | flops | bytes accessed | tf_op | source)
XLA Modules:
  0.0 103.1 jit_solution(12467153608924727491)
XLA Ops:
  0.0 0.8 copy.10
  0.8 0.1 reshape.26
  0.9 0.8 copy.11
  1.6 0.1 reshape.27
  1.7 0.1 pad_add_fusion.links.refs_0_
  1.8 1.2 %copy-done = bf16[2,32,32,256]{3,2,1,0:T(8,128)(2,1)S(1)} copy-done((bf16[2,32,32,256]{3,2,1,0:T(8,128)(2,1)S(1)}, bf16[2,32,32,256]{3,2,1,0:T(8,128)(2,1)}, u32[]{:S(2)}) %copy-start) | copy-done | bytes 1048600
  3.0 1.0 borders.1
  4.0 3.4 %collective-permute-start.1 = (bf16[272,256]{1,0:T(8,128)(2,1)S(1)}, bf16[272,256]{1,0:T(8,128)(2,1)S(1)}, u32[]{:S(2)}, u32[]{:S(2)}) collective-permute-start(bf16[272,256]{1,0:T(8,128)(2,1)S(1)} %borders.1), channel_id=1, source_target_pairs={{0,28},{1,29},{2,30},{3,31},{4,0},{5,1},{6,2},{7,3},{8,4},{9,5},{1... | collective-permute-start | bytes 417800 | tf_op jit(solution)/shard_map/ppermute | solution.py:23
  7.4 0.0 collective-permute-start
  7.4 0.9 constant_dynamic-slice_fusion.1
  8.3 2.6 %collective-permute-start.4 = (bf16[1,16,2304]{2,1,0:T(8,128)(2,1)S(1)}, bf16[1,16,2304]{2,1,0:T(8,128)(2,1)S(1)}, u32[]{:S(2)}, u32[]{:S(2)}) collective-permute-start(bf16[1,16,2304]{2,1,0:T(8,128)(2,1)S(1)} %constant_dynamic-slice_fusion.1), channel_id=1, source_target_pairs={{0,2},{1,3},{2,0},{3,1},{4,6},{5,7},{6,4},{7,5},{8,10},{9,11},{10,... | collective-permute-start | bytes 221192 | tf_op jit(solution)/shard_map/ppermute | solution.py:23
  10.9 0.4 collective-permute-start.17
  11.3 7.2 %collective-permute-done.4 = bf16[1,16,2304]{2,1,0:T(8,128)(2,1)S(1)} collective-permute-done((bf16[1,16,2304]{2,1,0:T(8,128)(2,1)S(1)}, bf16[1,16,2304]{2,1,0:T(8,128)(2,1)S(1)}, u32[]{:S(2)}, u32[]{:S(2)}) %collective-permute-start.4) | collective-permute-done | bytes 73760 | tf_op jit(solution)/shard_map/ppermute | solution.py:23
  18.5 0.2 collective-permute-start.5
  18.7 0.0 collective-permute-done.1.refs_4_
  18.7 0.0 collective-permute-done.refs_2_
  18.7 1.9 %collective-permute-start.3 = (bf16[304,256]{1,0:T(8,128)(2,1)S(1)}, bf16[304,256]{1,0:T(8,128)(2,1)S(1)}, u32[]{:S(2)}, u32[]{:S(2)}) collective-permute-start(bf16[304,256]{1,0:T(8,128)(2,1)S(1)} %pad_maximum_fusion.3), channel_id=1, source_target_pairs={{0,1},{1,2},{2,3},{3,0},{4,5},{5,6},{6,7},{7,4},{8,9},{9,10},{10,1... | collective-permute-start | bytes 466952 | tf_op jit(solution)/shard_map/ppermute | solution.py:23
  20.7 2.0 %collective-permute-start.2 = (bf16[304,256]{1,0:T(8,128)(2,1)S(1)}, bf16[304,256]{1,0:T(8,128)(2,1)S(1)}, u32[]{:S(2)}, u32[]{:S(2)}) collective-permute-start(bf16[304,256]{1,0:T(8,128)(2,1)S(1)} %pad_maximum_fusion.3), channel_id=1, source_target_pairs={{0,3},{1,0},{2,1},{3,2},{4,7},{5,4},{6,5},{7,6},{8,11},{9,8},{10,9... | collective-permute-start | bytes 466952 | tf_op jit(solution)/shard_map/ppermute | solution.py:23
  22.6 0.0 collective-permute-done.17
  22.7 0.0 copy-start.1
  22.7 0.0 copy-start.3
  22.7 0.0 copy-start.4
  22.7 0.2 collective-permute-start.18
  22.9 2.9 %collective-permute-done.5 = bf16[2,16,2304]{2,1,0:T(8,128)(2,1)S(1)} collective-permute-done((bf16[2,16,2304]{2,1,0:T(8,128)(2,1)S(1)}, bf16[2,16,2304]{2,1,0:T(8,128)(2,1)S(1)}, u32[]{:S(2)}, u32[]{:S(2)}) %collective-permute-start.5) | collective-permute-done | bytes 147488 | tf_op jit(solution)/shard_map/ppermute | solution.py:23
  25.9 0.7 collective-permute-start.8
  26.6 0.5 collective-permute-start.7
  27.1 10.3 %collective-permute-done.18 = bf16[2,16,4608]{2,1,0:T(8,128)(2,1)S(1)} collective-permute-done((bf16[2,16,4608]{2,1,0:T(8,128)(2,1)S(1)}, bf16[2,16,4608]{2,1,0:T(8,128)(2,1)S(1)}, u32[]{:S(2)}, u32[]{:S(2)}) %collective-permute-start.18) | collective-permute-done | bytes 294944 | tf_op jit(solution)/shard_map/ppermute | solution.py:23
  37.4 1.1 %collective-permute-start.6 = (bf16[3,16,2304]{2,1,0:T(8,128)(2,1)S(1)}, bf16[3,16,2304]{2,1,0:T(8,128)(2,1)S(1)}, u32[]{:S(2)}, u32[]{:S(2)}) collective-permute-start(bf16[3,16,2304]{2,1,0:T(8,128)(2,1)S(1)} %pad_maximum_fusion.2.refs_8_), channel_id=1, source_target_pairs={{0,8},{1,9},{2,10},{3,11},{4,12},{5,13},{6,14},{7,15},{8,0},{9,1},... | collective-permute-start | bytes 663560 | tf_op jit(solution)/shard_map/ppermute | solution.py:23
  38.5 0.0 collective-permute-done.3.refs_5_
  38.5 0.1 collective-permute-start.9
  38.6 0.0 collective-permute-done.8.refs_11_
  38.6 0.5 collective-permute-start.12
  39.1 0.0 collective-permute-done.7.refs_10_
  39.1 0.1 collective-permute-start.11
  39.2 5.2 %collective-permute-done.6.refs_9_ = bf16[3,16,2304]{2,1,0:T(8,128)(2,1)S(1)} collective-permute-done((bf16[3,16,2304]{2,1,0:T(8,128)(2,1)S(1)}, bf16[3,16,2304]{2,1,0:T(8,128)(2,1)S(1)}, u32[]{:S(2)}, u32[]{:S(2)}) %collective-permute-start.6) | collective-permute-done | bytes 221216 | tf_op jit(solution)/shard_map/ppermute | solution.py:23
  44.4 0.0 collective-permute-start.10
  44.4 0.1 pad_maximum_fusion.refs_8_
  44.4 0.0 collective-permute-done.2.refs_3_
  44.4 2.6 %collective-permute-start.21 = (bf16[3,16,4608]{2,1,0:T(8,128)(2,1)S(1)}, bf16[3,16,4608]{2,1,0:T(8,128)(2,1)S(1)}, u32[]{:S(2)}, u32[]{:S(2)}) collective-permute-start(bf16[3,16,4608]{2,1,0:T(8,128)(2,1)S(1)} %pad_maximum_fusion.refs_8_), channel_id=1, source_target_pairs={{0,24},{1,25},{2,26},{3,27},{4,28},{5,29},{6,30},{7,31},{8,16},{9,... | collective-permute-start | bytes 1327112 | tf_op jit(solution)/shard_map/ppermute | solution.py:23
  47.0 0.0 collective-permute-done.9.refs_12_
  47.0 0.7 collective-permute-start.20
  47.7 0.0 collective-permute-done.12.refs_15_
  47.7 0.3 collective-permute-start.19
  48.0 0.0 collective-permute-done.11.refs_14_
  48.0 0.0 collective-permute-done.10.refs_13_
  48.0 0.0 copy-start.5
  48.1 11.5 %first.1 = (bf16[2,32,32,512]{3,2,1,0:T(8,128)(2,1)S(1)}, bf16[80,512]{1,0:T(8,128)(2,1)S(1)}, bf16[64,512]{1,0:T(8,128)(2,1)S(1)}, bf16[80,512]{1,0:T(8,128)(2,1)S(1)}, bf16[64,512]{1,0:T(8,128)(2,1)S(1)}) custom-call(s32[50]{0:T(128)S(1)} %pad_add_fusion.links.refs_0_, bf16[2,32,32,256]{3,2,1,0:T(8,128)(2,1)S(1)} %copy-done.1, ...), custom_call_target="tpu_custom_call" | custom-call | flops 4831838208 | bytes 8388608 | tf_op jit(solution)/shard_map/first/pallas_call | solution.py:310
  59.5 0.1 collective-permute-start.13
  59.6 1.8 %collective-permute-start.22 = (bf16[3,16,4608]{2,1,0:T(8,128)(2,1)S(1)}, bf16[3,16,4608]{2,1,0:T(8,128)(2,1)S(1)}, u32[]{:S(2)}, u32[]{:S(2)}) collective-permute-start(bf16[3,16,4608]{2,1,0:T(8,128)(2,1)S(1)} %pad_maximum_fusion.refs_8_), channel_id=1, source_target_pairs={{0,4},{1,5},{2,6},{3,7},{4,0},{5,1},{6,2},{7,3},{8,12},{9,13},{10,... | collective-permute-start | bytes 1327112 | tf_op jit(solution)/shard_map/ppermute | solution.py:23
  61.4 0.0 collective-permute-done.21.refs_11_
  61.4 0.0 collective-permute-start.25
  61.4 6.4 %collective-permute-done.20.refs_10_ = bf16[3,16,4608]{2,1,0:T(8,128)(2,1)S(1)} collective-permute-done((bf16[3,16,4608]{2,1,0:T(8,128)(2,1)S(1)}, bf16[3,16,4608]{2,1,0:T(8,128)(2,1)S(1)}, u32[]{:S(2)}, u32[]{:S(2)}) %collective-permute-start.20) | collective-permute-done | bytes 442400 | tf_op jit(solution)/shard_map/ppermute | solution.py:23
  67.9 0.0 collective-permute-start.24
  67.9 0.3 collective-permute-done.19.refs_9_
  68.2 0.2 collective-permute-start.23
  68.4 0.0 collective-permute-done.13.refs_2_
  68.4 1.4 %collective-permute-start.14 = (bf16[80,512]{1,0:T(8,128)(2,1)S(1)}, bf16[80,512]{1,0:T(8,128)(2,1)S(1)}, u32[]{:S(2)}, u32[]{:S(2)}) collective-permute-start(bf16[80,512]{1,0:T(8,128)(2,1)S(1)} %get-tuple-element.13), channel_id=1, source_target_pairs={{0,28},{1,29},{2,30},{3,31},{4,0},{5,1},{6,2},{7,3},{8,4},{9,5},{1... | collective-permute-start | bytes 245768 | tf_op jit(solution)/shard_map/ppermute | solution.py:23
  69.8 2.1 %collective-permute-done.14.refs_4_ = bf16[80,512]{1,0:T(8,128)(2,1)S(1)} collective-permute-done((bf16[80,512]{1,0:T(8,128)(2,1)S(1)}, bf16[80,512]{1,0:T(8,128)(2,1)S(1)}, u32[]{:S(2)}, u32[]{:S(2)}) %collective-permute-start.14) | collective-permute-done | bytes 81952 | tf_op jit(solution)/shard_map/ppermute | solution.py:23
  71.9 0.2 collective-permute-start.16
  72.1 7.1 %collective-permute-done.16.refs_5_ = bf16[96,512]{1,0:T(8,128)(2,1)S(1)} collective-permute-done((bf16[96,512]{1,0:T(8,128)(2,1)S(1)}, bf16[96,512]{1,0:T(8,128)(2,1)S(1)}, u32[]{:S(2)}, u32[]{:S(2)}) %collective-permute-start.16) | collective-permute-done | bytes 98336 | tf_op jit(solution)/shard_map/ppermute | solution.py:23
  79.2 1.2 %collective-permute-start.15 = (bf16[96,512]{1,0:T(8,128)(2,1)S(1)}, bf16[96,512]{1,0:T(8,128)(2,1)S(1)}, u32[]{:S(2)}, u32[]{:S(2)}) collective-permute-start(bf16[96,512]{1,0:T(8,128)(2,1)S(1)} %get-tuple-element.20), channel_id=1, source_target_pairs={{0,3},{1,0},{2,1},{3,2},{4,7},{5,4},{6,5},{7,6},{8,11},{9,8},{10,9... | collective-permute-start | bytes 294920 | tf_op jit(solution)/shard_map/ppermute | solution.py:23
  80.4 3.4 %collective-permute-done.15.refs_3_ = bf16[96,512]{1,0:T(8,128)(2,1)S(1)} collective-permute-done((bf16[96,512]{1,0:T(8,128)(2,1)S(1)}, bf16[96,512]{1,0:T(8,128)(2,1)S(1)}, u32[]{:S(2)}, u32[]{:S(2)}) %collective-permute-start.15) | collective-permute-done | bytes 98336 | tf_op jit(solution)/shard_map/ppermute | solution.py:23
  83.8 0.0 collective-permute-done.23.refs_13_
  83.8 19.1 %second.1 = bf16[2,16,16,512]{3,2,1,0:T(8,128)(2,1)} custom-call(s32[50]{0:T(128)S(1)} %pad_add_fusion.links.refs_0_, bf16[2,32,32,512]{3,2,1,0:T(8,128)(2,1)S(1)} %get-tuple-element.10.refs_1_, bf16[80,512]{1,0:T(8,128)(2,1)S(1)} %collective-permute-done.13.refs_2_, bf16[96,512]{1,0:T(8,128)(2,1)S(1)} %collective-permute-done.15.refs_3_, ...), custom_call_target="tpu_custom_call" | custom-call | flops 9663676416 | bytes 8388608 | tf_op jit(solution)/shard_map/second/pallas_call | solution.py:310
  (22 shorter events, 0.2 us)
Async XLA Ops:
  1.8 1.2 %copy-start = (bf16[2,32,32,256]{3,2,1,0:T(8,128)(2,1)S(1)}, bf16[2,32,32,256]{3,2,1,0:T(8,128)(2,1)}, u32[]{:S(2)}) copy-start(bf16[2,32,32,256]{3,2,1,0:T(8,128)(2,1)} %refs_1_.1) | copy-start | bytes 3145732
  3.0 7.8 %copy-start.2 = (bf16[128,4608]{1,0:T(8,128)(2,1)S(1)}, bf16[128,4608]{1,0:T(8,128)(2,1)}, u32[]{:S(2)}) copy-start(bf16[128,4608]{1,0:T(8,128)(2,1)} %refs_7_.3) | copy-start | bytes 3538948
  4.0 14.7 %collective-permute-start.1 = (bf16[272,256]{1,0:T(8,128)(2,1)S(1)}, bf16[272,256]{1,0:T(8,128)(2,1)S(1)}, u32[]{:S(2)}, u32[]{:S(2)}) collective-permute-start(bf16[272,256]{1,0:T(8,128)(2,1)S(1)} %borders.1), channel_id=1, source_target_pairs={{0,28},{1,29},{2,30},{3,31},{4,0},{5,1},{6,2},{7,3},{8,4},{9,5},{1... | collective-permute-start | bytes 417800 | tf_op jit(solution)/shard_map/ppermute | solution.py:23
  7.4 11.3 %collective-permute-start = (bf16[272,256]{1,0:T(8,128)(2,1)S(1)}, bf16[272,256]{1,0:T(8,128)(2,1)S(1)}, u32[]{:S(2)}, u32[]{:S(2)}) collective-permute-start(bf16[272,256]{1,0:T(8,128)(2,1)S(1)} %borders.1), channel_id=1, source_target_pairs={{0,4},{1,5},{2,6},{3,7},{4,8},{5,9},{6,10},{7,11},{8,12},{9,13},{1... | collective-permute-start | bytes 417800 | tf_op jit(solution)/shard_map/ppermute | solution.py:23
  8.3 10.2 %collective-permute-start.4 = (bf16[1,16,2304]{2,1,0:T(8,128)(2,1)S(1)}, bf16[1,16,2304]{2,1,0:T(8,128)(2,1)S(1)}, u32[]{:S(2)}, u32[]{:S(2)}) collective-permute-start(bf16[1,16,2304]{2,1,0:T(8,128)(2,1)S(1)} %constant_dynamic-slice_fusion.1), channel_id=1, source_target_pairs={{0,2},{1,3},{2,0},{3,1},{4,6},{5,7},{6,4},{7,5},{8,10},{9,11},{10,... | collective-permute-start | bytes 221192 | tf_op jit(solution)/shard_map/ppermute | solution.py:23
  10.9 11.8 %collective-permute-start.17 = (bf16[1,16,4608]{2,1,0:T(8,128)(2,1)S(1)}, bf16[1,16,4608]{2,1,0:T(8,128)(2,1)S(1)}, u32[]{:S(2)}, u32[]{:S(2)}) collective-permute-start(bf16[1,16,4608]{2,1,0:T(8,128)(2,1)S(1)} %constant_dynamic-slice_fusion), channel_id=1, source_target_pairs={{0,2},{1,3},{2,0},{3,1},{4,6},{5,7},{6,4},{7,5},{8,10},{9,11},{10,... | collective-permute-start | bytes 442376 | tf_op jit(solution)/shard_map/ppermute | solution.py:23
  18.5 7.3 %collective-permute-start.5 = (bf16[2,16,2304]{2,1,0:T(8,128)(2,1)S(1)}, bf16[2,16,2304]{2,1,0:T(8,128)(2,1)S(1)}, u32[]{:S(2)}, u32[]{:S(2)}) collective-permute-start(bf16[2,16,2304]{2,1,0:T(8,128)(2,1)S(1)} %pad_maximum_fusion.4), channel_id=1, source_target_pairs={{0,1},{1,0},{2,3},{3,2},{4,5},{5,4},{6,7},{7,6},{8,9},{9,8},{10,11... | collective-permute-start | bytes 442376 | tf_op jit(solution)/shard_map/ppermute | solution.py:23
  18.7 19.8 %collective-permute-start.3 = (bf16[304,256]{1,0:T(8,128)(2,1)S(1)}, bf16[304,256]{1,0:T(8,128)(2,1)S(1)}, u32[]{:S(2)}, u32[]{:S(2)}) collective-permute-start(bf16[304,256]{1,0:T(8,128)(2,1)S(1)} %pad_maximum_fusion.3), channel_id=1, source_target_pairs={{0,1},{1,2},{2,3},{3,0},{4,5},{5,6},{6,7},{7,4},{8,9},{9,10},{10,1... | collective-permute-start | bytes 466952 | tf_op jit(solution)/shard_map/ppermute | solution.py:23
  20.7 23.8 %collective-permute-start.2 = (bf16[304,256]{1,0:T(8,128)(2,1)S(1)}, bf16[304,256]{1,0:T(8,128)(2,1)S(1)}, u32[]{:S(2)}, u32[]{:S(2)}) collective-permute-start(bf16[304,256]{1,0:T(8,128)(2,1)S(1)} %pad_maximum_fusion.3), channel_id=1, source_target_pairs={{0,3},{1,0},{2,1},{3,2},{4,7},{5,4},{6,5},{7,6},{8,11},{9,8},{10,9... | collective-permute-start | bytes 466952 | tf_op jit(solution)/shard_map/ppermute | solution.py:23
  22.7 25.4 %copy-start.1 = (bf16[2,32,32,256]{3,2,1,0:T(8,128)(2,1)S(1)}, bf16[2,32,32,256]{3,2,1,0:T(8,128)(2,1)}, u32[]{:S(2)}) copy-start(bf16[2,32,32,256]{3,2,1,0:T(8,128)(2,1)} %refs_1_.1) | copy-start | bytes 3145732
  22.7 25.4 %copy-start.3 = (bf16[128,2304]{1,0:T(8,128)(2,1)S(1)}, bf16[128,2304]{1,0:T(8,128)(2,1)}, u32[]{:S(2)}) copy-start(bf16[128,2304]{1,0:T(8,128)(2,1)} %refs_7_.2) | copy-start | bytes 1769476
  22.7 25.4 %copy-start.4 = (f32[512]{0:T(512)S(1)}, f32[512]{0:T(512)}, u32[]{:S(2)}) copy-start(f32[512]{0:T(512)} %param.9) | copy-start | bytes 6148
  22.7 14.7 %collective-permute-start.18 = (bf16[2,16,4608]{2,1,0:T(8,128)(2,1)S(1)}, bf16[2,16,4608]{2,1,0:T(8,128)(2,1)S(1)}, u32[]{:S(2)}, u32[]{:S(2)}) collective-permute-start(bf16[2,16,4608]{2,1,0:T(8,128)(2,1)S(1)} %pad_maximum_fusion.1), channel_id=1, source_target_pairs={{0,1},{1,0},{2,3},{3,2},{4,5},{5,4},{6,7},{7,6},{8,9},{9,8},{10,11... | collective-permute-start | bytes 884744 | tf_op jit(solution)/shard_map/ppermute | solution.py:23
  25.9 12.7 %collective-permute-start.8 = (bf16[3,16,2304]{2,1,0:T(8,128)(2,1)S(1)}, bf16[3,16,2304]{2,1,0:T(8,128)(2,1)S(1)}, u32[]{:S(2)}, u32[]{:S(2)}) collective-permute-start(bf16[3,16,2304]{2,1,0:T(8,128)(2,1)S(1)} %pad_maximum_fusion.2.refs_8_), channel_id=1, source_target_pairs={{0,24},{1,25},{2,26},{3,27},{4,28},{5,29},{6,30},{7,31},{8,16},{9,... | collective-permute-start | bytes 663560 | tf_op jit(solution)/shard_map/ppermute | solution.py:23
  26.6 12.5 %collective-permute-start.7 = (bf16[3,16,2304]{2,1,0:T(8,128)(2,1)S(1)}, bf16[3,16,2304]{2,1,0:T(8,128)(2,1)S(1)}, u32[]{:S(2)}, u32[]{:S(2)}) collective-permute-start(bf16[3,16,2304]{2,1,0:T(8,128)(2,1)S(1)} %pad_maximum_fusion.2.refs_8_), channel_id=1, source_target_pairs={{0,16},{1,17},{2,18},{3,19},{4,20},{5,21},{6,22},{7,23},{8,24},{9,... | collective-permute-start | bytes 663560 | tf_op jit(solution)/shard_map/ppermute | solution.py:23
  37.4 7.0 %collective-permute-start.6 = (bf16[3,16,2304]{2,1,0:T(8,128)(2,1)S(1)}, bf16[3,16,2304]{2,1,0:T(8,128)(2,1)S(1)}, u32[]{:S(2)}, u32[]{:S(2)}) collective-permute-start(bf16[3,16,2304]{2,1,0:T(8,128)(2,1)S(1)} %pad_maximum_fusion.2.refs_8_), channel_id=1, source_target_pairs={{0,8},{1,9},{2,10},{3,11},{4,12},{5,13},{6,14},{7,15},{8,0},{9,1},... | collective-permute-start | bytes 663560 | tf_op jit(solution)/shard_map/ppermute | solution.py:23
  38.5 8.5 %collective-permute-start.9 = (bf16[3,16,2304]{2,1,0:T(8,128)(2,1)S(1)}, bf16[3,16,2304]{2,1,0:T(8,128)(2,1)S(1)}, u32[]{:S(2)}, u32[]{:S(2)}) collective-permute-start(bf16[3,16,2304]{2,1,0:T(8,128)(2,1)S(1)} %pad_maximum_fusion.2.refs_8_), channel_id=1, source_target_pairs={{0,4},{1,5},{2,6},{3,7},{4,0},{5,1},{6,2},{7,3},{8,12},{9,13},{10,... | collective-permute-start | bytes 663560 | tf_op jit(solution)/shard_map/ppermute | solution.py:23
  38.6 9.1 %collective-permute-start.12 = (bf16[3,16,2304]{2,1,0:T(8,128)(2,1)S(1)}, bf16[3,16,2304]{2,1,0:T(8,128)(2,1)S(1)}, u32[]{:S(2)}, u32[]{:S(2)}) collective-permute-start(bf16[3,16,2304]{2,1,0:T(8,128)(2,1)S(1)} %collective-permute-done.8.refs_11_), channel_id=1, source_target_pairs={{0,4},{1,5},{2,6},{3,7},{4,0},{5,1},{6,2},{7,3},{8,12},{9,13},{10,... | collective-permute-start | bytes 663560 | tf_op jit(solution)/shard_map/ppermute | solution.py:23
  39.1 8.9 %collective-permute-start.11 = (bf16[3,16,2304]{2,1,0:T(8,128)(2,1)S(1)}, bf16[3,16,2304]{2,1,0:T(8,128)(2,1)S(1)}, u32[]{:S(2)}, u32[]{:S(2)}) collective-permute-start(bf16[3,16,2304]{2,1,0:T(8,128)(2,1)S(1)} %collective-permute-done.7.refs_10_), channel_id=1, source_target_pairs={{0,4},{1,5},{2,6},{3,7},{4,0},{5,1},{6,2},{7,3},{8,12},{9,13},{10,... | collective-permute-start | bytes 663560 | tf_op jit(solution)/shard_map/ppermute | solution.py:23
  44.4 3.6 %collective-permute-start.10 = (bf16[3,16,2304]{2,1,0:T(8,128)(2,1)S(1)}, bf16[3,16,2304]{2,1,0:T(8,128)(2,1)S(1)}, u32[]{:S(2)}, u32[]{:S(2)}) collective-permute-start(bf16[3,16,2304]{2,1,0:T(8,128)(2,1)S(1)} %collective-permute-done.6.refs_9_), channel_id=1, source_target_pairs={{0,4},{1,5},{2,6},{3,7},{4,0},{5,1},{6,2},{7,3},{8,12},{9,13},{10,... | collective-permute-start | bytes 663560 | tf_op jit(solution)/shard_map/ppermute | solution.py:23
  44.4 17.0 %collective-permute-start.21 = (bf16[3,16,4608]{2,1,0:T(8,128)(2,1)S(1)}, bf16[3,16,4608]{2,1,0:T(8,128)(2,1)S(1)}, u32[]{:S(2)}, u32[]{:S(2)}) collective-permute-start(bf16[3,16,4608]{2,1,0:T(8,128)(2,1)S(1)} %pad_maximum_fusion.refs_8_), channel_id=1, source_target_pairs={{0,24},{1,25},{2,26},{3,27},{4,28},{5,29},{6,30},{7,31},{8,16},{9,... | collective-permute-start | bytes 1327112 | tf_op jit(solution)/shard_map/ppermute | solution.py:23
  47.0 20.9 %collective-permute-start.20 = (bf16[3,16,4608]{2,1,0:T(8,128)(2,1)S(1)}, bf16[3,16,4608]{2,1,0:T(8,128)(2,1)S(1)}, u32[]{:S(2)}, u32[]{:S(2)}) collective-permute-start(bf16[3,16,4608]{2,1,0:T(8,128)(2,1)S(1)} %pad_maximum_fusion.refs_8_), channel_id=1, source_target_pairs={{0,16},{1,17},{2,18},{3,19},{4,20},{5,21},{6,22},{7,23},{8,24},{9,... | collective-permute-start | bytes 1327112 | tf_op jit(solution)/shard_map/ppermute | solution.py:23
  47.7 20.5 %collective-permute-start.19 = (bf16[3,16,4608]{2,1,0:T(8,128)(2,1)S(1)}, bf16[3,16,4608]{2,1,0:T(8,128)(2,1)S(1)}, u32[]{:S(2)}, u32[]{:S(2)}) collective-permute-start(bf16[3,16,4608]{2,1,0:T(8,128)(2,1)S(1)} %pad_maximum_fusion.refs_8_), channel_id=1, source_target_pairs={{0,8},{1,9},{2,10},{3,11},{4,12},{5,13},{6,14},{7,15},{8,0},{9,1},... | collective-permute-start | bytes 1327112 | tf_op jit(solution)/shard_map/ppermute | solution.py:23
  48.0 35.8 %copy-start.5 = (f32[512]{0:T(512)S(1)}, f32[512]{0:T(512)}, u32[]{:S(2)}) copy-start(f32[512]{0:T(512)} %param.11) | copy-start | bytes 6148
  59.5 8.9 %collective-permute-start.13 = (bf16[80,512]{1,0:T(8,128)(2,1)S(1)}, bf16[80,512]{1,0:T(8,128)(2,1)S(1)}, u32[]{:S(2)}, u32[]{:S(2)}) collective-permute-start(bf16[80,512]{1,0:T(8,128)(2,1)S(1)} %get-tuple-element.11), channel_id=1, source_target_pairs={{0,4},{1,5},{2,6},{3,7},{4,8},{5,9},{6,10},{7,11},{8,12},{9,13},{1... | collective-permute-start | bytes 245768 | tf_op jit(solution)/shard_map/ppermute | solution.py:23
  59.6 24.2 %collective-permute-start.22 = (bf16[3,16,4608]{2,1,0:T(8,128)(2,1)S(1)}, bf16[3,16,4608]{2,1,0:T(8,128)(2,1)S(1)}, u32[]{:S(2)}, u32[]{:S(2)}) collective-permute-start(bf16[3,16,4608]{2,1,0:T(8,128)(2,1)S(1)} %pad_maximum_fusion.refs_8_), channel_id=1, source_target_pairs={{0,4},{1,5},{2,6},{3,7},{4,0},{5,1},{6,2},{7,3},{8,12},{9,13},{10,... | collective-permute-start | bytes 1327112 | tf_op jit(solution)/shard_map/ppermute | solution.py:23
  61.4 22.3 %collective-permute-start.25 = (bf16[3,16,4608]{2,1,0:T(8,128)(2,1)S(1)}, bf16[3,16,4608]{2,1,0:T(8,128)(2,1)S(1)}, u32[]{:S(2)}, u32[]{:S(2)}) collective-permute-start(bf16[3,16,4608]{2,1,0:T(8,128)(2,1)S(1)} %collective-permute-done.21.refs_11_), channel_id=1, source_target_pairs={{0,4},{1,5},{2,6},{3,7},{4,0},{5,1},{6,2},{7,3},{8,12},{9,13},{10,... | collective-permute-start | bytes 1327112 | tf_op jit(solution)/shard_map/ppermute | solution.py:23
  67.9 15.9 %collective-permute-start.24 = (bf16[3,16,4608]{2,1,0:T(8,128)(2,1)S(1)}, bf16[3,16,4608]{2,1,0:T(8,128)(2,1)S(1)}, u32[]{:S(2)}, u32[]{:S(2)}) collective-permute-start(bf16[3,16,4608]{2,1,0:T(8,128)(2,1)S(1)} %collective-permute-done.20.refs_10_), channel_id=1, source_target_pairs={{0,4},{1,5},{2,6},{3,7},{4,0},{5,1},{6,2},{7,3},{8,12},{9,13},{10,... | collective-permute-start | bytes 1327112 | tf_op jit(solution)/shard_map/ppermute | solution.py:23
  68.2 15.6 %collective-permute-start.23 = (bf16[3,16,4608]{2,1,0:T(8,128)(2,1)S(1)}, bf16[3,16,4608]{2,1,0:T(8,128)(2,1)S(1)}, u32[]{:S(2)}, u32[]{:S(2)}) collective-permute-start(bf16[3,16,4608]{2,1,0:T(8,128)(2,1)S(1)} %collective-permute-done.19.refs_9_), channel_id=1, source_target_pairs={{0,4},{1,5},{2,6},{3,7},{4,0},{5,1},{6,2},{7,3},{8,12},{9,13},{10,... | collective-permute-start | bytes 1327112 | tf_op jit(solution)/shard_map/ppermute | solution.py:23
  68.4 3.5 %collective-permute-start.14 = (bf16[80,512]{1,0:T(8,128)(2,1)S(1)}, bf16[80,512]{1,0:T(8,128)(2,1)S(1)}, u32[]{:S(2)}, u32[]{:S(2)}) collective-permute-start(bf16[80,512]{1,0:T(8,128)(2,1)S(1)} %get-tuple-element.13), channel_id=1, source_target_pairs={{0,28},{1,29},{2,30},{3,31},{4,0},{5,1},{6,2},{7,3},{8,4},{9,5},{1... | collective-permute-start | bytes 245768 | tf_op jit(solution)/shard_map/ppermute | solution.py:23
  71.9 7.2 %collective-permute-start.16 = (bf16[96,512]{1,0:T(8,128)(2,1)S(1)}, bf16[96,512]{1,0:T(8,128)(2,1)S(1)}, u32[]{:S(2)}, u32[]{:S(2)}) collective-permute-start(bf16[96,512]{1,0:T(8,128)(2,1)S(1)} %get-tuple-element.19), channel_id=1, source_target_pairs={{0,1},{1,2},{2,3},{3,0},{4,5},{5,6},{6,7},{7,4},{8,9},{9,10},{10,1... | collective-permute-start | bytes 294920 | tf_op jit(solution)/shard_map/ppermute | solution.py:23
  79.2 4.6 %collective-permute-start.15 = (bf16[96,512]{1,0:T(8,128)(2,1)S(1)}, bf16[96,512]{1,0:T(8,128)(2,1)S(1)}, u32[]{:S(2)}, u32[]{:S(2)}) collective-permute-start(bf16[96,512]{1,0:T(8,128)(2,1)S(1)} %get-tuple-element.20), channel_id=1, source_target_pairs={{0,3},{1,0},{2,1},{3,2},{4,7},{5,4},{6,5},{7,6},{8,11},{9,8},{10,9... | collective-permute-start | bytes 294920 | tf_op jit(solution)/shard_map/ppermute | solution.py:23

commit v2 on v1

--- a/solution.py
+++ b/solution.py
@@ -32,7 +32,12 @@
     return bits[::-1]
 
 
-def gather_rows(weight):
+def across(x, dy, dx):
+    tall = lax.axis_size("tile") // 4
+    return move(x, lambda t, f: (((t // 4 + dy) % tall) * 4 + ((t // 2 % 2) ^ dx) * 2 + t % 2, f))
+
+
+def gather_rows(weight, relay):
     rows, cols = (lax.axis_size("tile"), lax.axis_size("fsdp"))
     tall = rows // 4
     share = weight.shape[0] // rows
@@ -45,12 +50,18 @@
         there = move(there, lambda t, f: (t, f ^ bit))
         held.update({h ^ bit: there[i : i + 1] for i, h in enumerate(sorted(held))})
     unit = jnp.concatenate([held[h] for h in range(1, cols)], axis=0)
-    near = [unit]
+    sent = [(unit, 0, 0)]
     for step in range(1, 2 * tall):
-        dy, dx = divmod(step, 2)
-        near.append(move(unit, lambda t, f: (((t // 4 + dy) % tall) * 4 + ((t // 2 % 2) ^ dx) * 2 + t % 2, f)))
-    other = [move(x, lambda t, f: (t ^ 1, f)) for x in near]
-    return near + other
+        if not (relay and step == 3):
+            sent.append((across(unit, *divmod(step, 2)), step, 0))
+    if relay:
+        half = width // 2
+        by_x, by_y = (sent[1][0], sent[2][0])
+        sent.append((across(by_x[:, :, :half], 1, 0), 3, 0))
+        sent.append((across(by_y[:, :, half:], 0, 1), 3, half))
+    other = [move(x, lambda t, f: (t ^ 1, f)) for x, _, _ in sent]
+    places = [(0, *place[1:]) for place in sent] + [(1, *place[1:]) for place in sent]
+    return [x for x, _, _ in sent] + other, places
 
 
 def place(weight, pieces):
@@ -102,9 +113,10 @@
         bundle[pl.ds(start + 2 * edge, edge), :] = chunk[-edge:]
 
 
-def request_of(links, link, tiles, edge, turned):
-    home = lax.rem(links[link], tiles) * 4 + links[link + 1]
-    turns = turned + jnp.where(links[link + 1] >= 2, 1, 0) + jnp.where(links[link + 2] == 1, 0, 1)
+def request_of(links, tile, side, tiles, edge):
+    near_id, near_side, flag = (links[i, tile, side] for i in range(3))
+    home = lax.rem(near_id, tiles) * 4 + near_side
+    turns = (1 if side >= 2 else 0) + jnp.where(near_side >= 2, 1, 0) + jnp.where(flag == 1, 0, 1)
     forward = lax.rem(turns, 2) == 0
     return home * edge + jnp.where(forward, 0, edge - 1), jnp.where(forward, 1, -1)
 
@@ -121,7 +133,7 @@
         row = lax.broadcasted_iota(jnp.int32, cells.shape, 0)
         lane = lax.broadcasted_iota(jnp.int32, cells.shape, 1)
         for side in range(tiles * 4):
-            first, step = request_of(links, 2 + side * 3, tiles, edge, 1 if side % 4 >= 2 else 0)
+            first, step = request_of(links, side // 4, side % 4, tiles, edge)
             asked = jnp.where(lane < 128, first, step).astype(jnp.float32)
             cells = jnp.where(row == tiles * 4 + side, asked, cells)
     bundle[strips:, :] = cells.astype(jnp.bfloat16)
@@ -164,7 +176,7 @@
     )(links, field)
 
 
-def surround(field, near, links, chosen, halos, wide):
+def surround(field, near, side_links, corner_links, chosen, halos, wide):
     tiles, edge, _, channels = field.shape
     strips = tiles * edge if chosen else tiles * 4 * edge
     cells_at = strips if chosen else strips + PAD
@@ -183,16 +195,13 @@
             if chosen:
                 halos[tile, side] = near[side][tile * edge : (tile + 1) * edge, :].astype(jnp.float32)
                 continue
-            first, step = request_of(
-                links, 2 + (tile * 4 + side) * 3, tiles, edge, 1 if side >= 2 else 0
-            )
+            first, step = request_of(side_links, tile, side, tiles, edge)
             picker = one_hot(edge, strips, lambda n: first + step * n)
             halos[tile, side] = select(picker, near[side][:strips, :])
         cells = []
         for corner, (source, low) in enumerate(((3, 0), (1, 0), (1, PAD), (3, PAD))):
-            link = 2 + (tiles * 4 + tile * 4 + corner) * 3
-            pick = lax.rem(links[link], tiles) * 4 + links[link + 1]
-            pick = jnp.where(links[link + 2] == 1, pick, -1)
+            near_id, near_corner, flag = (corner_links[i, tile, corner] for i in range(3))
+            pick = jnp.where(flag == 1, lax.rem(near_id, tiles) * 4 + near_corner, -1)
             picker = one_hot(8, PAD, lambda n: pick)
             cells.append(select(picker, near[source][cells_at + low : cells_at + low + PAD, :])[:1])
         put(tile, 0, halos[tile, 0], cells[0], cells[1])
@@ -207,53 +216,36 @@
                 put(tile, row + 1, field[tile, row], before, after)
 
 
-def fetch_weight(sources, whole, links, sems):
-    copies = []
-    if len(sources) == 1:
-        copies.append(pltpu.make_async_copy(sources[0], whole, sems.at[0]))
+def fetch_weight(sources, places, whole, place_of):
+    own, *pieces = sources
+    hops, share, _ = pieces[0].shape
+    rows = own.shape[0] // share
+    t, f = (place_of[0], place_of[1])
+    tall = rows // 4
+    whole[pl.ds(pl.multiple_of(f * rows * share, share), rows * share), :] = own[...]
+    for piece, (core, step, low) in zip(pieces, places):
+        dy, dx = divmod(step, 2)
+        far_y = lax.rem(t // 4 + tall - dy, tall)
+        far_x = lax.rem(t // 2 + dx, 2)
+        far = far_y * 4 + far_x * 2 + lax.rem(t + core, 2)
+        for hop in range(1, hops + 1):
+            start = pl.multiple_of(((f ^ hop) * rows + far) * share, share)
+            whole[pl.ds(start, share), low : low + piece.shape[2]] = piece[hop - 1]
+
+
+def conv_kernel(places, pooling, *refs):
+    place_of, side_links, corner_links, field, north, east, south, west, bias = refs[:9]
+    near = (north, east, south, west)
+    count = 1 + len(places)
+    sources = refs[9 : 9 + count]
+    outs = refs[9 + count : -5]
+    halos, wide, whole, total, bundle = refs[-5:]
+    tiles, edge, _, channels = field.shape
+    if count == 1:
+        whole = sources[0]
     else:
-        own, *pieces = sources
-        hops, share, _ = pieces[0].shape
-        steps = len(pieces) // 2
-        cols = hops + 1
-        rows = own.shape[0] // share
-        t, f = (links[0], links[1])
-        tall = steps // 2
-        copies.append(
-            pltpu.make_async_copy(
-                own, whole.at[pl.ds(pl.multiple_of(f * rows * share, share), rows * share)], sems.at[0]
-            )
-        )
-        for core in range(2):
-            for step in range(steps):
-                dy, dx = divmod(step, 2)
-                far_y = lax.rem(t // 4 + tall - dy, tall)
-                far_x = lax.rem(t // 2 + dx, 2)
-                far = far_y * 4 + far_x * 2 + lax.rem(t + core, 2)
-                for hop in range(1, cols):
-                    far_f = f ^ hop
-                    start = pl.multiple_of((far_f * rows + far) * share, share)
-                    copies.append(
-                        pltpu.make_async_copy(
-                            pieces[core * steps + step].at[hop - 1], whole.at[pl.ds(start, share)], sems.at[len(copies)]
-                        )
-                    )
-    for copy in copies:
-        copy.start()
-    return copies
-
-
-def conv_kernel(count, pooling, *refs):
-    links, field, north, east, south, west, bias = refs[:7]
-    near = (north, east, south, west)
-    sources = refs[7 : 7 + count]
-    outs = refs[7 + count : -6]
-    halos, wide, whole, sems, total, bundle = refs[-6:]
-    tiles, edge, _, channels = field.shape
-    copies = fetch_weight(sources, whole, links, sems)
-    surround(field, near, links, pooling, halos, wide)
-    for copy in copies:
-        copy.wait()
+        fetch_weight(sources, places, whole, place_of)
+    surround(field, near, side_links, corner_links, pooling, halos, wide)
     rows = edge // 2
     depth = 3 * channels
     for tile in range(tiles):
@@ -293,7 +285,8 @@
                 out[tiles * edge :, :] = bundle[tiles * 4 * edge :, :]
 
 
-def conv(field, near, links, bias, sources, pooling):
+def conv(field, near, links, bias, weight, pooling):
+    sources, places = weight
     tiles, edge, _, channels = field.shape
     width = bias.shape[0]
     if pooling:
@@ -304,19 +297,16 @@
         )
     vmem = pl.BlockSpec(memory_space=pltpu.VMEM)
     smem = pl.BlockSpec(memory_space=pltpu.SMEM)
-    anywhere = pl.BlockSpec(memory_space=pl.ANY)
-    copies = 1 + sum(piece.shape[0] for piece in sources[1:])
     flops = 2 * tiles * edge * edge * 9 * channels * width
     return pl.pallas_call(
-        functools.partial(conv_kernel, len(sources), pooling),
+        functools.partial(conv_kernel, places, pooling),
         out_shape=outs,
-        in_specs=[smem] + [vmem] * 6 + [anywhere] * len(sources),
+        in_specs=[smem] * 3 + [vmem] * (6 + len(sources)),
         out_specs=[vmem] * len(outs),
         scratch_shapes=[
             pltpu.VMEM((tiles, 4, edge, channels), jnp.float32),
             pltpu.VMEM((tiles, edge + 2, edge, 3 * channels), jnp.bfloat16),
-            pltpu.VMEM((width, 9 * channels), jnp.bfloat16),
-            pltpu.SemaphoreType.DMA((copies,)),
+            pltpu.VMEM((width if len(sources) > 1 else 8, 9 * channels), jnp.bfloat16),
             pltpu.VMEM((edge * edge // 4, 128), jnp.float32),
             pltpu.VMEM((tiles * 4 * edge + PAD, width), jnp.bfloat16),
         ],
@@ -324,7 +314,7 @@
         compiler_params=pltpu.CompilerParams(vmem_limit_bytes=GRANT),
         name="second" if pooling else "first",
     )(
-        links,
+        *links,
         field,
         *near,
         bias.reshape(1, width),
@@ -341,27 +331,22 @@
     return north, east, south, west
 
 
-def sources_of(weight):
-    pieces = gather_rows(weight)
+def sources_of(weight, relay):
+    pieces, places = gather_rows(weight, relay)
     if pieces[0].shape[1] % 16 == 0:
-        return (weight, *pieces)
-    return (place(weight, pieces),)
+        return (weight, *pieces), tuple(places)
+    return (place(weight, pieces),), ()
 
 
 def shards(
     tiles_in, first_weight, first_bias, second_weight, second_bias, side_links, corner_links
 ):
-    links = jnp.concatenate(
-        [
-            lax.axis_index("tile").reshape(1),
-            lax.axis_index("fsdp").reshape(1),
-            side_links.reshape(-1),
-            corner_links.reshape(-1),
-        ]
-    )
-    first = sources_of(first_weight)
-    second = sources_of(second_weight)
-    bundle = borders(tiles_in, links)
+    place_of = jnp.stack([lax.axis_index("tile"), lax.axis_index("fsdp")])
+    side_links = side_links.transpose(2, 0, 1)
+    links = (place_of, side_links, corner_links.transpose(2, 0, 1))
+    first = sources_of(first_weight, False)
+    second = sources_of(second_weight, lax.axis_size("tile") == 8)
+    bundle = borders(tiles_in, side_links)
     near = exchange(bundle, bundle, bundle, bundle)
     hidden, *strips = conv(tiles_in, near, links, first_bias, first, False)
     near = exchange(*strips)

time: 103 us -> 88.1 us (0.86)
  waiting for transfers between devices: 45 us -> 35 us
  Pallas kernels: 31.5 us -> 23.1 us
  starting transfers between devices: 22.1 us -> 26.4 us
    ppermute x26 -> x28, waiting for transfers between devices: 45 us -> 35 us  [move(): return lax.ppermute(x, AXES, pairs)]
    pallas_call x2, Pallas kernels: 30.6 us -> 22.1 us  [conv(): pl.pallas_call(functools.partial(conv_kernel, places, pooling), out_shape...]
    ppermute x26 -> x28, starting transfers between devices: 22.1 us -> 26.4 us  [move(): return lax.ppermute(x, AXES, pairs)]
    unnamed x14 -> x18, local copies, waits for them, and re-layouts: 2.81 us -> 1.95 us
  transfers between devices with their start and end apart: 26 -> 28, of which waited for: 9 -> 10; matrix products, arithmetic and copies ran while one was open for 1% -> 1% of each run, Pallas kernels for 11% -> 10%
where the time goes in v2:
time: 88.1 us; the launch traced here: 87.8 us
  waiting for transfers between devices  35 us (40%)
  starting transfers between devices  26.4 us (30%)
  Pallas kernels  23.1 us (26%)
  local copies, waits for them, and re-layouts  2.92 us (3%)
    ppermute x28, waiting for transfers between devices, move(): return lax.ppermute(x, AXES, pairs)  35 us
    ppermute x28, starting transfers between devices, move(): return lax.ppermute(x, AXES, pairs)  26.4 us
    pallas_call x2, Pallas kernels, conv(): pl.pallas_call(functools.partial(conv_kernel, places, pooling), out_shape...  22.1 us
    unnamed x18, local copies, waits for them, and re-layouts  1.95 us
  transfers between devices with their start and end apart: 28, of which 10 were waited for; matrix products, arithmetic and copies ran while one was open for 1% of the time, Pallas kernels for 10%

profile of v2, /device:TPU:0, one launch (start us, length us, event | category | flops | bytes accessed | tf_op | source)
XLA Modules:
  0.0 87.8 jit_solution(18439047546035491952)
XLA Ops:
  0.0 1.2 %copy-done = bf16[2,32,32,256]{3,2,1,0:T(8,128)(2,1)S(1)} copy-done((bf16[2,32,32,256]{3,2,1,0:T(8,128)(2,1)S(1)}, bf16[2,32,32,256]{3,2,1,0:T(8,128)(2,1)}, u32[]{:S(2)}) %copy-start) | copy-done | bytes 1048600
  1.2 0.7 copy-done.4
  1.9 1.0 %borders.1 = bf16[272,256]{1,0:T(8,128)(2,1)S(1)} custom-call(s32[3,2,4]{2,1,0:T(2,128)S(1)} %bitcast.10, bf16[2,32,32,256]{3,2,1,0:T(8,128)(2,1)S(1)} %copy-done), custom_call_target="tpu_custom_call" | custom-call | tf_op jit(solution)/shard_map/borders/pallas_call | solution.py:169
  2.9 3.4 %collective-permute-start.1 = (bf16[272,256]{1,0:T(8,128)(2,1)S(1)}, bf16[272,256]{1,0:T(8,128)(2,1)S(1)}, u32[]{:S(2)}, u32[]{:S(2)}) collective-permute-start(bf16[272,256]{1,0:T(8,128)(2,1)S(1)} %borders.1), channel_id=1, source_target_pairs={{0,28},{1,29},{2,30},{3,31},{4,0},{5,1},{6,2},{7,3},{8,4},{9,5},{1... | collective-permute-start | bytes 417800 | tf_op jit(solution)/shard_map/ppermute | solution.py:23
  6.3 0.0 collective-permute-start
  6.3 0.9 %constant_dynamic-slice_fusion.1 = bf16[1,16,2304]{2,1,0:T(8,128)(2,1)S(1)} fusion(bf16[8,16,2304]{2,1,0:T(8,128)(2,1)} %bitcast.9, s32[]{:T(128)S(6)} %select_n.6), kind=kLoop, calls=%fused_computation.11 | loop fusion | bytes 147460 | tf_op jit(solution)/shard_map/jit(dynamic_index_in_dim)/dynamic_slice | solution.py:46
  7.2 2.6 %collective-permute-start.4 = (bf16[1,16,2304]{2,1,0:T(8,128)(2,1)S(1)}, bf16[1,16,2304]{2,1,0:T(8,128)(2,1)S(1)}, u32[]{:S(2)}, u32[]{:S(2)}) collective-permute-start(bf16[1,16,2304]{2,1,0:T(8,128)(2,1)S(1)} %constant_dynamic-slice_fusion.1), channel_id=1, source_target_pairs={{0,2},{1,3},{2,0},{3,1},{4,6},{5,7},{6,4},{7,5},{8,10},{9,11},{10,... | collective-permute-start | bytes 221192 | tf_op jit(solution)/shard_map/ppermute | solution.py:23
  9.8 0.4 collective-permute-start.17
  10.2 0.1 pad_add_fusion.refs_0_
  10.3 7.1 %collective-permute-done.4 = bf16[1,16,2304]{2,1,0:T(8,128)(2,1)S(1)} collective-permute-done((bf16[1,16,2304]{2,1,0:T(8,128)(2,1)S(1)}, bf16[1,16,2304]{2,1,0:T(8,128)(2,1)S(1)}, u32[]{:S(2)}, u32[]{:S(2)}) %collective-permute-start.4) | collective-permute-done | bytes 73760 | tf_op jit(solution)/shard_map/ppermute | solution.py:23
  17.4 0.2 collective-permute-start.5
  17.6 0.0 collective-permute-done.1.refs_6_
  17.6 0.0 collective-permute-done.refs_4_
  17.7 1.9 %collective-permute-start.3 = (bf16[304,256]{1,0:T(8,128)(2,1)S(1)}, bf16[304,256]{1,0:T(8,128)(2,1)S(1)}, u32[]{:S(2)}, u32[]{:S(2)}) collective-permute-start(bf16[304,256]{1,0:T(8,128)(2,1)S(1)} %pad_maximum_fusion.3), channel_id=1, source_target_pairs={{0,1},{1,2},{2,3},{3,0},{4,5},{5,6},{6,7},{7,4},{8,9},{9,10},{10,1... | collective-permute-start | bytes 466952 | tf_op jit(solution)/shard_map/ppermute | solution.py:23
  19.6 2.0 %collective-permute-start.2 = (bf16[304,256]{1,0:T(8,128)(2,1)S(1)}, bf16[304,256]{1,0:T(8,128)(2,1)S(1)}, u32[]{:S(2)}, u32[]{:S(2)}) collective-permute-start(bf16[304,256]{1,0:T(8,128)(2,1)S(1)} %pad_maximum_fusion.3), channel_id=1, source_target_pairs={{0,3},{1,0},{2,1},{3,2},{4,7},{5,4},{6,5},{7,6},{8,11},{9,8},{10,9... | collective-permute-start | bytes 466952 | tf_op jit(solution)/shard_map/ppermute | solution.py:23
  21.6 0.0 copy-start.1
  21.6 0.0 copy-start.3
  21.6 0.0 copy-start.5
  21.6 0.0 copy-start.6
  21.6 0.0 copy-start.7
  21.6 0.2 collective-permute-start.18
  21.8 2.9 %collective-permute-done.5 = bf16[2,16,2304]{2,1,0:T(8,128)(2,1)S(1)} collective-permute-done((bf16[2,16,2304]{2,1,0:T(8,128)(2,1)S(1)}, bf16[2,16,2304]{2,1,0:T(8,128)(2,1)S(1)}, u32[]{:S(2)}, u32[]{:S(2)}) %collective-permute-start.5) | collective-permute-done | bytes 147488 | tf_op jit(solution)/shard_map/ppermute | solution.py:23
  24.8 0.7 collective-permute-start.8
  25.5 0.5 collective-permute-start.7
  26.0 10.3 %collective-permute-done.18 = bf16[2,16,4608]{2,1,0:T(8,128)(2,1)S(1)} collective-permute-done((bf16[2,16,4608]{2,1,0:T(8,128)(2,1)S(1)}, bf16[2,16,4608]{2,1,0:T(8,128)(2,1)S(1)}, u32[]{:S(2)}, u32[]{:S(2)}) %collective-permute-start.18) | collective-permute-done | bytes 294944 | tf_op jit(solution)/shard_map/ppermute | solution.py:23
  36.3 1.1 %collective-permute-start.6 = (bf16[3,16,2304]{2,1,0:T(8,128)(2,1)S(1)}, bf16[3,16,2304]{2,1,0:T(8,128)(2,1)S(1)}, u32[]{:S(2)}, u32[]{:S(2)}) collective-permute-start(bf16[3,16,2304]{2,1,0:T(8,128)(2,1)S(1)} %pad_maximum_fusion.2.refs_10_), channel_id=1, source_target_pairs={{0,8},{1,9},{2,10},{3,11},{4,12},{5,13},{6,14},{7,15},{8,0},{9,1},... | collective-permute-start | bytes 663560 | tf_op jit(solution)/shard_map/ppermute | solution.py:23
  37.4 0.0 collective-permute-done.3.refs_7_
  37.4 0.1 collective-permute-start.9
  37.5 0.0 collective-permute-done.8.refs_13_
  37.5 0.5 collective-permute-start.12
  38.0 0.1 collective-permute-start.11
  38.1 5.2 %collective-permute-done.6.refs_11_ = bf16[3,16,2304]{2,1,0:T(8,128)(2,1)S(1)} collective-permute-done((bf16[3,16,2304]{2,1,0:T(8,128)(2,1)S(1)}, bf16[3,16,2304]{2,1,0:T(8,128)(2,1)S(1)}, u32[]{:S(2)}, u32[]{:S(2)}) %collective-permute-start.6) | collective-permute-done | bytes 221216 | tf_op jit(solution)/shard_map/ppermute | solution.py:23
  43.3 0.0 collective-permute-start.10
  43.3 0.1 pad_maximum_fusion.refs_10_
  43.4 0.0 collective-permute-done.2.refs_5_
  43.4 1.8 %collective-permute-start.20 = (bf16[3,16,4608]{2,1,0:T(8,128)(2,1)S(1)}, bf16[3,16,4608]{2,1,0:T(8,128)(2,1)S(1)}, u32[]{:S(2)}, u32[]{:S(2)}) collective-permute-start(bf16[3,16,4608]{2,1,0:T(8,128)(2,1)S(1)} %pad_maximum_fusion.refs_10_), channel_id=1, source_target_pairs={{0,16},{1,17},{2,18},{3,19},{4,20},{5,21},{6,22},{7,23},{8,24},{9,... | collective-permute-start | bytes 1327112 | tf_op jit(solution)/shard_map/ppermute | solution.py:23
  45.1 1.4 %collective-permute-start.19 = (bf16[3,16,4608]{2,1,0:T(8,128)(2,1)S(1)}, bf16[3,16,4608]{2,1,0:T(8,128)(2,1)S(1)}, u32[]{:S(2)}, u32[]{:S(2)}) collective-permute-start(bf16[3,16,4608]{2,1,0:T(8,128)(2,1)S(1)} %pad_maximum_fusion.refs_10_), channel_id=1, source_target_pairs={{0,8},{1,9},{2,10},{3,11},{4,12},{5,13},{6,14},{7,15},{8,0},{9,1},... | collective-permute-start | bytes 1327112 | tf_op jit(solution)/shard_map/ppermute | solution.py:23
  46.5 0.0 collective-permute-done.12.refs_17_
  46.6 8.5 %first.1 = (bf16[2,32,32,512]{3,2,1,0:T(8,128)(2,1)S(1)}, bf16[80,512]{1,0:T(8,128)(2,1)S(1)}, bf16[64,512]{1,0:T(8,128)(2,1)S(1)}, bf16[80,512]{1,0:T(8,128)(2,1)S(1)}, bf16[64,512]{1,0:T(8,128)(2,1)S(1)}) custom-call(s32[2]{0:T(128)S(1)} %pad_add_fusion.refs_0_, s32[3,2,4]{2,1,0:T(2,128)S(1)} %bitcast.11, s32[3,2,4]{2,1,0:T(2,128)S(1)} %bitcast.13, ...), custom_call_target="tpu_custom_call" | custom-call | flops 4831838208 | bytes 8388608 | tf_op jit(solution)/shard_map/first/pallas_call | solution.py:301
  55.1 0.0 copy-start.8
  55.1 0.1 collective-permute-start.13
  55.2 2.6 %collective-permute-start.14 = (bf16[80,512]{1,0:T(8,128)(2,1)S(1)}, bf16[80,512]{1,0:T(8,128)(2,1)S(1)}, u32[]{:S(2)}, u32[]{:S(2)}) collective-permute-start(bf16[80,512]{1,0:T(8,128)(2,1)S(1)} %get-tuple-element.13), channel_id=1, source_target_pairs={{0,28},{1,29},{2,30},{3,31},{4,0},{5,1},{6,2},{7,3},{8,4},{9,5},{1... | collective-permute-start | bytes 245768 | tf_op jit(solution)/shard_map/ppermute | solution.py:23
  57.8 2.9 %collective-permute-done.13.refs_4_ = bf16[80,512]{1,0:T(8,128)(2,1)S(1)} collective-permute-done((bf16[80,512]{1,0:T(8,128)(2,1)S(1)}, bf16[80,512]{1,0:T(8,128)(2,1)S(1)}, u32[]{:S(2)}, u32[]{:S(2)}) %collective-permute-start.13) | collective-permute-done | bytes 81952 | tf_op jit(solution)/shard_map/ppermute | solution.py:23
  60.7 0.0 collective-permute-done.14.refs_6_
  60.7 0.4 collective-permute-start.16
  61.1 3.5 %collective-permute-start.15 = (bf16[96,512]{1,0:T(8,128)(2,1)S(1)}, bf16[96,512]{1,0:T(8,128)(2,1)S(1)}, u32[]{:S(2)}, u32[]{:S(2)}) collective-permute-start(bf16[96,512]{1,0:T(8,128)(2,1)S(1)} %get-tuple-element.20), channel_id=1, source_target_pairs={{0,3},{1,0},{2,1},{3,2},{4,7},{5,4},{6,5},{7,6},{8,11},{9,8},{10,9... | collective-permute-start | bytes 294920 | tf_op jit(solution)/shard_map/ppermute | solution.py:23
  64.6 0.0 collective-permute-start.23
  64.6 0.0 collective-permute-done.20.refs_12_
  64.6 1.0 %collective-permute-start.22 = (bf16[3,16,2304]{2,1,0:T(8,128)(2,1)S(1)}, bf16[3,16,2304]{2,1,0:T(8,128)(2,1)S(1)}, u32[]{:S(2)}, u32[]{:S(2)}) collective-permute-start(bf16[3,16,2304]{2,1,0:T(8,128)(2,1)S(1)} %slice.49), channel_id=1, source_target_pairs={{0,8},{1,9},{2,10},{3,11},{4,12},{5,13},{6,14},{7,15},{8,0},{9,1},... | collective-permute-start | bytes 663560 | tf_op jit(solution)/shard_map/ppermute | solution.py:23
  65.6 0.0 collective-permute-done.19.refs_11_
  65.7 1.4 %collective-permute-start.21 = (bf16[3,16,2304]{2,1,0:T(8,128)(2,1)S(1)}, bf16[3,16,2304]{2,1,0:T(8,128)(2,1)S(1)}, u32[]{:S(2)}, u32[]{:S(2)}) collective-permute-start(bf16[3,16,2304]{2,1,0:T(8,128)(2,1)S(1)} %slice.48), channel_id=1, source_target_pairs={{0,16},{1,17},{2,18},{3,19},{4,20},{5,21},{6,22},{7,23},{8,24},{9,... | collective-permute-start | bytes 663560 | tf_op jit(solution)/shard_map/ppermute | solution.py:23
  67.0 0.8 collective-permute-done.16.refs_7_
  67.8 0.0 collective-permute-start.25
  67.8 0.0 collective-permute-done.15.refs_5_
  67.8 0.5 collective-permute-start.24
  68.4 4.2 %collective-permute-done.22.refs_14_ = bf16[3,16,2304]{2,1,0:T(8,128)(2,1)S(1)} collective-permute-done((bf16[3,16,2304]{2,1,0:T(8,128)(2,1)S(1)}, bf16[3,16,2304]{2,1,0:T(8,128)(2,1)S(1)}, u32[]{:S(2)}, u32[]{:S(2)}) %collective-permute-start.22) | collective-permute-done | bytes 221216 | tf_op jit(solution)/shard_map/ppermute | solution.py:23
  72.5 0.0 collective-permute-start.27
  72.5 0.3 collective-permute-done.21.refs_13_
  72.8 0.2 collective-permute-start.26
  73.0 0.0 collective-permute-done.23.refs_15_
  73.0 1.0 %collective-permute-done.27.refs_19_ = bf16[3,16,2304]{2,1,0:T(8,128)(2,1)S(1)} collective-permute-done((bf16[3,16,2304]{2,1,0:T(8,128)(2,1)S(1)}, bf16[3,16,2304]{2,1,0:T(8,128)(2,1)S(1)}, u32[]{:S(2)}, u32[]{:S(2)}) %collective-permute-start.27) | collective-permute-done | bytes 221216 | tf_op jit(solution)/shard_map/ppermute | solution.py:23
  74.0 0.0 collective-permute-done.25.refs_17_
  74.0 0.3 collective-permute-done.26.refs_18_
  74.3 13.5 %second.1 = bf16[2,16,16,512]{3,2,1,0:T(8,128)(2,1)} custom-call(s32[2]{0:T(128)S(1)} %pad_add_fusion.refs_0_, s32[3,2,4]{2,1,0:T(2,128)S(1)} %bitcast.12, s32[3,2,4]{2,1,0:T(2,128)S(1)} %bitcast.14, bf16[2,32,32,512]{3,2,1,0:T(8,128)(2,1)S(1)} %get-tuple-element.10.refs_3_, bf16[80,512]{1,0:T(8,128)(2,1)S(1)} %collective-permute-done.13.refs_4_, ...), custom_call_target="tpu_custom_call" | custom-call | flops 9663676416 | bytes 8388608 | tf_op jit(solution)/shard_map/second/pallas_call | solution.py:301
  (30 shorter events, 0.2 us)
Async XLA Ops:
  0.0 1.2 %copy-start = (bf16[2,32,32,256]{3,2,1,0:T(8,128)(2,1)S(1)}, bf16[2,32,32,256]{3,2,1,0:T(8,128)(2,1)}, u32[]{:S(2)}) copy-start(bf16[2,32,32,256]{3,2,1,0:T(8,128)(2,1)} %refs_3_.1) | copy-start | bytes 3145732
  1.2 0.7 copy-start.4
  1.9 7.9 %copy-start.2 = (bf16[128,4608]{1,0:T(8,128)(2,1)S(1)}, bf16[128,4608]{1,0:T(8,128)(2,1)}, u32[]{:S(2)}) copy-start(bf16[128,4608]{1,0:T(8,128)(2,1)} %refs_9_.3) | copy-start | bytes 3538948
  2.9 14.7 %collective-permute-start.1 = (bf16[272,256]{1,0:T(8,128)(2,1)S(1)}, bf16[272,256]{1,0:T(8,128)(2,1)S(1)}, u32[]{:S(2)}, u32[]{:S(2)}) collective-permute-start(bf16[272,256]{1,0:T(8,128)(2,1)S(1)} %borders.1), channel_id=1, source_target_pairs={{0,28},{1,29},{2,30},{3,31},{4,0},{5,1},{6,2},{7,3},{8,4},{9,5},{1... | collective-permute-start | bytes 417800 | tf_op jit(solution)/shard_map/ppermute | solution.py:23
  6.3 11.3 %collective-permute-start = (bf16[272,256]{1,0:T(8,128)(2,1)S(1)}, bf16[272,256]{1,0:T(8,128)(2,1)S(1)}, u32[]{:S(2)}, u32[]{:S(2)}) collective-permute-start(bf16[272,256]{1,0:T(8,128)(2,1)S(1)} %borders.1), channel_id=1, source_target_pairs={{0,4},{1,5},{2,6},{3,7},{4,8},{5,9},{6,10},{7,11},{8,12},{9,13},{1... | collective-permute-start | bytes 417800 | tf_op jit(solution)/shard_map/ppermute | solution.py:23
  7.2 10.2 %collective-permute-start.4 = (bf16[1,16,2304]{2,1,0:T(8,128)(2,1)S(1)}, bf16[1,16,2304]{2,1,0:T(8,128)(2,1)S(1)}, u32[]{:S(2)}, u32[]{:S(2)}) collective-permute-start(bf16[1,16,2304]{2,1,0:T(8,128)(2,1)S(1)} %constant_dynamic-slice_fusion.1), channel_id=1, source_target_pairs={{0,2},{1,3},{2,0},{3,1},{4,6},{5,7},{6,4},{7,5},{8,10},{9,11},{10,... | collective-permute-start | bytes 221192 | tf_op jit(solution)/shard_map/ppermute | solution.py:23
  9.8 11.8 %collective-permute-start.17 = (bf16[1,16,4608]{2,1,0:T(8,128)(2,1)S(1)}, bf16[1,16,4608]{2,1,0:T(8,128)(2,1)S(1)}, u32[]{:S(2)}, u32[]{:S(2)}) collective-permute-start(bf16[1,16,4608]{2,1,0:T(8,128)(2,1)S(1)} %constant_dynamic-slice_fusion), channel_id=1, source_target_pairs={{0,2},{1,3},{2,0},{3,1},{4,6},{5,7},{6,4},{7,5},{8,10},{9,11},{10,... | collective-permute-start | bytes 442376 | tf_op jit(solution)/shard_map/ppermute | solution.py:23
  17.4 7.3 %collective-permute-start.5 = (bf16[2,16,2304]{2,1,0:T(8,128)(2,1)S(1)}, bf16[2,16,2304]{2,1,0:T(8,128)(2,1)S(1)}, u32[]{:S(2)}, u32[]{:S(2)}) collective-permute-start(bf16[2,16,2304]{2,1,0:T(8,128)(2,1)S(1)} %pad_maximum_fusion.4), channel_id=1, source_target_pairs={{0,1},{1,0},{2,3},{3,2},{4,5},{5,4},{6,7},{7,6},{8,9},{9,8},{10,11... | collective-permute-start | bytes 442376 | tf_op jit(solution)/shard_map/ppermute | solution.py:23
  17.7 19.8 %collective-permute-start.3 = (bf16[304,256]{1,0:T(8,128)(2,1)S(1)}, bf16[304,256]{1,0:T(8,128)(2,1)S(1)}, u32[]{:S(2)}, u32[]{:S(2)}) collective-permute-start(bf16[304,256]{1,0:T(8,128)(2,1)S(1)} %pad_maximum_fusion.3), channel_id=1, source_target_pairs={{0,1},{1,2},{2,3},{3,0},{4,5},{5,6},{6,7},{7,4},{8,9},{9,10},{10,1... | collective-permute-start | bytes 466952 | tf_op jit(solution)/shard_map/ppermute | solution.py:23
  19.6 23.8 %collective-permute-start.2 = (bf16[304,256]{1,0:T(8,128)(2,1)S(1)}, bf16[304,256]{1,0:T(8,128)(2,1)S(1)}, u32[]{:S(2)}, u32[]{:S(2)}) collective-permute-start(bf16[304,256]{1,0:T(8,128)(2,1)S(1)} %pad_maximum_fusion.3), channel_id=1, source_target_pairs={{0,3},{1,0},{2,1},{3,2},{4,7},{5,4},{6,5},{7,6},{8,11},{9,8},{10,9... | collective-permute-start | bytes 466952 | tf_op jit(solution)/shard_map/ppermute | solution.py:23
  21.6 24.9 %copy-start.1 = (bf16[2,32,32,256]{3,2,1,0:T(8,128)(2,1)S(1)}, bf16[2,32,32,256]{3,2,1,0:T(8,128)(2,1)}, u32[]{:S(2)}) copy-start(bf16[2,32,32,256]{3,2,1,0:T(8,128)(2,1)} %refs_3_.1) | copy-start | bytes 3145732
  21.6 24.9 %copy-start.3 = (bf16[128,2304]{1,0:T(8,128)(2,1)S(1)}, bf16[128,2304]{1,0:T(8,128)(2,1)}, u32[]{:S(2)}) copy-start(bf16[128,2304]{1,0:T(8,128)(2,1)} %refs_9_.2) | copy-start | bytes 1769476
  21.6 24.9 %copy-start.5 = (s32[2,4,3]{1,0,2:T(2,128)S(1)}, s32[2,4,3]{1,0,2:T(2,128)}, u32[]{:S(2)}) copy-start(s32[2,4,3]{1,0,2:T(2,128)} %param.12) | copy-start | bytes 292
  21.6 24.9 %copy-start.6 = (s32[2,4,3]{1,0,2:T(2,128)S(1)}, s32[2,4,3]{1,0,2:T(2,128)}, u32[]{:S(2)}) copy-start(s32[2,4,3]{1,0,2:T(2,128)} %param.13) | copy-start | bytes 292
  21.6 24.9 %copy-start.7 = (f32[512]{0:T(512)S(1)}, f32[512]{0:T(512)}, u32[]{:S(2)}) copy-start(f32[512]{0:T(512)} %param.9) | copy-start | bytes 6148
  21.6 14.7 %collective-permute-start.18 = (bf16[2,16,4608]{2,1,0:T(8,128)(2,1)S(1)}, bf16[2,16,4608]{2,1,0:T(8,128)(2,1)S(1)}, u32[]{:S(2)}, u32[]{:S(2)}) collective-permute-start(bf16[2,16,4608]{2,1,0:T(8,128)(2,1)S(1)} %pad_maximum_fusion.1), channel_id=1, source_target_pairs={{0,1},{1,0},{2,3},{3,2},{4,5},{5,4},{6,7},{7,6},{8,9},{9,8},{10,11... | collective-permute-start | bytes 884744 | tf_op jit(solution)/shard_map/ppermute | solution.py:23
  24.8 12.7 %collective-permute-start.8 = (bf16[3,16,2304]{2,1,0:T(8,128)(2,1)S(1)}, bf16[3,16,2304]{2,1,0:T(8,128)(2,1)S(1)}, u32[]{:S(2)}, u32[]{:S(2)}) collective-permute-start(bf16[3,16,2304]{2,1,0:T(8,128)(2,1)S(1)} %pad_maximum_fusion.2.refs_10_), channel_id=1, source_target_pairs={{0,24},{1,25},{2,26},{3,27},{4,28},{5,29},{6,30},{7,31},{8,16},{9,... | collective-permute-start | bytes 663560 | tf_op jit(solution)/shard_map/ppermute | solution.py:23
  25.5 12.5 %collective-permute-start.7 = (bf16[3,16,2304]{2,1,0:T(8,128)(2,1)S(1)}, bf16[3,16,2304]{2,1,0:T(8,128)(2,1)S(1)}, u32[]{:S(2)}, u32[]{:S(2)}) collective-permute-start(bf16[3,16,2304]{2,1,0:T(8,128)(2,1)S(1)} %pad_maximum_fusion.2.refs_10_), channel_id=1, source_target_pairs={{0,16},{1,17},{2,18},{3,19},{4,20},{5,21},{6,22},{7,23},{8,24},{9,... | collective-permute-start | bytes 663560 | tf_op jit(solution)/shard_map/ppermute | solution.py:23
  36.3 7.0 %collective-permute-start.6 = (bf16[3,16,2304]{2,1,0:T(8,128)(2,1)S(1)}, bf16[3,16,2304]{2,1,0:T(8,128)(2,1)S(1)}, u32[]{:S(2)}, u32[]{:S(2)}) collective-permute-start(bf16[3,16,2304]{2,1,0:T(8,128)(2,1)S(1)} %pad_maximum_fusion.2.refs_10_), channel_id=1, source_target_pairs={{0,8},{1,9},{2,10},{3,11},{4,12},{5,13},{6,14},{7,15},{8,0},{9,1},... | collective-permute-start | bytes 663560 | tf_op jit(solution)/shard_map/ppermute | solution.py:23
  37.4 7.7 %collective-permute-start.9 = (bf16[3,16,2304]{2,1,0:T(8,128)(2,1)S(1)}, bf16[3,16,2304]{2,1,0:T(8,128)(2,1)S(1)}, u32[]{:S(2)}, u32[]{:S(2)}) collective-permute-start(bf16[3,16,2304]{2,1,0:T(8,128)(2,1)S(1)} %pad_maximum_fusion.2.refs_10_), channel_id=1, source_target_pairs={{0,4},{1,5},{2,6},{3,7},{4,0},{5,1},{6,2},{7,3},{8,12},{9,13},{10,... | collective-permute-start | bytes 663560 | tf_op jit(solution)/shard_map/ppermute | solution.py:23
  37.5 9.0 %collective-permute-start.12 = (bf16[3,16,2304]{2,1,0:T(8,128)(2,1)S(1)}, bf16[3,16,2304]{2,1,0:T(8,128)(2,1)S(1)}, u32[]{:S(2)}, u32[]{:S(2)}) collective-permute-start(bf16[3,16,2304]{2,1,0:T(8,128)(2,1)S(1)} %collective-permute-done.8.refs_13_), channel_id=1, source_target_pairs={{0,4},{1,5},{2,6},{3,7},{4,0},{5,1},{6,2},{7,3},{8,12},{9,13},{10,... | collective-permute-start | bytes 663560 | tf_op jit(solution)/shard_map/ppermute | solution.py:23
  38.0 8.5 %collective-permute-start.11 = (bf16[3,16,2304]{2,1,0:T(8,128)(2,1)S(1)}, bf16[3,16,2304]{2,1,0:T(8,128)(2,1)S(1)}, u32[]{:S(2)}, u32[]{:S(2)}) collective-permute-start(bf16[3,16,2304]{2,1,0:T(8,128)(2,1)S(1)} %collective-permute-done.7.refs_12_), channel_id=1, source_target_pairs={{0,4},{1,5},{2,6},{3,7},{4,0},{5,1},{6,2},{7,3},{8,12},{9,13},{10,... | collective-permute-start | bytes 663560 | tf_op jit(solution)/shard_map/ppermute | solution.py:23
  43.3 3.2 %collective-permute-start.10 = (bf16[3,16,2304]{2,1,0:T(8,128)(2,1)S(1)}, bf16[3,16,2304]{2,1,0:T(8,128)(2,1)S(1)}, u32[]{:S(2)}, u32[]{:S(2)}) collective-permute-start(bf16[3,16,2304]{2,1,0:T(8,128)(2,1)S(1)} %collective-permute-done.6.refs_11_), channel_id=1, source_target_pairs={{0,4},{1,5},{2,6},{3,7},{4,0},{5,1},{6,2},{7,3},{8,12},{9,13},{10,... | collective-permute-start | bytes 663560 | tf_op jit(solution)/shard_map/ppermute | solution.py:23
  43.4 21.2 %collective-permute-start.20 = (bf16[3,16,4608]{2,1,0:T(8,128)(2,1)S(1)}, bf16[3,16,4608]{2,1,0:T(8,128)(2,1)S(1)}, u32[]{:S(2)}, u32[]{:S(2)}) collective-permute-start(bf16[3,16,4608]{2,1,0:T(8,128)(2,1)S(1)} %pad_maximum_fusion.refs_10_), channel_id=1, source_target_pairs={{0,16},{1,17},{2,18},{3,19},{4,20},{5,21},{6,22},{7,23},{8,24},{9,... | collective-permute-start | bytes 1327112 | tf_op jit(solution)/shard_map/ppermute | solution.py:23
  45.1 20.5 %collective-permute-start.19 = (bf16[3,16,4608]{2,1,0:T(8,128)(2,1)S(1)}, bf16[3,16,4608]{2,1,0:T(8,128)(2,1)S(1)}, u32[]{:S(2)}, u32[]{:S(2)}) collective-permute-start(bf16[3,16,4608]{2,1,0:T(8,128)(2,1)S(1)} %pad_maximum_fusion.refs_10_), channel_id=1, source_target_pairs={{0,8},{1,9},{2,10},{3,11},{4,12},{5,13},{6,14},{7,15},{8,0},{9,1},... | collective-permute-start | bytes 1327112 | tf_op jit(solution)/shard_map/ppermute | solution.py:23
  55.1 19.2 %copy-start.8 = (f32[512]{0:T(512)S(1)}, f32[512]{0:T(512)}, u32[]{:S(2)}) copy-start(f32[512]{0:T(512)} %param.11) | copy-start | bytes 6148
  55.1 5.6 %collective-permute-start.13 = (bf16[80,512]{1,0:T(8,128)(2,1)S(1)}, bf16[80,512]{1,0:T(8,128)(2,1)S(1)}, u32[]{:S(2)}, u32[]{:S(2)}) collective-permute-start(bf16[80,512]{1,0:T(8,128)(2,1)S(1)} %get-tuple-element.11), channel_id=1, source_target_pairs={{0,4},{1,5},{2,6},{3,7},{4,8},{5,9},{6,10},{7,11},{8,12},{9,13},{1... | collective-permute-start | bytes 245768 | tf_op jit(solution)/shard_map/ppermute | solution.py:23
  55.2 5.5 %collective-permute-start.14 = (bf16[80,512]{1,0:T(8,128)(2,1)S(1)}, bf16[80,512]{1,0:T(8,128)(2,1)S(1)}, u32[]{:S(2)}, u32[]{:S(2)}) collective-permute-start(bf16[80,512]{1,0:T(8,128)(2,1)S(1)} %get-tuple-element.13), channel_id=1, source_target_pairs={{0,28},{1,29},{2,30},{3,31},{4,0},{5,1},{6,2},{7,3},{8,4},{9,5},{1... | collective-permute-start | bytes 245768 | tf_op jit(solution)/shard_map/ppermute | solution.py:23
  60.7 7.1 %collective-permute-start.16 = (bf16[96,512]{1,0:T(8,128)(2,1)S(1)}, bf16[96,512]{1,0:T(8,128)(2,1)S(1)}, u32[]{:S(2)}, u32[]{:S(2)}) collective-permute-start(bf16[96,512]{1,0:T(8,128)(2,1)S(1)} %get-tuple-element.19), channel_id=1, source_target_pairs={{0,1},{1,2},{2,3},{3,0},{4,5},{5,6},{6,7},{7,4},{8,9},{9,10},{10,1... | collective-permute-start | bytes 294920 | tf_op jit(solution)/shard_map/ppermute | solution.py:23
  61.1 6.8 %collective-permute-start.15 = (bf16[96,512]{1,0:T(8,128)(2,1)S(1)}, bf16[96,512]{1,0:T(8,128)(2,1)S(1)}, u32[]{:S(2)}, u32[]{:S(2)}) collective-permute-start(bf16[96,512]{1,0:T(8,128)(2,1)S(1)} %get-tuple-element.20), channel_id=1, source_target_pairs={{0,3},{1,0},{2,1},{3,2},{4,7},{5,4},{6,5},{7,6},{8,11},{9,8},{10,9... | collective-permute-start | bytes 294920 | tf_op jit(solution)/shard_map/ppermute | solution.py:23
  64.6 8.4 %collective-permute-start.23 = (bf16[3,16,4608]{2,1,0:T(8,128)(2,1)S(1)}, bf16[3,16,4608]{2,1,0:T(8,128)(2,1)S(1)}, u32[]{:S(2)}, u32[]{:S(2)}) collective-permute-start(bf16[3,16,4608]{2,1,0:T(8,128)(2,1)S(1)} %pad_maximum_fusion.refs_10_), channel_id=1, source_target_pairs={{0,4},{1,5},{2,6},{3,7},{4,0},{5,1},{6,2},{7,3},{8,12},{9,13},{10,... | collective-permute-start | bytes 1327112 | tf_op jit(solution)/shard_map/ppermute | solution.py:23
  64.6 7.9 %collective-permute-start.22 = (bf16[3,16,2304]{2,1,0:T(8,128)(2,1)S(1)}, bf16[3,16,2304]{2,1,0:T(8,128)(2,1)S(1)}, u32[]{:S(2)}, u32[]{:S(2)}) collective-permute-start(bf16[3,16,2304]{2,1,0:T(8,128)(2,1)S(1)} %slice.49), channel_id=1, source_target_pairs={{0,8},{1,9},{2,10},{3,11},{4,12},{5,13},{6,14},{7,15},{8,0},{9,1},... | collective-permute-start | bytes 663560 | tf_op jit(solution)/shard_map/ppermute | solution.py:23
  65.7 7.1 %collective-permute-start.21 = (bf16[3,16,2304]{2,1,0:T(8,128)(2,1)S(1)}, bf16[3,16,2304]{2,1,0:T(8,128)(2,1)S(1)}, u32[]{:S(2)}, u32[]{:S(2)}) collective-permute-start(bf16[3,16,2304]{2,1,0:T(8,128)(2,1)S(1)} %slice.48), channel_id=1, source_target_pairs={{0,16},{1,17},{2,18},{3,19},{4,20},{5,21},{6,22},{7,23},{8,24},{9,... | collective-permute-start | bytes 663560 | tf_op jit(solution)/shard_map/ppermute | solution.py:23
  67.8 6.2 %collective-permute-start.25 = (bf16[3,16,4608]{2,1,0:T(8,128)(2,1)S(1)}, bf16[3,16,4608]{2,1,0:T(8,128)(2,1)S(1)}, u32[]{:S(2)}, u32[]{:S(2)}) collective-permute-start(bf16[3,16,4608]{2,1,0:T(8,128)(2,1)S(1)} %collective-permute-done.20.refs_12_), channel_id=1, source_target_pairs={{0,4},{1,5},{2,6},{3,7},{4,0},{5,1},{6,2},{7,3},{8,12},{9,13},{10,... | collective-permute-start | bytes 1327112 | tf_op jit(solution)/shard_map/ppermute | solution.py:23
  67.8 6.5 %collective-permute-start.24 = (bf16[3,16,4608]{2,1,0:T(8,128)(2,1)S(1)}, bf16[3,16,4608]{2,1,0:T(8,128)(2,1)S(1)}, u32[]{:S(2)}, u32[]{:S(2)}) collective-permute-start(bf16[3,16,4608]{2,1,0:T(8,128)(2,1)S(1)} %collective-permute-done.19.refs_11_), channel_id=1, source_target_pairs={{0,4},{1,5},{2,6},{3,7},{4,0},{5,1},{6,2},{7,3},{8,12},{9,13},{10,... | collective-permute-start | bytes 1327112 | tf_op jit(solution)/shard_map/ppermute | solution.py:23
  72.5 1.5 %collective-permute-start.27 = (bf16[3,16,2304]{2,1,0:T(8,128)(2,1)S(1)}, bf16[3,16,2304]{2,1,0:T(8,128)(2,1)S(1)}, u32[]{:S(2)}, u32[]{:S(2)}) collective-permute-start(bf16[3,16,2304]{2,1,0:T(8,128)(2,1)S(1)} %collective-permute-done.22.refs_14_), channel_id=1, source_target_pairs={{0,4},{1,5},{2,6},{3,7},{4,0},{5,1},{6,2},{7,3},{8,12},{9,13},{10,... | collective-permute-start | bytes 663560 | tf_op jit(solution)/shard_map/ppermute | solution.py:23
  72.8 1.5 %collective-permute-start.26 = (bf16[3,16,2304]{2,1,0:T(8,128)(2,1)S(1)}, bf16[3,16,2304]{2,1,0:T(8,128)(2,1)S(1)}, u32[]{:S(2)}, u32[]{:S(2)}) collective-permute-start(bf16[3,16,2304]{2,1,0:T(8,128)(2,1)S(1)} %collective-permute-done.21.refs_13_), channel_id=1, source_target_pairs={{0,4},{1,5},{2,6},{3,7},{4,0},{5,1},{6,2},{7,3},{8,12},{9,13},{10,... | collective-permute-start | bytes 663560 | tf_op jit(solution)/shard_map/ppermute | solution.py:23

commit v3 on v2

--- a/solution.py
+++ b/solution.py
@@ -37,19 +37,27 @@
     return move(x, lambda t, f: (((t // 4 + dy) % tall) * 4 + ((t // 2 % 2) ^ dx) * 2 + t % 2, f))
 
 
-def gather_rows(weight, relay):
+def gather_rows(weight, relay, asked):
     rows, cols = (lax.axis_size("tile"), lax.axis_size("fsdp"))
     tall = rows // 4
     share = weight.shape[0] // rows
     width = weight.shape[1]
     parts = weight.reshape(rows, share, width)
     mine = lax.dynamic_index_in_dim(parts, lax.axis_index("tile"), 0, keepdims=True)
-    held = {0: mine}
-    for bit in doublings(cols):
-        there = jnp.concatenate([held[h] for h in sorted(held)], axis=0)
-        there = move(there, lambda t, f: (t, f ^ bit))
-        held.update({h ^ bit: there[i : i + 1] for i, h in enumerate(sorted(held))})
-    unit = jnp.concatenate([held[h] for h in range(1, cols)], axis=0)
+    notes = None
+    if asked is not None:
+        mine = jnp.concatenate([mine, asked[None]], axis=2)
+        parts = [shift(mine, 0, k) for k in range(1, cols)]
+        hops = [(-k, 0) for k in range(1, cols)]
+        notes = (parts[0], parts[-1])
+    else:
+        parts, hops = ([mine], [(0, 0)])
+        for bit in doublings(cols):
+            there = parts[0] if len(parts) == 1 else jnp.concatenate(parts, axis=0)
+            parts.append(move(there, lambda t, f: (t, f ^ bit)))
+            hops += [(0, hop ^ bit) for _, hop in hops]
+        parts, hops = (parts[1:], hops[1:])
+    unit = jnp.concatenate(parts, axis=0)
     sent = [(unit, 0, 0)]
     for step in range(1, 2 * tall):
         if not (relay and step == 3):
@@ -61,10 +69,10 @@
         sent.append((across(by_y[:, :, half:], 0, 1), 3, half))
     other = [move(x, lambda t, f: (t ^ 1, f)) for x, _, _ in sent]
     places = [(0, *place[1:]) for place in sent] + [(1, *place[1:]) for place in sent]
-    return [x for x, _, _ in sent] + other, places
-
-
-def place(weight, pieces):
+    return [x for x, _, _ in sent] + other, places, hops, notes
+
+
+def place(weight, pieces, hops):
     rows, cols = (lax.axis_size("tile"), lax.axis_size("fsdp"))
     tall = rows // 4
     share, width = pieces[0].shape[1:]
@@ -75,8 +83,10 @@
     core = (source_t ^ t) & 1
     dx = ((source_t ^ t) >> 1) & 1
     dy = (t // 4 - source_t // 4) % tall
+    order = [hops.index((0, hop)) for hop in range(1, cols)]
     hop = f ^ source_f
-    index = (core * 2 * tall + dy * 2 + dx) * (cols - 1) + hop - 1
+    at = jnp.array([0] + order)[hop]
+    index = (core * 2 * tall + dy * 2 + dx) * (cols - 1) + at
     index = jnp.where(hop == 0, 0, index)
     whole = jnp.take(pieces, index.reshape(-1), axis=0).reshape(cols, rows * share, width)
     whole = lax.dynamic_update_index_in_dim(whole, weight, f, 0)
@@ -121,7 +131,7 @@
     return home * edge + jnp.where(forward, 0, edge - 1), jnp.where(forward, 1, -1)
 
 
-def put_corners(bundle, tiles, edge, links=None):
+def put_corners(bundle, tiles, edge, asked=None):
     def source(n):
         corner = n & 3
         across = jnp.where((corner == 1) | (corner == 2), edge - 1, 0)
@@ -129,57 +139,68 @@
 
     strips = tiles * 4 * edge
     cells = select(one_hot(PAD, strips, source), bundle[:strips, :])
-    if links is not None:
-        row = lax.broadcasted_iota(jnp.int32, cells.shape, 0)
-        lane = lax.broadcasted_iota(jnp.int32, cells.shape, 1)
-        for side in range(tiles * 4):
-            first, step = request_of(links, side // 4, side % 4, tiles, edge)
-            asked = jnp.where(lane < 128, first, step).astype(jnp.float32)
-            cells = jnp.where(row == tiles * 4 + side, asked, cells)
     bundle[strips:, :] = cells.astype(jnp.bfloat16)
-
-
-def answer(out, bundle, near, side, tiles, edge):
+    if asked is not None:
+        moved = select(one_hot(PAD, asked.shape[0], lambda n: n - tiles * 4), asked[...])
+        below = lax.broadcasted_iota(jnp.int32, moved.shape, 0) >= tiles * 4
+        bundle[strips:, :128] = jnp.where(below, moved, cells[:, :128]).astype(jnp.bfloat16)
+
+
+def answer(out, bundle, asked, side, tiles, edge):
     strips = tiles * 4 * edge
-    asked = near[strips : strips + PAD, :256].astype(jnp.float32)
+    asked = asked.astype(jnp.float32)
+    asked = jnp.concatenate([asked] * (strips // 128), axis=1)
+    step = jnp.where(jnp.floor(asked * (1.0 / edge)) * edge == asked, 1.0, -1.0)
     n = lax.broadcasted_iota(jnp.int32, (edge, strips), 0).astype(jnp.float32)
     column = lax.broadcasted_iota(jnp.int32, (edge, strips), 1).astype(jnp.float32)
     for tile in range(tiles):
-        row = tiles * 4 + tile * 4 + side
-        first, step = (
-            jnp.concatenate([asked[row : row + 1, low : low + 128]] * (strips // 128), axis=1)
-            for low in (0, 128)
-        )
-        picker = jnp.where(column == first + step * n, 1.0, 0.0).astype(jnp.bfloat16)
+        row = tile * 4 + side
+        picker = column == asked[row : row + 1] + step[row : row + 1] * n
+        picker = jnp.where(picker, 1.0, 0.0).astype(jnp.bfloat16)
         out[tile * edge : (tile + 1) * edge, :] = select(picker, bundle[:strips, :]).astype(jnp.bfloat16)
 
 
-def borders_kernel(links, field, bundle):
+def replies_kernel(tiles, edge, bundle, from_west, from_east, north, south, to_east, to_west):
+    strips = tiles * 4 * edge
+    for out, note, side in ((to_east, from_east, 3), (to_west, from_west, 1)):
+        answer(out, bundle, note[0, :, note.shape[2] - 128 :], side, tiles, edge)
+        out[tiles * edge : tiles * edge + PAD, :] = north[strips:, :]
+        out[tiles * edge + PAD :, :] = south[strips:, :]
+
+
+def replies(bundle, notes, north, south, tiles, edge):
+    out = jax.ShapeDtypeStruct((tiles * edge + 2 * PAD, bundle.shape[1]), jnp.bfloat16)
+    return pl.pallas_call(
+        functools.partial(replies_kernel, tiles, edge),
+        out_shape=(out, out),
+        compiler_params=pltpu.CompilerParams(vmem_limit_bytes=8 << 20),
+        name="replies",
+    )(bundle, *notes, north, south)
+
+
+def borders_kernel(asked, field, bundle):
     tiles, edge, _, channels = field.shape
     for tile in range(tiles):
         for half in range(2):
             rows = edge // 2
             chunk = field[tile, half * rows : (half + 1) * rows].reshape(rows * edge, channels)
             put_borders(bundle, tile, half, chunk, edge)
-    put_corners(bundle, tiles, edge, links)
-
-
-def borders(field, links):
+    put_corners(bundle, tiles, edge, asked)
+
+
+def borders(field, asked):
     tiles, edge, _, channels = field.shape
     return pl.pallas_call(
         borders_kernel,
         out_shape=jax.ShapeDtypeStruct((tiles * 4 * edge + PAD, channels), jnp.bfloat16),
-        in_specs=[pl.BlockSpec(memory_space=pltpu.SMEM), pl.BlockSpec(memory_space=pltpu.VMEM)],
-        out_specs=pl.BlockSpec(memory_space=pltpu.VMEM),
         compiler_params=pltpu.CompilerParams(vmem_limit_bytes=16 << 20),
         name="borders",
-    )(links, field)
+    )(asked, field)
 
 
 def surround(field, near, side_links, corner_links, chosen, halos, wide):
     tiles, edge, _, channels = field.shape
-    strips = tiles * edge if chosen else tiles * 4 * edge
-    cells_at = strips if chosen else strips + PAD
+    strips = tiles * 4 * edge
     column = lax.broadcasted_iota(jnp.int32, (edge, channels), 0)
 
     def put(tile, row, middle, before, after):
@@ -192,7 +213,7 @@
 
     for tile in range(tiles):
         for side in range(4):
-            if chosen:
+            if chosen[side]:
                 halos[tile, side] = near[side][tile * edge : (tile + 1) * edge, :].astype(jnp.float32)
                 continue
             first, step = request_of(side_links, tile, side, tiles, edge)
@@ -203,6 +224,7 @@
             near_id, near_corner, flag = (corner_links[i, tile, corner] for i in range(3))
             pick = jnp.where(flag == 1, lax.rem(near_id, tiles) * 4 + near_corner, -1)
             picker = one_hot(8, PAD, lambda n: pick)
+            cells_at = tiles * edge if chosen[source] else strips + PAD
             cells.append(select(picker, near[source][cells_at + low : cells_at + low + PAD, :])[:1])
         put(tile, 0, halos[tile, 0], cells[0], cells[1])
         put(tile, edge + 1, halos[tile, 2], cells[3], cells[2])
@@ -216,9 +238,11 @@
                 put(tile, row + 1, field[tile, row], before, after)
 
 
-def fetch_weight(sources, places, whole, place_of):
+def fetch_weight(sources, places, hops, whole, place_of):
     own, *pieces = sources
-    hops, share, _ = pieces[0].shape
+    share = pieces[0].shape[1]
+    cols = len(hops) + 1
+    width = whole.shape[1]
     rows = own.shape[0] // share
     t, f = (place_of[0], place_of[1])
     tall = rows // 4
@@ -228,24 +252,28 @@
         far_y = lax.rem(t // 4 + tall - dy, tall)
         far_x = lax.rem(t // 2 + dx, 2)
         far = far_y * 4 + far_x * 2 + lax.rem(t + core, 2)
-        for hop in range(1, hops + 1):
-            start = pl.multiple_of(((f ^ hop) * rows + far) * share, share)
-            whole[pl.ds(start, share), low : low + piece.shape[2]] = piece[hop - 1]
-
-
-def conv_kernel(places, pooling, *refs):
+        high = min(low + piece.shape[2], width)
+        for i, (back, flip) in enumerate(hops):
+            far_f = lax.rem(f + cols + back, cols) ^ flip
+            start = pl.multiple_of((far_f * rows + far) * share, share)
+            whole[pl.ds(start, share), low:high] = piece[i, :, : high - low]
+
+
+def conv_kernel(places, hops, chosen, pooling, *refs):
     place_of, side_links, corner_links, field, north, east, south, west, bias = refs[:9]
     near = (north, east, south, west)
     count = 1 + len(places)
     sources = refs[9 : 9 + count]
-    outs = refs[9 + count : -5]
+    asking = 2 if chosen[1] and not pooling else 0
+    notes = refs[9 + count : 9 + count + asking]
+    outs = refs[9 + count + asking : -5]
     halos, wide, whole, total, bundle = refs[-5:]
     tiles, edge, _, channels = field.shape
     if count == 1:
         whole = sources[0]
     else:
-        fetch_weight(sources, places, whole, place_of)
-    surround(field, near, side_links, corner_links, pooling, halos, wide)
+        fetch_weight(sources, places, hops, whole, place_of)
+    surround(field, near, side_links, corner_links, chosen, halos, wide)
     rows = edge // 2
     depth = 3 * channels
     for tile in range(tiles):
@@ -280,13 +308,18 @@
     if not pooling:
         put_corners(bundle, tiles, edge)
         for side, out in enumerate(outs[1:]):
-            answer(out, bundle, near[side], (side + 2) % 4, tiles, edge)
+            if notes and side % 2:
+                note = notes[(3 - side) // 2]
+                asked = note[0, :, note.shape[2] - 128 :]
+            else:
+                asked = near[side][tiles * 4 * edge + tiles * 4 : tiles * 4 * edge + PAD, :128]
+            answer(out, bundle, asked, (side + 2) % 4, tiles, edge)
             if side in (0, 2):
                 out[tiles * edge :, :] = bundle[tiles * 4 * edge :, :]
 
 
-def conv(field, near, links, bias, weight, pooling):
-    sources, places = weight
+def conv(field, near, links, bias, weight, chosen, pooling, notes=()):
+    sources, places, hops = weight
     tiles, edge, _, channels = field.shape
     width = bias.shape[0]
     if pooling:
@@ -299,9 +332,9 @@
     smem = pl.BlockSpec(memory_space=pltpu.SMEM)
     flops = 2 * tiles * edge * edge * 9 * channels * width
     return pl.pallas_call(
-        functools.partial(conv_kernel, places, pooling),
+        functools.partial(conv_kernel, places, hops, chosen, pooling),
         out_shape=outs,
-        in_specs=[smem] * 3 + [vmem] * (6 + len(sources)),
+        in_specs=[smem] * 3 + [vmem] * (6 + len(sources) + len(notes)),
         out_specs=[vmem] * len(outs),
         scratch_shapes=[
             pltpu.VMEM((tiles, 4, edge, channels), jnp.float32),
@@ -319,6 +352,7 @@
         *near,
         bias.reshape(1, width),
         *sources,
+        *notes,
     )
 
 
@@ -331,26 +365,49 @@
     return north, east, south, west
 
 
-def sources_of(weight, relay):
-    pieces, places = gather_rows(weight, relay)
+def codes(side_links, share, edge):
+    tiles = side_links.shape[0]
+    near_id, near_side, flag = (side_links[..., i] for i in range(3))
+    turned = (jnp.arange(4) >= 2)[None, :]
+    forward = ~(turned ^ (near_side >= 2) ^ (flag != 1))
+    first = (near_id % tiles * 4 + near_side) * edge + jnp.where(forward, 0, edge - 1)
+    first = jnp.concatenate([first.reshape(-1), jnp.zeros((share - tiles * 4,), first.dtype)])
+    return jnp.broadcast_to(first.astype(jnp.bfloat16)[:, None], (share, 128))
+
+
+def sources_of(weight, relay, asked):
+    pieces, places, hops, notes = gather_rows(weight, relay, asked)
     if pieces[0].shape[1] % 16 == 0:
-        return (weight, *pieces), tuple(places)
-    return (place(weight, pieces),), ()
+        return ((weight, *pieces), tuple(places), tuple(hops)), notes
+    return ((place(weight, pieces, hops),), (), ()), notes
 
 
 def shards(
     tiles_in, first_weight, first_bias, second_weight, second_bias, side_links, corner_links
 ):
+    tiles, edge, _, _ = tiles_in.shape
+    small = lax.axis_size("tile") == 8
     place_of = jnp.stack([lax.axis_index("tile"), lax.axis_index("fsdp")])
+    asked = codes(side_links, PAD, edge)
     side_links = side_links.transpose(2, 0, 1)
     links = (place_of, side_links, corner_links.transpose(2, 0, 1))
-    first = sources_of(first_weight, False)
-    second = sources_of(second_weight, lax.axis_size("tile") == 8)
-    bundle = borders(tiles_in, side_links)
-    near = exchange(bundle, bundle, bundle, bundle)
-    hidden, *strips = conv(tiles_in, near, links, first_bias, first, False)
+    first, notes = sources_of(first_weight, False, asked if small else None)
+    second, _ = sources_of(second_weight, small, None)
+    bundle = borders(tiles_in, asked)
+    if notes:
+        north = shift(bundle, 1, 0)
+        south = shift(bundle, -1, 0)
+        to_east, to_west = replies(bundle, notes, north, south, tiles, edge)
+        near = (north, shift(to_west, 0, -1), south, shift(to_east, 0, 1))
+        chosen = (False, True, False, True)
+    else:
+        near = exchange(bundle, bundle, bundle, bundle)
+        chosen = (False,) * 4
+    hidden, *strips = conv(
+        tiles_in, near, links, first_bias, first, chosen, False, notes or ()
+    )
     near = exchange(*strips)
-    return conv(hidden, near, links, second_bias, second, True)[0]
+    return conv(hidden, near, links, second_bias, second, (True,) * 4, True)[0]
 
 
 def solution(mesh):

time: 88.1 us -> 78.4 us (0.89)
  waiting for transfers between devices: 35 us -> 23.7 us
  starting transfers between devices: 26.4 us -> 27.3 us
    ppermute x28 -> x29, waiting for transfers between devices: 35 us -> 23.7 us  [move(): return lax.ppermute(x, AXES, pairs)]
    ppermute x28 -> x29, starting transfers between devices: 26.4 us -> 27.3 us  [move(): return lax.ppermute(x, AXES, pairs)]
    unnamed x18 -> x19, local copies, waits for them, and re-layouts: 1.95 us -> 1.3 us
    pallas_call x2 -> x3, Pallas kernels: 22.1 us -> 22.2 us  [the longest x2 22 us: conv(): pl.pallas_call(functools.partial(conv_kernel, places, hops, chosen, pooli...]
  transfers between devices with their start and end apart: 28 -> 29, of which waited for: 10 -> 13; matrix products, arithmetic and copies ran while one was open for 1% -> 0% of each run, Pallas kernels for 10% -> 12%
where the time goes in v3:
time: 78.4 us; the launch traced here: 78.1 us
  starting transfers between devices  27.3 us (35%)
  waiting for transfers between devices  23.7 us (30%)
  Pallas kernels  22.6 us (29%)
  local copies, waits for them, and re-layouts  3.46 us (4%)
  other arithmetic  0.84 us (1%)
    ppermute x29, starting transfers between devices, move(): return lax.ppermute(x, AXES, pairs)  27.3 us
    ppermute x29, waiting for transfers between devices, move(): return lax.ppermute(x, AXES, pairs)  23.7 us
    pallas_call x2, Pallas kernels, conv(): pl.pallas_call(functools.partial(conv_kernel, places, hops, chosen, pooli...  22 us
  transfers between devices with their start and end apart: 29, of which 13 were waited for; matrix products, arithmetic and copies ran while one was open for 0% of the time, Pallas kernels for 12%

profile of v3, /device:TPU:0, one launch (start us, length us, event | category | flops | bytes accessed | tf_op | source)
XLA Modules:
  0.0 78.1 jit_solution(5010383459004676144)
XLA Ops:
  0.0 0.7 slice_compare_fusion
  0.7 0.7 fusion.3
  1.4 0.1 ne.19
  1.5 0.1 xor.16
  1.6 0.1 squeeze.7
  1.6 0.1 squeeze.8
  1.8 0.9 %constant_dynamic-slice_fusion.1 = bf16[1,16,2304]{2,1,0:T(8,128)(2,1)S(1)} fusion(bf16[8,16,2304]{2,1,0:T(8,128)(2,1)} %bitcast.15, s32[]{:T(128)S(6)} %select_n.21), kind=kLoop, calls=%fused_computation.23 | loop fusion | bytes 147460 | tf_op jit(solution)/shard_map/jit(dynamic_index_in_dim)/dynamic_slice | solution.py:46
  2.7 0.1 broadcast_in_dim_broadcast_in_dim.2
  2.7 4.1 %collective-permute-start.6 = (bf16[1,16,2432]{2,1,0:T(8,128)(2,1)S(1)}, bf16[1,16,2432]{2,1,0:T(8,128)(2,1)S(1)}, u32[]{:S(2)}, u32[]{:S(2)}) collective-permute-start(bf16[1,16,2432]{2,1,0:T(8,128)(2,1)S(1)} %pad_maximum_fusion.5), channel_id=1, source_target_pairs={{0,2},{1,3},{2,0},{3,1},{4,6},{5,7},{6,4},{7,5},{8,10},{9,11},{10,... | collective-permute-start | bytes 233480 | tf_op jit(solution)/shard_map/ppermute | solution.py:23
  6.9 1.3 %collective-permute-start.2 = (bf16[1,16,2432]{2,1,0:T(8,128)(2,1)S(1)}, bf16[1,16,2432]{2,1,0:T(8,128)(2,1)S(1)}, u32[]{:S(2)}, u32[]{:S(2)}) collective-permute-start(bf16[1,16,2432]{2,1,0:T(8,128)(2,1)S(1)} %pad_maximum_fusion.5), channel_id=1, source_target_pairs={{0,3},{1,0},{2,1},{3,2},{4,7},{5,4},{6,5},{7,6},{8,11},{9,8},{10,9... | collective-permute-start | bytes 233480 | tf_op jit(solution)/shard_map/ppermute | solution.py:23
  8.2 0.7 collective-permute-start.1
  8.9 0.1 broadcast_in_dim.14.asked
  9.0 1.2 %copy-done = bf16[2,32,32,256]{3,2,1,0:T(8,128)(2,1)S(1)} copy-done((bf16[2,32,32,256]{3,2,1,0:T(8,128)(2,1)S(1)}, bf16[2,32,32,256]{3,2,1,0:T(8,128)(2,1)}, u32[]{:S(2)}) %copy-start) | copy-done | bytes 1048600
  10.2 0.4 borders.1.bundle
  10.6 1.1 %collective-permute-start.3 = (bf16[272,256]{1,0:T(8,128)(2,1)S(1)}, bf16[272,256]{1,0:T(8,128)(2,1)S(1)}, u32[]{:S(2)}, u32[]{:S(2)}) collective-permute-start(bf16[272,256]{1,0:T(8,128)(2,1)S(1)} %borders.1.bundle), channel_id=1, source_target_pairs={{0,28},{1,29},{2,30},{3,31},{4,0},{5,1},{6,2},{7,3},{8,4},{9,5},{1... | collective-permute-start | bytes 417800 | tf_op jit(solution)/shard_map/ppermute | solution.py:23
  11.7 0.1 pad_add_fusion.refs_0_
  11.8 2.6 %collective-permute-done.1.from_west.refs_18_ = bf16[1,16,2432]{2,1,0:T(8,128)(2,1)S(1)} collective-permute-done((bf16[1,16,2432]{2,1,0:T(8,128)(2,1)S(1)}, bf16[1,16,2432]{2,1,0:T(8,128)(2,1)S(1)}, u32[]{:S(2)}, u32[]{:S(2)}) %collective-permute-start.1) | collective-permute-done | bytes 77856 | tf_op jit(solution)/shard_map/ppermute | solution.py:23
  14.4 2.5 %collective-permute-start.18 = (bf16[1,16,4608]{2,1,0:T(8,128)(2,1)S(1)}, bf16[1,16,4608]{2,1,0:T(8,128)(2,1)S(1)}, u32[]{:S(2)}, u32[]{:S(2)}) collective-permute-start(bf16[1,16,4608]{2,1,0:T(8,128)(2,1)S(1)} %constant_dynamic-slice_fusion), channel_id=1, source_target_pairs={{0,2},{1,3},{2,0},{3,1},{4,6},{5,7},{6,4},{7,5},{8,10},{9,11},{10,... | collective-permute-start | bytes 442376 | tf_op jit(solution)/shard_map/ppermute | solution.py:23
  16.9 0.0 copy-start.3
  16.9 0.0 copy-start.4
  16.9 0.0 copy-start.5
  16.9 0.0 copy-start.6
  16.9 0.0 collective-permute-done.6
  17.0 2.5 %collective-permute-start.9 = (bf16[3,16,2432]{2,1,0:T(8,128)(2,1)S(1)}, bf16[3,16,2432]{2,1,0:T(8,128)(2,1)S(1)}, u32[]{:S(2)}, u32[]{:S(2)}) collective-permute-start(bf16[3,16,2432]{2,1,0:T(8,128)(2,1)S(1)} %constant_dynamic-update-slice_fusion.refs_10_), channel_id=1, source_target_pairs={{0,24},{1,25},{2,26},{3,27},{4,28},{5,29},{6,30},{7,31},{8,16},{9,... | collective-permute-start | bytes 700424 | tf_op jit(solution)/shard_map/ppermute | solution.py:23
  19.5 0.5 collective-permute-start.8
  20.0 0.5 collective-permute-start.7
  20.5 0.2 replies.1
  20.7 0.5 collective-permute-start.4
  21.2 3.0 %collective-permute-done.18 = bf16[1,16,4608]{2,1,0:T(8,128)(2,1)S(1)} collective-permute-done((bf16[1,16,4608]{2,1,0:T(8,128)(2,1)S(1)}, bf16[1,16,4608]{2,1,0:T(8,128)(2,1)S(1)}, u32[]{:S(2)}, u32[]{:S(2)}) %collective-permute-start.18) | collective-permute-done | bytes 147488 | tf_op jit(solution)/shard_map/ppermute | solution.py:23
  24.2 0.1 collective-permute-start.19
  24.3 0.7 collective-permute-done.4.refs_5_
  25.0 1.6 %collective-permute-done.9.refs_13_ = bf16[3,16,2432]{2,1,0:T(8,128)(2,1)S(1)} collective-permute-done((bf16[3,16,2432]{2,1,0:T(8,128)(2,1)S(1)}, bf16[3,16,2432]{2,1,0:T(8,128)(2,1)S(1)}, u32[]{:S(2)}, u32[]{:S(2)}) %collective-permute-start.9) | collective-permute-done | bytes 233504 | tf_op jit(solution)/shard_map/ppermute | solution.py:23
  26.5 0.1 collective-permute-start.5
  26.7 3.5 %collective-permute-done.8.refs_12_ = bf16[3,16,2432]{2,1,0:T(8,128)(2,1)S(1)} collective-permute-done((bf16[3,16,2432]{2,1,0:T(8,128)(2,1)S(1)}, bf16[3,16,2432]{2,1,0:T(8,128)(2,1)S(1)}, u32[]{:S(2)}, u32[]{:S(2)}) %collective-permute-start.8) | collective-permute-done | bytes 233504 | tf_op jit(solution)/shard_map/ppermute | solution.py:23
  30.1 0.0 collective-permute-start.13
  30.1 0.1 collective-permute-done.7.refs_11_
  30.2 0.4 collective-permute-start.12
  30.6 3.2 %collective-permute-done.19 = bf16[2,16,4608]{2,1,0:T(8,128)(2,1)S(1)} collective-permute-done((bf16[2,16,4608]{2,1,0:T(8,128)(2,1)S(1)}, bf16[2,16,4608]{2,1,0:T(8,128)(2,1)S(1)}, u32[]{:S(2)}, u32[]{:S(2)}) %collective-permute-start.19) | collective-permute-done | bytes 294944 | tf_op jit(solution)/shard_map/ppermute | solution.py:23
  33.8 0.0 collective-permute-start.11
  33.9 1.6 %collective-permute-start.21 = (bf16[3,16,4608]{2,1,0:T(8,128)(2,1)S(1)}, bf16[3,16,4608]{2,1,0:T(8,128)(2,1)S(1)}, u32[]{:S(2)}, u32[]{:S(2)}) collective-permute-start(bf16[3,16,4608]{2,1,0:T(8,128)(2,1)S(1)} %constant_dynamic-update-slice_fusion.3.refs_10_), channel_id=1, source_target_pairs={{0,16},{1,17},{2,18},{3,19},{4,20},{5,21},{6,22},{7,23},{8,24},{9,... | collective-permute-start | bytes 1327112 | tf_op jit(solution)/shard_map/ppermute | solution.py:23
  35.4 0.0 collective-permute-done.10.refs_14_
  35.5 1.5 %collective-permute-start.20 = (bf16[3,16,4608]{2,1,0:T(8,128)(2,1)S(1)}, bf16[3,16,4608]{2,1,0:T(8,128)(2,1)S(1)}, u32[]{:S(2)}, u32[]{:S(2)}) collective-permute-start(bf16[3,16,4608]{2,1,0:T(8,128)(2,1)S(1)} %constant_dynamic-update-slice_fusion.3.refs_10_), channel_id=1, source_target_pairs={{0,8},{1,9},{2,10},{3,11},{4,12},{5,13},{6,14},{7,15},{8,0},{9,1},... | collective-permute-start | bytes 1327112 | tf_op jit(solution)/shard_map/ppermute | solution.py:23
  36.9 0.0 collective-permute-done.13.refs_17_
  36.9 0.0 collective-permute-done.12.refs_16_
  36.9 0.0 collective-permute-done.11.refs_15_
  37.0 8.5 %first.1 = (bf16[2,32,32,512]{3,2,1,0:T(8,128)(2,1)S(1)}, bf16[80,512]{1,0:T(8,128)(2,1)S(1)}, bf16[64,512]{1,0:T(8,128)(2,1)S(1)}, bf16[80,512]{1,0:T(8,128)(2,1)S(1)}, bf16[64,512]{1,0:T(8,128)(2,1)S(1)}) custom-call(s32[2]{0:T(128)S(1)} %pad_add_fusion.refs_0_, s32[3,2,4]{2,1,0:T(2,128)S(1)} %bitcast.16, s32[3,2,4]{2,1,0:T(2,128)S(1)} %bitcast.18, ...), custom_call_target="tpu_custom_call" | custom-call | flops 4831838208 | bytes 8388608 | tf_op jit(solution)/shard_map/first/pallas_call | solution.py:334
  45.5 0.0 copy-start.7
  45.5 0.1 collective-permute-start.14
  45.5 2.6 %collective-permute-start.15 = (bf16[80,512]{1,0:T(8,128)(2,1)S(1)}, bf16[80,512]{1,0:T(8,128)(2,1)S(1)}, u32[]{:S(2)}, u32[]{:S(2)}) collective-permute-start(bf16[80,512]{1,0:T(8,128)(2,1)S(1)} %get-tuple-element.17), channel_id=1, source_target_pairs={{0,28},{1,29},{2,30},{3,31},{4,0},{5,1},{6,2},{7,3},{8,4},{9,5},{1... | collective-permute-start | bytes 245768 | tf_op jit(solution)/shard_map/ppermute | solution.py:23
  48.2 2.8 %collective-permute-done.14.refs_4_ = bf16[80,512]{1,0:T(8,128)(2,1)S(1)} collective-permute-done((bf16[80,512]{1,0:T(8,128)(2,1)S(1)}, bf16[80,512]{1,0:T(8,128)(2,1)S(1)}, u32[]{:S(2)}, u32[]{:S(2)}) %collective-permute-start.14) | collective-permute-done | bytes 81952 | tf_op jit(solution)/shard_map/ppermute | solution.py:23
  51.0 0.0 collective-permute-done.15.refs_6_
  51.0 0.3 collective-permute-start.17
  51.3 3.6 %collective-permute-start.16 = (bf16[96,512]{1,0:T(8,128)(2,1)S(1)}, bf16[96,512]{1,0:T(8,128)(2,1)S(1)}, u32[]{:S(2)}, u32[]{:S(2)}) collective-permute-start(bf16[96,512]{1,0:T(8,128)(2,1)S(1)} %get-tuple-element.20), channel_id=1, source_target_pairs={{0,3},{1,0},{2,1},{3,2},{4,7},{5,4},{6,5},{7,6},{8,11},{9,8},{10,9... | collective-permute-start | bytes 294920 | tf_op jit(solution)/shard_map/ppermute | solution.py:23
  54.9 0.9 %collective-permute-start.23 = (bf16[3,16,2304]{2,1,0:T(8,128)(2,1)S(1)}, bf16[3,16,2304]{2,1,0:T(8,128)(2,1)S(1)}, u32[]{:S(2)}, u32[]{:S(2)}) collective-permute-start(bf16[3,16,2304]{2,1,0:T(8,128)(2,1)S(1)} %slice.31), channel_id=1, source_target_pairs={{0,8},{1,9},{2,10},{3,11},{4,12},{5,13},{6,14},{7,15},{8,0},{9,1},... | collective-permute-start | bytes 663560 | tf_op jit(solution)/shard_map/ppermute | solution.py:23
  55.8 1.6 %collective-permute-start.22 = (bf16[3,16,2304]{2,1,0:T(8,128)(2,1)S(1)}, bf16[3,16,2304]{2,1,0:T(8,128)(2,1)S(1)}, u32[]{:S(2)}, u32[]{:S(2)}) collective-permute-start(bf16[3,16,2304]{2,1,0:T(8,128)(2,1)S(1)} %slice.30), channel_id=1, source_target_pairs={{0,16},{1,17},{2,18},{3,19},{4,20},{5,21},{6,22},{7,23},{8,24},{9,... | collective-permute-start | bytes 663560 | tf_op jit(solution)/shard_map/ppermute | solution.py:23
  57.4 0.6 collective-permute-done.17.refs_7_
  58.0 0.0 collective-permute-done.16.refs_5_
  58.0 0.5 collective-permute-start.25
  58.5 4.3 %collective-permute-done.23.refs_14_ = bf16[3,16,2304]{2,1,0:T(8,128)(2,1)S(1)} collective-permute-done((bf16[3,16,2304]{2,1,0:T(8,128)(2,1)S(1)}, bf16[3,16,2304]{2,1,0:T(8,128)(2,1)S(1)}, u32[]{:S(2)}, u32[]{:S(2)}) %collective-permute-start.23) | collective-permute-done | bytes 221216 | tf_op jit(solution)/shard_map/ppermute | solution.py:23
  62.8 0.1 collective-permute-done.22.refs_13_
  63.0 0.4 collective-permute-start.27
  63.3 1.0 %collective-permute-done.28.refs_19_ = bf16[3,16,2304]{2,1,0:T(8,128)(2,1)S(1)} collective-permute-done((bf16[3,16,2304]{2,1,0:T(8,128)(2,1)S(1)}, bf16[3,16,2304]{2,1,0:T(8,128)(2,1)S(1)}, u32[]{:S(2)}, u32[]{:S(2)}) %collective-permute-start.28) | collective-permute-done | bytes 221216 | tf_op jit(solution)/shard_map/ppermute | solution.py:23
  64.3 0.3 collective-permute-done.27.refs_18_
  64.6 13.5 %second.1 = bf16[2,16,16,512]{3,2,1,0:T(8,128)(2,1)} custom-call(s32[2]{0:T(128)S(1)} %pad_add_fusion.refs_0_, s32[3,2,4]{2,1,0:T(2,128)S(1)} %bitcast.17, s32[3,2,4]{2,1,0:T(2,128)S(1)} %bitcast.19, bf16[2,32,32,512]{3,2,1,0:T(8,128)(2,1)S(1)} %get-tuple-element.14.refs_3_, bf16[80,512]{1,0:T(8,128)(2,1)S(1)} %collective-permute-done.14.refs_4_, ...), custom_call_target="tpu_custom_call" | custom-call | flops 9663676416 | bytes 8388608 | tf_op jit(solution)/shard_map/second/pallas_call | solution.py:334
  (41 shorter events, 0.3 us)
Async XLA Ops:
  2.7 14.2 %collective-permute-start.6 = (bf16[1,16,2432]{2,1,0:T(8,128)(2,1)S(1)}, bf16[1,16,2432]{2,1,0:T(8,128)(2,1)S(1)}, u32[]{:S(2)}, u32[]{:S(2)}) collective-permute-start(bf16[1,16,2432]{2,1,0:T(8,128)(2,1)S(1)} %pad_maximum_fusion.5), channel_id=1, source_target_pairs={{0,2},{1,3},{2,0},{3,1},{4,6},{5,7},{6,4},{7,5},{8,10},{9,11},{10,... | collective-permute-start | bytes 233480 | tf_op jit(solution)/shard_map/ppermute | solution.py:23
  6.9 10.1 %collective-permute-start.2 = (bf16[1,16,2432]{2,1,0:T(8,128)(2,1)S(1)}, bf16[1,16,2432]{2,1,0:T(8,128)(2,1)S(1)}, u32[]{:S(2)}, u32[]{:S(2)}) collective-permute-start(bf16[1,16,2432]{2,1,0:T(8,128)(2,1)S(1)} %pad_maximum_fusion.5), channel_id=1, source_target_pairs={{0,3},{1,0},{2,1},{3,2},{4,7},{5,4},{6,5},{7,6},{8,11},{9,8},{10,9... | collective-permute-start | bytes 233480 | tf_op jit(solution)/shard_map/ppermute | solution.py:23
  8.2 6.2 %collective-permute-start.1 = (bf16[1,16,2432]{2,1,0:T(8,128)(2,1)S(1)}, bf16[1,16,2432]{2,1,0:T(8,128)(2,1)S(1)}, u32[]{:S(2)}, u32[]{:S(2)}) collective-permute-start(bf16[1,16,2432]{2,1,0:T(8,128)(2,1)S(1)} %pad_maximum_fusion.5), channel_id=1, source_target_pairs={{0,1},{1,2},{2,3},{3,0},{4,5},{5,6},{6,7},{7,4},{8,9},{9,10},{10,1... | collective-permute-start | bytes 233480 | tf_op jit(solution)/shard_map/ppermute | solution.py:23
  9.0 1.2 %copy-start = (bf16[2,32,32,256]{3,2,1,0:T(8,128)(2,1)S(1)}, bf16[2,32,32,256]{3,2,1,0:T(8,128)(2,1)}, u32[]{:S(2)}) copy-start(bf16[2,32,32,256]{3,2,1,0:T(8,128)(2,1)} %refs_3_.1) | copy-start | bytes 3145732
  10.2 1.5 %copy-start.2 = (bf16[128,4608]{1,0:T(8,128)(2,1)S(1)}, bf16[128,4608]{1,0:T(8,128)(2,1)}, u32[]{:S(2)}) copy-start(bf16[128,4608]{1,0:T(8,128)(2,1)} %refs_9_.3) | copy-start | bytes 3538948
  10.6 9.4 %collective-permute-start.3 = (bf16[272,256]{1,0:T(8,128)(2,1)S(1)}, bf16[272,256]{1,0:T(8,128)(2,1)S(1)}, u32[]{:S(2)}, u32[]{:S(2)}) collective-permute-start(bf16[272,256]{1,0:T(8,128)(2,1)S(1)} %borders.1.bundle), channel_id=1, source_target_pairs={{0,28},{1,29},{2,30},{3,31},{4,0},{5,1},{6,2},{7,3},{8,4},{9,5},{1... | collective-permute-start | bytes 417800 | tf_op jit(solution)/shard_map/ppermute | solution.py:23
  11.7 8.9 %collective-permute-start = (bf16[272,256]{1,0:T(8,128)(2,1)S(1)}, bf16[272,256]{1,0:T(8,128)(2,1)S(1)}, u32[]{:S(2)}, u32[]{:S(2)}) collective-permute-start(bf16[272,256]{1,0:T(8,128)(2,1)S(1)} %borders.1.bundle), channel_id=1, source_target_pairs={{0,4},{1,5},{2,6},{3,7},{4,8},{5,9},{6,10},{7,11},{8,12},{9,13},{1... | collective-permute-start | bytes 417800 | tf_op jit(solution)/shard_map/ppermute | solution.py:23
  14.4 9.8 %collective-permute-start.18 = (bf16[1,16,4608]{2,1,0:T(8,128)(2,1)S(1)}, bf16[1,16,4608]{2,1,0:T(8,128)(2,1)S(1)}, u32[]{:S(2)}, u32[]{:S(2)}) collective-permute-start(bf16[1,16,4608]{2,1,0:T(8,128)(2,1)S(1)} %constant_dynamic-slice_fusion), channel_id=1, source_target_pairs={{0,2},{1,3},{2,0},{3,1},{4,6},{5,7},{6,4},{7,5},{8,10},{9,11},{10,... | collective-permute-start | bytes 442376 | tf_op jit(solution)/shard_map/ppermute | solution.py:23
  16.9 20.1 %copy-start.1 = (bf16[2,32,32,256]{3,2,1,0:T(8,128)(2,1)S(1)}, bf16[2,32,32,256]{3,2,1,0:T(8,128)(2,1)}, u32[]{:S(2)}) copy-start(bf16[2,32,32,256]{3,2,1,0:T(8,128)(2,1)} %refs_3_.1) | copy-start | bytes 3145732
  16.9 20.1 %copy-start.3 = (bf16[128,2304]{1,0:T(8,128)(2,1)S(1)}, bf16[128,2304]{1,0:T(8,128)(2,1)}, u32[]{:S(2)}) copy-start(bf16[128,2304]{1,0:T(8,128)(2,1)} %refs_9_.2) | copy-start | bytes 1769476
  16.9 20.1 %copy-start.4 = (s32[2,4,3]{1,0,2:T(2,128)S(1)}, s32[2,4,3]{1,0,2:T(2,128)}, u32[]{:S(2)}) copy-start(s32[2,4,3]{1,0,2:T(2,128)} %param.12) | copy-start | bytes 292
  16.9 20.1 %copy-start.5 = (s32[2,4,3]{1,0,2:T(2,128)S(1)}, s32[2,4,3]{1,0,2:T(2,128)}, u32[]{:S(2)}) copy-start(s32[2,4,3]{1,0,2:T(2,128)} %param.13) | copy-start | bytes 292
  16.9 20.1 %copy-start.6 = (f32[512]{0:T(512)S(1)}, f32[512]{0:T(512)}, u32[]{:S(2)}) copy-start(f32[512]{0:T(512)} %param.9) | copy-start | bytes 6148
  17.0 9.6 %collective-permute-start.9 = (bf16[3,16,2432]{2,1,0:T(8,128)(2,1)S(1)}, bf16[3,16,2432]{2,1,0:T(8,128)(2,1)S(1)}, u32[]{:S(2)}, u32[]{:S(2)}) collective-permute-start(bf16[3,16,2432]{2,1,0:T(8,128)(2,1)S(1)} %constant_dynamic-update-slice_fusion.refs_10_), channel_id=1, source_target_pairs={{0,24},{1,25},{2,26},{3,27},{4,28},{5,29},{6,30},{7,31},{8,16},{9,... | collective-permute-start | bytes 700424 | tf_op jit(solution)/shard_map/ppermute | solution.py:23
  19.5 10.6 %collective-permute-start.8 = (bf16[3,16,2432]{2,1,0:T(8,128)(2,1)S(1)}, bf16[3,16,2432]{2,1,0:T(8,128)(2,1)S(1)}, u32[]{:S(2)}, u32[]{:S(2)}) collective-permute-start(bf16[3,16,2432]{2,1,0:T(8,128)(2,1)S(1)} %constant_dynamic-update-slice_fusion.refs_10_), channel_id=1, source_target_pairs={{0,16},{1,17},{2,18},{3,19},{4,20},{5,21},{6,22},{7,23},{8,24},{9,... | collective-permute-start | bytes 700424 | tf_op jit(solution)/shard_map/ppermute | solution.py:23
  20.0 10.2 %collective-permute-start.7 = (bf16[3,16,2432]{2,1,0:T(8,128)(2,1)S(1)}, bf16[3,16,2432]{2,1,0:T(8,128)(2,1)S(1)}, u32[]{:S(2)}, u32[]{:S(2)}) collective-permute-start(bf16[3,16,2432]{2,1,0:T(8,128)(2,1)S(1)} %constant_dynamic-update-slice_fusion.refs_10_), channel_id=1, source_target_pairs={{0,8},{1,9},{2,10},{3,11},{4,12},{5,13},{6,14},{7,15},{8,0},{9,1},... | collective-permute-start | bytes 700424 | tf_op jit(solution)/shard_map/ppermute | solution.py:23
  20.7 4.2 %collective-permute-start.4 = (bf16[96,256]{1,0:T(8,128)(2,1)S(1)}, bf16[96,256]{1,0:T(8,128)(2,1)S(1)}, u32[]{:S(2)}, u32[]{:S(2)}) collective-permute-start(bf16[96,256]{1,0:T(8,128)(2,1)S(1)} %get-tuple-element.12), channel_id=1, source_target_pairs={{0,3},{1,0},{2,1},{3,2},{4,7},{5,4},{6,5},{7,6},{8,11},{9,8},{10,9... | collective-permute-start | bytes 147464 | tf_op jit(solution)/shard_map/ppermute | solution.py:23
  24.2 9.6 %collective-permute-start.19 = (bf16[2,16,4608]{2,1,0:T(8,128)(2,1)S(1)}, bf16[2,16,4608]{2,1,0:T(8,128)(2,1)S(1)}, u32[]{:S(2)}, u32[]{:S(2)}) collective-permute-start(bf16[2,16,4608]{2,1,0:T(8,128)(2,1)S(1)} %pad_maximum_fusion), channel_id=1, source_target_pairs={{0,1},{1,0},{2,3},{3,2},{4,5},{5,4},{6,7},{7,6},{8,9},{9,8},{10,11... | collective-permute-start | bytes 884744 | tf_op jit(solution)/shard_map/ppermute | solution.py:23
  25.0 10.5 %collective-permute-start.10 = (bf16[3,16,2432]{2,1,0:T(8,128)(2,1)S(1)}, bf16[3,16,2432]{2,1,0:T(8,128)(2,1)S(1)}, u32[]{:S(2)}, u32[]{:S(2)}) collective-permute-start(bf16[3,16,2432]{2,1,0:T(8,128)(2,1)S(1)} %constant_dynamic-update-slice_fusion.refs_10_), channel_id=1, source_target_pairs={{0,4},{1,5},{2,6},{3,7},{4,0},{5,1},{6,2},{7,3},{8,12},{9,13},{10,... | collective-permute-start | bytes 700424 | tf_op jit(solution)/shard_map/ppermute | solution.py:23
  26.5 7.3 %collective-permute-start.5 = (bf16[96,256]{1,0:T(8,128)(2,1)S(1)}, bf16[96,256]{1,0:T(8,128)(2,1)S(1)}, u32[]{:S(2)}, u32[]{:S(2)}) collective-permute-start(bf16[96,256]{1,0:T(8,128)(2,1)S(1)} %get-tuple-element.13), channel_id=1, source_target_pairs={{0,1},{1,2},{2,3},{3,0},{4,5},{5,6},{6,7},{7,4},{8,9},{9,10},{10,1... | collective-permute-start | bytes 147464 | tf_op jit(solution)/shard_map/ppermute | solution.py:23
  30.1 6.8 %collective-permute-start.13 = (bf16[3,16,2432]{2,1,0:T(8,128)(2,1)S(1)}, bf16[3,16,2432]{2,1,0:T(8,128)(2,1)S(1)}, u32[]{:S(2)}, u32[]{:S(2)}) collective-permute-start(bf16[3,16,2432]{2,1,0:T(8,128)(2,1)S(1)} %collective-permute-done.9.refs_13_), channel_id=1, source_target_pairs={{0,4},{1,5},{2,6},{3,7},{4,0},{5,1},{6,2},{7,3},{8,12},{9,13},{10,... | collective-permute-start | bytes 700424 | tf_op jit(solution)/shard_map/ppermute | solution.py:23
  30.2 6.7 %collective-permute-start.12 = (bf16[3,16,2432]{2,1,0:T(8,128)(2,1)S(1)}, bf16[3,16,2432]{2,1,0:T(8,128)(2,1)S(1)}, u32[]{:S(2)}, u32[]{:S(2)}) collective-permute-start(bf16[3,16,2432]{2,1,0:T(8,128)(2,1)S(1)} %collective-permute-done.8.refs_12_), channel_id=1, source_target_pairs={{0,4},{1,5},{2,6},{3,7},{4,0},{5,1},{6,2},{7,3},{8,12},{9,13},{10,... | collective-permute-start | bytes 700424 | tf_op jit(solution)/shard_map/ppermute | solution.py:23
  33.8 3.1 %collective-permute-start.11 = (bf16[3,16,2432]{2,1,0:T(8,128)(2,1)S(1)}, bf16[3,16,2432]{2,1,0:T(8,128)(2,1)S(1)}, u32[]{:S(2)}, u32[]{:S(2)}) collective-permute-start(bf16[3,16,2432]{2,1,0:T(8,128)(2,1)S(1)} %collective-permute-done.7.refs_11_), channel_id=1, source_target_pairs={{0,4},{1,5},{2,6},{3,7},{4,0},{5,1},{6,2},{7,3},{8,12},{9,13},{10,... | collective-permute-start | bytes 700424 | tf_op jit(solution)/shard_map/ppermute | solution.py:23
  33.9 21.0 %collective-permute-start.21 = (bf16[3,16,4608]{2,1,0:T(8,128)(2,1)S(1)}, bf16[3,16,4608]{2,1,0:T(8,128)(2,1)S(1)}, u32[]{:S(2)}, u32[]{:S(2)}) collective-permute-start(bf16[3,16,4608]{2,1,0:T(8,128)(2,1)S(1)} %constant_dynamic-update-slice_fusion.3.refs_10_), channel_id=1, source_target_pairs={{0,16},{1,17},{2,18},{3,19},{4,20},{5,21},{6,22},{7,23},{8,24},{9,... | collective-permute-start | bytes 1327112 | tf_op jit(solution)/shard_map/ppermute | solution.py:23
  35.5 20.4 %collective-permute-start.20 = (bf16[3,16,4608]{2,1,0:T(8,128)(2,1)S(1)}, bf16[3,16,4608]{2,1,0:T(8,128)(2,1)S(1)}, u32[]{:S(2)}, u32[]{:S(2)}) collective-permute-start(bf16[3,16,4608]{2,1,0:T(8,128)(2,1)S(1)} %constant_dynamic-update-slice_fusion.3.refs_10_), channel_id=1, source_target_pairs={{0,8},{1,9},{2,10},{3,11},{4,12},{5,13},{6,14},{7,15},{8,0},{9,1},... | collective-permute-start | bytes 1327112 | tf_op jit(solution)/shard_map/ppermute | solution.py:23
  45.5 19.1 %copy-start.7 = (f32[512]{0:T(512)S(1)}, f32[512]{0:T(512)}, u32[]{:S(2)}) copy-start(f32[512]{0:T(512)} %param.11) | copy-start | bytes 6148
  45.5 5.5 %collective-permute-start.14 = (bf16[80,512]{1,0:T(8,128)(2,1)S(1)}, bf16[80,512]{1,0:T(8,128)(2,1)S(1)}, u32[]{:S(2)}, u32[]{:S(2)}) collective-permute-start(bf16[80,512]{1,0:T(8,128)(2,1)S(1)} %get-tuple-element.15), channel_id=1, source_target_pairs={{0,4},{1,5},{2,6},{3,7},{4,8},{5,9},{6,10},{7,11},{8,12},{9,13},{1... | collective-permute-start | bytes 245768 | tf_op jit(solution)/shard_map/ppermute | solution.py:23
  45.5 5.4 %collective-permute-start.15 = (bf16[80,512]{1,0:T(8,128)(2,1)S(1)}, bf16[80,512]{1,0:T(8,128)(2,1)S(1)}, u32[]{:S(2)}, u32[]{:S(2)}) collective-permute-start(bf16[80,512]{1,0:T(8,128)(2,1)S(1)} %get-tuple-element.17), channel_id=1, source_target_pairs={{0,28},{1,29},{2,30},{3,31},{4,0},{5,1},{6,2},{7,3},{8,4},{9,5},{1... | collective-permute-start | bytes 245768 | tf_op jit(solution)/shard_map/ppermute | solution.py:23
  51.0 7.0 %collective-permute-start.17 = (bf16[96,512]{1,0:T(8,128)(2,1)S(1)}, bf16[96,512]{1,0:T(8,128)(2,1)S(1)}, u32[]{:S(2)}, u32[]{:S(2)}) collective-permute-start(bf16[96,512]{1,0:T(8,128)(2,1)S(1)} %get-tuple-element.19), channel_id=1, source_target_pairs={{0,1},{1,2},{2,3},{3,0},{4,5},{5,6},{6,7},{7,4},{8,9},{9,10},{10,1... | collective-permute-start | bytes 294920 | tf_op jit(solution)/shard_map/ppermute | solution.py:23
  51.3 6.7 %collective-permute-start.16 = (bf16[96,512]{1,0:T(8,128)(2,1)S(1)}, bf16[96,512]{1,0:T(8,128)(2,1)S(1)}, u32[]{:S(2)}, u32[]{:S(2)}) collective-permute-start(bf16[96,512]{1,0:T(8,128)(2,1)S(1)} %get-tuple-element.20), channel_id=1, source_target_pairs={{0,3},{1,0},{2,1},{3,2},{4,7},{5,4},{6,5},{7,6},{8,11},{9,8},{10,9... | collective-permute-start | bytes 294920 | tf_op jit(solution)/shard_map/ppermute | solution.py:23
  54.9 8.4 %collective-permute-start.24 = (bf16[3,16,4608]{2,1,0:T(8,128)(2,1)S(1)}, bf16[3,16,4608]{2,1,0:T(8,128)(2,1)S(1)}, u32[]{:S(2)}, u32[]{:S(2)}) collective-permute-start(bf16[3,16,4608]{2,1,0:T(8,128)(2,1)S(1)} %constant_dynamic-update-slice_fusion.3.refs_10_), channel_id=1, source_target_pairs={{0,4},{1,5},{2,6},{3,7},{4,0},{5,1},{6,2},{7,3},{8,12},{9,13},{10,... | collective-permute-start | bytes 1327112 | tf_op jit(solution)/shard_map/ppermute | solution.py:23
  54.9 7.9 %collective-permute-start.23 = (bf16[3,16,2304]{2,1,0:T(8,128)(2,1)S(1)}, bf16[3,16,2304]{2,1,0:T(8,128)(2,1)S(1)}, u32[]{:S(2)}, u32[]{:S(2)}) collective-permute-start(bf16[3,16,2304]{2,1,0:T(8,128)(2,1)S(1)} %slice.31), channel_id=1, source_target_pairs={{0,8},{1,9},{2,10},{3,11},{4,12},{5,13},{6,14},{7,15},{8,0},{9,1},... | collective-permute-start | bytes 663560 | tf_op jit(solution)/shard_map/ppermute | solution.py:23
  55.8 7.1 %collective-permute-start.22 = (bf16[3,16,2304]{2,1,0:T(8,128)(2,1)S(1)}, bf16[3,16,2304]{2,1,0:T(8,128)(2,1)S(1)}, u32[]{:S(2)}, u32[]{:S(2)}) collective-permute-start(bf16[3,16,2304]{2,1,0:T(8,128)(2,1)S(1)} %slice.30), channel_id=1, source_target_pairs={{0,16},{1,17},{2,18},{3,19},{4,20},{5,21},{6,22},{7,23},{8,24},{9,... | collective-permute-start | bytes 663560 | tf_op jit(solution)/shard_map/ppermute | solution.py:23
  58.0 6.3 %collective-permute-start.26 = (bf16[3,16,4608]{2,1,0:T(8,128)(2,1)S(1)}, bf16[3,16,4608]{2,1,0:T(8,128)(2,1)S(1)}, u32[]{:S(2)}, u32[]{:S(2)}) collective-permute-start(bf16[3,16,4608]{2,1,0:T(8,128)(2,1)S(1)} %collective-permute-done.21.refs_12_), channel_id=1, source_target_pairs={{0,4},{1,5},{2,6},{3,7},{4,0},{5,1},{6,2},{7,3},{8,12},{9,13},{10,... | collective-permute-start | bytes 1327112 | tf_op jit(solution)/shard_map/ppermute | solution.py:23
  58.0 6.6 %collective-permute-start.25 = (bf16[3,16,4608]{2,1,0:T(8,128)(2,1)S(1)}, bf16[3,16,4608]{2,1,0:T(8,128)(2,1)S(1)}, u32[]{:S(2)}, u32[]{:S(2)}) collective-permute-start(bf16[3,16,4608]{2,1,0:T(8,128)(2,1)S(1)} %collective-permute-done.20.refs_11_), channel_id=1, source_target_pairs={{0,4},{1,5},{2,6},{3,7},{4,0},{5,1},{6,2},{7,3},{8,12},{9,13},{10,... | collective-permute-start | bytes 1327112 | tf_op jit(solution)/shard_map/ppermute | solution.py:23
  62.8 1.5 %collective-permute-start.28 = (bf16[3,16,2304]{2,1,0:T(8,128)(2,1)S(1)}, bf16[3,16,2304]{2,1,0:T(8,128)(2,1)S(1)}, u32[]{:S(2)}, u32[]{:S(2)}) collective-permute-start(bf16[3,16,2304]{2,1,0:T(8,128)(2,1)S(1)} %collective-permute-done.23.refs_14_), channel_id=1, source_target_pairs={{0,4},{1,5},{2,6},{3,7},{4,0},{5,1},{6,2},{7,3},{8,12},{9,13},{10,... | collective-permute-start | bytes 663560 | tf_op jit(solution)/shard_map/ppermute | solution.py:23
  63.0 1.7 %collective-permute-start.27 = (bf16[3,16,2304]{2,1,0:T(8,128)(2,1)S(1)}, bf16[3,16,2304]{2,1,0:T(8,128)(2,1)S(1)}, u32[]{:S(2)}, u32[]{:S(2)}) collective-permute-start(bf16[3,16,2304]{2,1,0:T(8,128)(2,1)S(1)} %collective-permute-done.22.refs_13_), channel_id=1, source_target_pairs={{0,4},{1,5},{2,6},{3,7},{4,0},{5,1},{6,2},{7,3},{8,12},{9,13},{10,... | collective-permute-start | bytes 663560 | tf_op jit(solution)/shard_map/ppermute | solution.py:23

commit v4 on v3

--- a/solution.py
+++ b/solution.py
@@ -50,6 +50,11 @@
         parts = [shift(mine, 0, k) for k in range(1, cols)]
         hops = [(-k, 0) for k in range(1, cols)]
         notes = (parts[0], parts[-1])
+    elif relay and cols == 4:
+        far = move(mine, lambda t, f: (t, f ^ 2))
+        by = move(mine, lambda t, f: (t, f ^ 1))
+        parts = [far, by, move(far, lambda t, f: (t, f ^ 1))]
+        hops = [(0, 2), (0, 1), (0, 3)]
     else:
         parts, hops = ([mine], [(0, 0)])
         for bit in doublings(cols):
@@ -222,7 +227,10 @@
         cells = []
         for corner, (source, low) in enumerate(((3, 0), (1, 0), (1, PAD), (3, PAD))):
             near_id, near_corner, flag = (corner_links[i, tile, corner] for i in range(3))
-            pick = jnp.where(flag == 1, lax.rem(near_id, tiles) * 4 + near_corner, -1)
+            pick = lax.rem(near_id, tiles) * 4 + near_corner
+            if all(chosen):
+                pick, low = (pick + (0 if low else PAD // 2), 0)
+            pick = jnp.where(flag == 1, pick, -1)
             picker = one_hot(8, PAD, lambda n: pick)
             cells_at = tiles * edge if chosen[source] else strips + PAD
             cells.append(select(picker, near[source][cells_at + low : cells_at + low + PAD, :])[:1])
@@ -314,8 +322,12 @@
             else:
                 asked = near[side][tiles * 4 * edge + tiles * 4 : tiles * 4 * edge + PAD, :128]
             answer(out, bundle, asked, (side + 2) % 4, tiles, edge)
-            if side in (0, 2):
-                out[tiles * edge :, :] = bundle[tiles * 4 * edge :, :]
+            cells = bundle[tiles * 4 * edge :, :]
+            if side == 0:
+                out[tiles * edge :, :] = cells
+            if side == 2:
+                lower = one_hot(PAD, PAD, lambda n: n - PAD // 2)
+                out[tiles * edge :, :] = select(lower, cells).astype(jnp.bfloat16)
 
 
 def conv(field, near, links, bias, weight, chosen, pooling, notes=()):
@@ -356,10 +368,13 @@
     )
 
 
-def exchange(to_north, to_east, to_south, to_west):
+def exchange(to_north, to_east, to_south, to_west, name):
     north = shift(to_south, 1, 0)
     south = shift(to_north, -1, 0)
-    cells = [north[-PAD:], south[-PAD:]]
+    if name == "g":
+        cells = [north[-PAD:] + south[-PAD:]]
+    else:
+        cells = [north[-PAD:], south[-PAD:]]
     west = shift(jnp.concatenate([to_east, *cells], axis=0), 0, 1)
     east = shift(jnp.concatenate([to_west, *cells], axis=0), 0, -1)
     return north, east, south, west
@@ -401,12 +416,12 @@
         near = (north, shift(to_west, 0, -1), south, shift(to_east, 0, 1))
         chosen = (False, True, False, True)
     else:
-        near = exchange(bundle, bundle, bundle, bundle)
+        near = exchange(bundle, bundle, bundle, bundle, "h")
         chosen = (False,) * 4
     hidden, *strips = conv(
         tiles_in, near, links, first_bias, first, chosen, False, notes or ()
     )
-    near = exchange(*strips)
+    near = exchange(*strips, "g")
     return conv(hidden, near, links, second_bias, second, (True,) * 4, True)[0]
 
 

time: 78.4 us -> 82.4 us (1.051)
  starting transfers between devices: 27.3 us -> 31.7 us
  waiting for transfers between devices: 23.7 us -> 22.5 us
  local copies, waits for them, and re-layouts: 3.46 us -> 4.35 us
    ppermute x29 -> x30, starting transfers between devices: 27.3 us -> 31.7 us  [move(): return lax.ppermute(x, AXES, pairs)]
    ppermute x29 -> x30, waiting for transfers between devices: 23.7 us -> 22.5 us  [move(): return lax.ppermute(x, AXES, pairs)]
    unnamed x19 -> x20, local copies, waits for them, and re-layouts: 1.3 us -> 2.21 us
  transfers between devices with their start and end apart: 29 -> 30, of which waited for: 13 -> 10; matrix products, arithmetic and copies ran while one was open for 0% -> 1% of each run, Pallas kernels for 12% -> 11%
where the time goes in v4:
time: 82.4 us; the launch traced here: 82.1 us
  starting transfers between devices  31.7 us (38%)
  Pallas kernels  22.6 us (27%)
  waiting for transfers between devices  22.5 us (27%)
  local copies, waits for them, and re-layouts  4.35 us (5%)
    ppermute x30, starting transfers between devices, move(): return lax.ppermute(x, AXES, pairs)  31.7 us
    ppermute x30, waiting for transfers between devices, move(): return lax.ppermute(x, AXES, pairs)  22.5 us
    pallas_call x2, Pallas kernels, conv(): pl.pallas_call(functools.partial(conv_kernel, places, hops, chosen, pooli...  22 us
    unnamed x20, local copies, waits for them, and re-layouts  2.21 us
  transfers between devices with their start and end apart: 30, of which 10 were waited for; matrix products, arithmetic and copies ran while one was open for 1% of the time, Pallas kernels for 11%

profile of v4, /device:TPU:0, one launch (start us, length us, event | category | flops | bytes accessed | tf_op | source)
XLA Modules:
  0.0 82.1 jit_solution(4599146820447941775)
XLA Ops:
  0.0 0.7 slice_compare_fusion
  0.7 0.7 fusion.3
  1.4 0.1 ne.19
  1.5 0.1 xor.16
  1.6 0.1 squeeze.7
  1.6 0.1 squeeze.8
  1.8 0.9 %constant_dynamic-slice_fusion.1 = bf16[1,16,2304]{2,1,0:T(8,128)(2,1)S(1)} fusion(bf16[8,16,2304]{2,1,0:T(8,128)(2,1)} %bitcast.15, s32[]{:T(128)S(6)} %select_n.21), kind=kLoop, calls=%fused_computation.22 | loop fusion | bytes 147460 | tf_op jit(solution)/shard_map/jit(dynamic_index_in_dim)/dynamic_slice | solution.py:46
  2.7 0.1 broadcast_in_dim_broadcast_in_dim.2
  2.7 4.1 %collective-permute-start.6 = (bf16[1,16,2432]{2,1,0:T(8,128)(2,1)S(1)}, bf16[1,16,2432]{2,1,0:T(8,128)(2,1)}, u32[]{:S(2)}, u32[]{:S(2)}) collective-permute-start(bf16[1,16,2432]{2,1,0:T(8,128)(2,1)S(1)} %pad_maximum_fusion.2), channel_id=1, source_target_pairs={{0,2},{1,3},{2,0},{3,1},{4,6},{5,7},{6,4},{7,5},{8,10},{9,11},{10,... | collective-permute-start | bytes 233480 | tf_op jit(solution)/shard_map/ppermute | solution.py:23
  6.9 1.3 %collective-permute-start.2 = (bf16[1,16,2432]{2,1,0:T(8,128)(2,1)S(1)}, bf16[1,16,2432]{2,1,0:T(8,128)(2,1)S(1)}, u32[]{:S(2)}, u32[]{:S(2)}) collective-permute-start(bf16[1,16,2432]{2,1,0:T(8,128)(2,1)S(1)} %pad_maximum_fusion.2), channel_id=1, source_target_pairs={{0,3},{1,0},{2,1},{3,2},{4,7},{5,4},{6,5},{7,6},{8,11},{9,8},{10,9... | collective-permute-start | bytes 233480 | tf_op jit(solution)/shard_map/ppermute | solution.py:23
  8.2 0.7 collective-permute-start.1
  8.9 0.1 broadcast_in_dim.14.asked
  9.0 1.2 %copy-done = bf16[2,32,32,256]{3,2,1,0:T(8,128)(2,1)S(1)} copy-done((bf16[2,32,32,256]{3,2,1,0:T(8,128)(2,1)S(1)}, bf16[2,32,32,256]{3,2,1,0:T(8,128)(2,1)}, u32[]{:S(2)}) %copy-start) | copy-done | bytes 1048600
  10.2 0.4 borders.1.bundle
  10.6 0.0 copy-start.4
  10.6 0.0 copy-start.5
  10.6 0.0 copy-start.6
  10.6 1.1 %collective-permute-start.3 = (bf16[272,256]{1,0:T(8,128)(2,1)S(1)}, bf16[272,256]{1,0:T(8,128)(2,1)S(1)}, u32[]{:S(2)}, u32[]{:S(2)}) collective-permute-start(bf16[272,256]{1,0:T(8,128)(2,1)S(1)} %borders.1.bundle), channel_id=1, source_target_pairs={{0,28},{1,29},{2,30},{3,31},{4,0},{5,1},{6,2},{7,3},{8,4},{9,5},{1... | collective-permute-start | bytes 417800 | tf_op jit(solution)/shard_map/ppermute | solution.py:23
  11.8 0.1 pad_add_fusion.refs_0_
  11.8 2.6 %collective-permute-done.1.from_west.refs_18_ = bf16[1,16,2432]{2,1,0:T(8,128)(2,1)S(1)} collective-permute-done((bf16[1,16,2432]{2,1,0:T(8,128)(2,1)S(1)}, bf16[1,16,2432]{2,1,0:T(8,128)(2,1)S(1)}, u32[]{:S(2)}, u32[]{:S(2)}) %collective-permute-start.1) | collective-permute-done | bytes 77856 | tf_op jit(solution)/shard_map/ppermute | solution.py:23
  14.4 0.5 collective-permute-start.19
  15.0 0.0 collective-permute-done.6
  15.0 2.2 %collective-permute-start.18 = (bf16[1,16,4608]{2,1,0:T(8,128)(2,1)S(1)}, bf16[1,16,4608]{2,1,0:T(8,128)(2,1)S(1)}, u32[]{:S(2)}, u32[]{:S(2)}) collective-permute-start(bf16[1,16,4608]{2,1,0:T(8,128)(2,1)S(1)} %constant_dynamic-slice_fusion), channel_id=1, source_target_pairs={{0,2},{1,3},{2,0},{3,1},{4,6},{5,7},{6,4},{7,5},{8,10},{9,11},{10,... | collective-permute-start | bytes 442376 | tf_op jit(solution)/shard_map/ppermute | solution.py:23
  17.1 0.9 %constant_dynamic-update-slice_fusion.1 = bf16[3,16,2432]{2,1,0:T(8,128)(2,1)S(1)} fusion(bf16[3,16,2432]{2,1,0:T(8,128)(2,1)S(1)} %constant_dynamic-update-slice_fusion.2, bf16[1,16,2432]{2,1,0:T(8,128)(2,1)} %collective-permute-done.6), kind=kLoop, calls=%fused_computation.5 | loop fusion | bytes 155648
  18.0 2.5 %collective-permute-start.9 = (bf16[3,16,2432]{2,1,0:T(8,128)(2,1)S(1)}, bf16[3,16,2432]{2,1,0:T(8,128)(2,1)S(1)}, u32[]{:S(2)}, u32[]{:S(2)}) collective-permute-start(bf16[3,16,2432]{2,1,0:T(8,128)(2,1)S(1)} %constant_dynamic-update-slice_fusion.refs_10_), channel_id=1, source_target_pairs={{0,24},{1,25},{2,26},{3,27},{4,28},{5,29},{6,30},{7,31},{8,16},{9,... | collective-permute-start | bytes 700424 | tf_op jit(solution)/shard_map/ppermute | solution.py:23
  20.5 0.0 collective-permute-done.3.south.refs_6_
  20.5 0.5 collective-permute-start.8
  21.0 0.0 collective-permute-done.north.refs_4_
  21.1 0.5 collective-permute-start.7
  21.6 0.2 replies.1
  21.8 0.0 collective-permute-done.18
  21.8 5.9 %collective-permute-start.4 = (bf16[96,256]{1,0:T(8,128)(2,1)S(1)}, bf16[96,256]{1,0:T(8,128)(2,1)S(1)}, u32[]{:S(2)}, u32[]{:S(2)}) collective-permute-start(bf16[96,256]{1,0:T(8,128)(2,1)S(1)} %get-tuple-element.12), channel_id=1, source_target_pairs={{0,3},{1,0},{2,1},{3,2},{4,7},{5,4},{6,5},{7,6},{8,11},{9,8},{10,9... | collective-permute-start | bytes 147464 | tf_op jit(solution)/shard_map/ppermute | solution.py:23
  27.7 0.1 collective-permute-start.10
  27.8 1.9 %collective-permute-done.4.refs_5_ = bf16[96,256]{1,0:T(8,128)(2,1)S(1)} collective-permute-done((bf16[96,256]{1,0:T(8,128)(2,1)S(1)}, bf16[96,256]{1,0:T(8,128)(2,1)S(1)}, u32[]{:S(2)}, u32[]{:S(2)}) %collective-permute-start.4) | collective-permute-done | bytes 49184 | tf_op jit(solution)/shard_map/ppermute | solution.py:23
  29.7 0.0 collective-permute-start.5
  29.8 0.0 collective-permute-done.9.refs_13_
  29.8 0.0 collective-permute-start.13
  29.8 1.3 %collective-permute-done.8.refs_12_ = bf16[3,16,2432]{2,1,0:T(8,128)(2,1)S(1)} collective-permute-done((bf16[3,16,2432]{2,1,0:T(8,128)(2,1)S(1)}, bf16[3,16,2432]{2,1,0:T(8,128)(2,1)S(1)}, u32[]{:S(2)}, u32[]{:S(2)}) %collective-permute-start.8) | collective-permute-done | bytes 233504 | tf_op jit(solution)/shard_map/ppermute | solution.py:23
  31.0 0.0 collective-permute-start.12
  31.0 0.1 collective-permute-done.7.refs_11_
  31.1 0.4 collective-permute-start.11
  31.5 4.6 %collective-permute-done.5.refs_7_ = bf16[96,256]{1,0:T(8,128)(2,1)S(1)} collective-permute-done((bf16[96,256]{1,0:T(8,128)(2,1)S(1)}, bf16[96,256]{1,0:T(8,128)(2,1)S(1)}, u32[]{:S(2)}, u32[]{:S(2)}) %collective-permute-start.5) | collective-permute-done | bytes 49184 | tf_op jit(solution)/shard_map/ppermute | solution.py:23
  36.1 0.0 collective-permute-start.20
  36.1 0.0 collective-permute-done.10.refs_14_
  36.2 0.0 collective-permute-done.11.refs_15_
  36.2 8.5 %first.1 = (bf16[2,32,32,512]{3,2,1,0:T(8,128)(2,1)S(1)}, bf16[80,512]{1,0:T(8,128)(2,1)S(1)}, bf16[64,512]{1,0:T(8,128)(2,1)S(1)}, bf16[80,512]{1,0:T(8,128)(2,1)S(1)}, bf16[64,512]{1,0:T(8,128)(2,1)S(1)}) custom-call(s32[2]{0:T(128)S(1)} %pad_add_fusion.refs_0_, s32[3,2,4]{2,1,0:T(2,128)S(1)} %bitcast.16, s32[3,2,4]{2,1,0:T(2,128)S(1)} %bitcast.18, ...), custom_call_target="tpu_custom_call" | custom-call | flops 4831838208 | bytes 8388608 | tf_op jit(solution)/shard_map/first/pallas_call | solution.py:346
  44.7 0.0 copy-start.7
  44.7 0.1 collective-permute-start.14
  44.8 2.6 %collective-permute-start.15 = (bf16[80,512]{1,0:T(8,128)(2,1)S(1)}, bf16[80,512]{1,0:T(8,128)(2,1)S(1)}, u32[]{:S(2)}, u32[]{:S(2)}) collective-permute-start(bf16[80,512]{1,0:T(8,128)(2,1)S(1)} %get-tuple-element.17), channel_id=1, source_target_pairs={{0,28},{1,29},{2,30},{3,31},{4,0},{5,1},{6,2},{7,3},{8,4},{9,5},{1... | collective-permute-start | bytes 245768 | tf_op jit(solution)/shard_map/ppermute | solution.py:23
  47.4 0.0 collective-permute-done.20
  47.4 1.6 %collective-permute-start.22 = (bf16[3,16,4608]{2,1,0:T(8,128)(2,1)S(1)}, bf16[3,16,4608]{2,1,0:T(8,128)(2,1)S(1)}, u32[]{:S(2)}, u32[]{:S(2)}) collective-permute-start(bf16[3,16,4608]{2,1,0:T(8,128)(2,1)S(1)} %constant_dynamic-update-slice_fusion.3.refs_10_), channel_id=1, source_target_pairs={{0,16},{1,17},{2,18},{3,19},{4,20},{5,21},{6,22},{7,23},{8,24},{9,... | collective-permute-start | bytes 1327112 | tf_op jit(solution)/shard_map/ppermute | solution.py:23
  49.0 0.6 collective-permute-start.21
  49.6 0.0 collective-permute-done.14.refs_4_
  49.6 0.6 collective-permute-done.15.refs_6_
  50.3 2.1 %collective-permute-start.17 = (bf16[80,512]{1,0:T(8,128)(2,1)S(1)}, bf16[80,512]{1,0:T(8,128)(2,1)S(1)}, u32[]{:S(2)}, u32[]{:S(2)}) collective-permute-start(bf16[80,512]{1,0:T(8,128)(2,1)S(1)} %get-tuple-element.19), channel_id=1, source_target_pairs={{0,1},{1,2},{2,3},{3,0},{4,5},{5,6},{6,7},{7,4},{8,9},{9,10},{10,1... | collective-permute-start | bytes 245768 | tf_op jit(solution)/shard_map/ppermute | solution.py:23
  52.3 1.8 %collective-permute-start.16 = (bf16[80,512]{1,0:T(8,128)(2,1)S(1)}, bf16[80,512]{1,0:T(8,128)(2,1)S(1)}, u32[]{:S(2)}, u32[]{:S(2)}) collective-permute-start(bf16[80,512]{1,0:T(8,128)(2,1)S(1)} %get-tuple-element.20), channel_id=1, source_target_pairs={{0,3},{1,0},{2,1},{3,2},{4,7},{5,4},{6,5},{7,6},{8,11},{9,8},{10,9... | collective-permute-start | bytes 245768 | tf_op jit(solution)/shard_map/ppermute | solution.py:23
  54.1 4.9 %collective-permute-done.22.refs_12_ = bf16[3,16,4608]{2,1,0:T(8,128)(2,1)S(1)} collective-permute-done((bf16[3,16,4608]{2,1,0:T(8,128)(2,1)S(1)}, bf16[3,16,4608]{2,1,0:T(8,128)(2,1)S(1)}, u32[]{:S(2)}, u32[]{:S(2)}) %collective-permute-start.22) | collective-permute-done | bytes 442400 | tf_op jit(solution)/shard_map/ppermute | solution.py:23
  59.0 2.0 %collective-permute-start.24 = (bf16[3,16,2304]{2,1,0:T(8,128)(2,1)S(1)}, bf16[3,16,2304]{2,1,0:T(8,128)(2,1)S(1)}, u32[]{:S(2)}, u32[]{:S(2)}) collective-permute-start(bf16[3,16,2304]{2,1,0:T(8,128)(2,1)S(1)} %slice.31), channel_id=1, source_target_pairs={{0,8},{1,9},{2,10},{3,11},{4,12},{5,13},{6,14},{7,15},{8,0},{9,1},... | collective-permute-start | bytes 663560 | tf_op jit(solution)/shard_map/ppermute | solution.py:23
  61.0 0.6 collective-permute-start.23
  61.6 0.5 collective-permute-start.26
  62.1 3.5 %collective-permute-done.24.refs_14_ = bf16[3,16,2304]{2,1,0:T(8,128)(2,1)S(1)} collective-permute-done((bf16[3,16,2304]{2,1,0:T(8,128)(2,1)S(1)}, bf16[3,16,2304]{2,1,0:T(8,128)(2,1)S(1)}, u32[]{:S(2)}, u32[]{:S(2)}) %collective-permute-start.24) | collective-permute-done | bytes 221216 | tf_op jit(solution)/shard_map/ppermute | solution.py:23
  65.6 1.5 %collective-permute-done.23.refs_13_ = bf16[3,16,2304]{2,1,0:T(8,128)(2,1)S(1)} collective-permute-done((bf16[3,16,2304]{2,1,0:T(8,128)(2,1)S(1)}, bf16[3,16,2304]{2,1,0:T(8,128)(2,1)S(1)}, u32[]{:S(2)}, u32[]{:S(2)}) %collective-permute-start.23) | collective-permute-done | bytes 221216 | tf_op jit(solution)/shard_map/ppermute | solution.py:23
  67.1 1.5 %collective-permute-done.28.refs_18_ = bf16[3,16,2304]{2,1,0:T(8,128)(2,1)S(1)} collective-permute-done((bf16[3,16,2304]{2,1,0:T(8,128)(2,1)S(1)}, bf16[3,16,2304]{2,1,0:T(8,128)(2,1)S(1)}, u32[]{:S(2)}, u32[]{:S(2)}) %collective-permute-start.28) | collective-permute-done | bytes 221216 | tf_op jit(solution)/shard_map/ppermute | solution.py:23
  68.6 13.5 %second.1 = bf16[2,16,16,512]{3,2,1,0:T(8,128)(2,1)} custom-call(s32[2]{0:T(128)S(1)} %pad_add_fusion.refs_0_, s32[3,2,4]{2,1,0:T(2,128)S(1)} %bitcast.17, s32[3,2,4]{2,1,0:T(2,128)S(1)} %bitcast.19, bf16[2,32,32,512]{3,2,1,0:T(8,128)(2,1)S(1)} %get-tuple-element.14.refs_3_, bf16[80,512]{1,0:T(8,128)(2,1)S(1)} %collective-permute-done.14.refs_4_, ...), custom_call_target="tpu_custom_call" | custom-call | flops 9663676416 | bytes 8388608 | tf_op jit(solution)/shard_map/second/pallas_call | solution.py:346
  (42 shorter events, 0.2 us)
Async XLA Ops:
  2.7 12.2 %collective-permute-start.6 = (bf16[1,16,2432]{2,1,0:T(8,128)(2,1)S(1)}, bf16[1,16,2432]{2,1,0:T(8,128)(2,1)}, u32[]{:S(2)}, u32[]{:S(2)}) collective-permute-start(bf16[1,16,2432]{2,1,0:T(8,128)(2,1)S(1)} %pad_maximum_fusion.2), channel_id=1, source_target_pairs={{0,2},{1,3},{2,0},{3,1},{4,6},{5,7},{6,4},{7,5},{8,10},{9,11},{10,... | collective-permute-start | bytes 233480 | tf_op jit(solution)/shard_map/ppermute | solution.py:23
  6.9 11.1 %collective-permute-start.2 = (bf16[1,16,2432]{2,1,0:T(8,128)(2,1)S(1)}, bf16[1,16,2432]{2,1,0:T(8,128)(2,1)S(1)}, u32[]{:S(2)}, u32[]{:S(2)}) collective-permute-start(bf16[1,16,2432]{2,1,0:T(8,128)(2,1)S(1)} %pad_maximum_fusion.2), channel_id=1, source_target_pairs={{0,3},{1,0},{2,1},{3,2},{4,7},{5,4},{6,5},{7,6},{8,11},{9,8},{10,9... | collective-permute-start | bytes 233480 | tf_op jit(solution)/shard_map/ppermute | solution.py:23
  8.2 6.2 %collective-permute-start.1 = (bf16[1,16,2432]{2,1,0:T(8,128)(2,1)S(1)}, bf16[1,16,2432]{2,1,0:T(8,128)(2,1)S(1)}, u32[]{:S(2)}, u32[]{:S(2)}) collective-permute-start(bf16[1,16,2432]{2,1,0:T(8,128)(2,1)S(1)} %pad_maximum_fusion.2), channel_id=1, source_target_pairs={{0,1},{1,2},{2,3},{3,0},{4,5},{5,6},{6,7},{7,4},{8,9},{9,10},{10,1... | collective-permute-start | bytes 233480 | tf_op jit(solution)/shard_map/ppermute | solution.py:23
  9.0 1.2 %copy-start = (bf16[2,32,32,256]{3,2,1,0:T(8,128)(2,1)S(1)}, bf16[2,32,32,256]{3,2,1,0:T(8,128)(2,1)}, u32[]{:S(2)}) copy-start(bf16[2,32,32,256]{3,2,1,0:T(8,128)(2,1)} %refs_3_.1) | copy-start | bytes 3145732
  10.2 1.6 %copy-start.2 = (bf16[128,4608]{1,0:T(8,128)(2,1)S(1)}, bf16[128,4608]{1,0:T(8,128)(2,1)}, u32[]{:S(2)}) copy-start(bf16[128,4608]{1,0:T(8,128)(2,1)} %refs_9_.3) | copy-start | bytes 3538948
  10.6 25.6 %copy-start.1 = (bf16[2,32,32,256]{3,2,1,0:T(8,128)(2,1)S(1)}, bf16[2,32,32,256]{3,2,1,0:T(8,128)(2,1)}, u32[]{:S(2)}) copy-start(bf16[2,32,32,256]{3,2,1,0:T(8,128)(2,1)} %refs_3_.1) | copy-start | bytes 3145732
  10.6 25.6 %copy-start.3 = (bf16[128,2304]{1,0:T(8,128)(2,1)S(1)}, bf16[128,2304]{1,0:T(8,128)(2,1)}, u32[]{:S(2)}) copy-start(bf16[128,2304]{1,0:T(8,128)(2,1)} %refs_9_.2) | copy-start | bytes 1769476
  10.6 25.6 %copy-start.4 = (s32[2,4,3]{1,0,2:T(2,128)S(1)}, s32[2,4,3]{1,0,2:T(2,128)}, u32[]{:S(2)}) copy-start(s32[2,4,3]{1,0,2:T(2,128)} %param.12) | copy-start | bytes 292
  10.6 25.6 %copy-start.5 = (s32[2,4,3]{1,0,2:T(2,128)S(1)}, s32[2,4,3]{1,0,2:T(2,128)}, u32[]{:S(2)}) copy-start(s32[2,4,3]{1,0,2:T(2,128)} %param.13) | copy-start | bytes 292
  10.6 25.6 %copy-start.6 = (f32[512]{0:T(512)S(1)}, f32[512]{0:T(512)}, u32[]{:S(2)}) copy-start(f32[512]{0:T(512)} %param.9) | copy-start | bytes 6148
  10.6 9.9 %collective-permute-start.3 = (bf16[272,256]{1,0:T(8,128)(2,1)S(1)}, bf16[272,256]{1,0:T(8,128)(2,1)S(1)}, u32[]{:S(2)}, u32[]{:S(2)}) collective-permute-start(bf16[272,256]{1,0:T(8,128)(2,1)S(1)} %borders.1.bundle), channel_id=1, source_target_pairs={{0,28},{1,29},{2,30},{3,31},{4,0},{5,1},{6,2},{7,3},{8,4},{9,5},{1... | collective-permute-start | bytes 417800 | tf_op jit(solution)/shard_map/ppermute | solution.py:23
  11.7 9.3 %collective-permute-start = (bf16[272,256]{1,0:T(8,128)(2,1)S(1)}, bf16[272,256]{1,0:T(8,128)(2,1)S(1)}, u32[]{:S(2)}, u32[]{:S(2)}) collective-permute-start(bf16[272,256]{1,0:T(8,128)(2,1)S(1)} %borders.1.bundle), channel_id=1, source_target_pairs={{0,4},{1,5},{2,6},{3,7},{4,8},{5,9},{6,10},{7,11},{8,12},{9,13},{1... | collective-permute-start | bytes 417800 | tf_op jit(solution)/shard_map/ppermute | solution.py:23
  14.4 13.3 %collective-permute-start.19 = (bf16[1,16,4608]{2,1,0:T(8,128)(2,1)S(1)}, bf16[1,16,4608]{2,1,0:T(8,128)(2,1)S(1)}, u32[]{:S(2)}, u32[]{:S(2)}) collective-permute-start(bf16[1,16,4608]{2,1,0:T(8,128)(2,1)S(1)} %constant_dynamic-slice_fusion), channel_id=1, source_target_pairs={{0,1},{1,0},{2,3},{3,2},{4,5},{5,4},{6,7},{7,6},{8,9},{9,8},{10,11... | collective-permute-start | bytes 442376 | tf_op jit(solution)/shard_map/ppermute | solution.py:23
  15.0 6.8 %collective-permute-start.18 = (bf16[1,16,4608]{2,1,0:T(8,128)(2,1)S(1)}, bf16[1,16,4608]{2,1,0:T(8,128)(2,1)S(1)}, u32[]{:S(2)}, u32[]{:S(2)}) collective-permute-start(bf16[1,16,4608]{2,1,0:T(8,128)(2,1)S(1)} %constant_dynamic-slice_fusion), channel_id=1, source_target_pairs={{0,2},{1,3},{2,0},{3,1},{4,6},{5,7},{6,4},{7,5},{8,10},{9,11},{10,... | collective-permute-start | bytes 442376 | tf_op jit(solution)/shard_map/ppermute | solution.py:23
  18.0 11.7 %collective-permute-start.9 = (bf16[3,16,2432]{2,1,0:T(8,128)(2,1)S(1)}, bf16[3,16,2432]{2,1,0:T(8,128)(2,1)S(1)}, u32[]{:S(2)}, u32[]{:S(2)}) collective-permute-start(bf16[3,16,2432]{2,1,0:T(8,128)(2,1)S(1)} %constant_dynamic-update-slice_fusion.refs_10_), channel_id=1, source_target_pairs={{0,24},{1,25},{2,26},{3,27},{4,28},{5,29},{6,30},{7,31},{8,16},{9,... | collective-permute-start | bytes 700424 | tf_op jit(solution)/shard_map/ppermute | solution.py:23
  20.5 10.5 %collective-permute-start.8 = (bf16[3,16,2432]{2,1,0:T(8,128)(2,1)S(1)}, bf16[3,16,2432]{2,1,0:T(8,128)(2,1)S(1)}, u32[]{:S(2)}, u32[]{:S(2)}) collective-permute-start(bf16[3,16,2432]{2,1,0:T(8,128)(2,1)S(1)} %constant_dynamic-update-slice_fusion.refs_10_), channel_id=1, source_target_pairs={{0,16},{1,17},{2,18},{3,19},{4,20},{5,21},{6,22},{7,23},{8,24},{9,... | collective-permute-start | bytes 700424 | tf_op jit(solution)/shard_map/ppermute | solution.py:23
  21.1 10.1 %collective-permute-start.7 = (bf16[3,16,2432]{2,1,0:T(8,128)(2,1)S(1)}, bf16[3,16,2432]{2,1,0:T(8,128)(2,1)S(1)}, u32[]{:S(2)}, u32[]{:S(2)}) collective-permute-start(bf16[3,16,2432]{2,1,0:T(8,128)(2,1)S(1)} %constant_dynamic-update-slice_fusion.refs_10_), channel_id=1, source_target_pairs={{0,8},{1,9},{2,10},{3,11},{4,12},{5,13},{6,14},{7,15},{8,0},{9,1},... | collective-permute-start | bytes 700424 | tf_op jit(solution)/shard_map/ppermute | solution.py:23
  21.8 7.9 %collective-permute-start.4 = (bf16[96,256]{1,0:T(8,128)(2,1)S(1)}, bf16[96,256]{1,0:T(8,128)(2,1)S(1)}, u32[]{:S(2)}, u32[]{:S(2)}) collective-permute-start(bf16[96,256]{1,0:T(8,128)(2,1)S(1)} %get-tuple-element.12), channel_id=1, source_target_pairs={{0,3},{1,0},{2,1},{3,2},{4,7},{5,4},{6,5},{7,6},{8,11},{9,8},{10,9... | collective-permute-start | bytes 147464 | tf_op jit(solution)/shard_map/ppermute | solution.py:23
  27.7 8.4 %collective-permute-start.10 = (bf16[3,16,2432]{2,1,0:T(8,128)(2,1)S(1)}, bf16[3,16,2432]{2,1,0:T(8,128)(2,1)S(1)}, u32[]{:S(2)}, u32[]{:S(2)}) collective-permute-start(bf16[3,16,2432]{2,1,0:T(8,128)(2,1)S(1)} %constant_dynamic-update-slice_fusion.refs_10_), channel_id=1, source_target_pairs={{0,4},{1,5},{2,6},{3,7},{4,0},{5,1},{6,2},{7,3},{8,12},{9,13},{10,... | collective-permute-start | bytes 700424 | tf_op jit(solution)/shard_map/ppermute | solution.py:23
  29.7 6.4 %collective-permute-start.5 = (bf16[96,256]{1,0:T(8,128)(2,1)S(1)}, bf16[96,256]{1,0:T(8,128)(2,1)S(1)}, u32[]{:S(2)}, u32[]{:S(2)}) collective-permute-start(bf16[96,256]{1,0:T(8,128)(2,1)S(1)} %get-tuple-element.13), channel_id=1, source_target_pairs={{0,1},{1,2},{2,3},{3,0},{4,5},{5,6},{6,7},{7,4},{8,9},{9,10},{10,1... | collective-permute-start | bytes 147464 | tf_op jit(solution)/shard_map/ppermute | solution.py:23
  29.8 6.4 %collective-permute-start.13 = (bf16[3,16,2432]{2,1,0:T(8,128)(2,1)S(1)}, bf16[3,16,2432]{2,1,0:T(8,128)(2,1)S(1)}, u32[]{:S(2)}, u32[]{:S(2)}) collective-permute-start(bf16[3,16,2432]{2,1,0:T(8,128)(2,1)S(1)} %collective-permute-done.9.refs_13_), channel_id=1, source_target_pairs={{0,4},{1,5},{2,6},{3,7},{4,0},{5,1},{6,2},{7,3},{8,12},{9,13},{10,... | collective-permute-start | bytes 700424 | tf_op jit(solution)/shard_map/ppermute | solution.py:23
  31.0 5.1 %collective-permute-start.12 = (bf16[3,16,2432]{2,1,0:T(8,128)(2,1)S(1)}, bf16[3,16,2432]{2,1,0:T(8,128)(2,1)S(1)}, u32[]{:S(2)}, u32[]{:S(2)}) collective-permute-start(bf16[3,16,2432]{2,1,0:T(8,128)(2,1)S(1)} %collective-permute-done.8.refs_12_), channel_id=1, source_target_pairs={{0,4},{1,5},{2,6},{3,7},{4,0},{5,1},{6,2},{7,3},{8,12},{9,13},{10,... | collective-permute-start | bytes 700424 | tf_op jit(solution)/shard_map/ppermute | solution.py:23
  31.1 5.0 %collective-permute-start.11 = (bf16[3,16,2432]{2,1,0:T(8,128)(2,1)S(1)}, bf16[3,16,2432]{2,1,0:T(8,128)(2,1)S(1)}, u32[]{:S(2)}, u32[]{:S(2)}) collective-permute-start(bf16[3,16,2432]{2,1,0:T(8,128)(2,1)S(1)} %collective-permute-done.7.refs_11_), channel_id=1, source_target_pairs={{0,4},{1,5},{2,6},{3,7},{4,0},{5,1},{6,2},{7,3},{8,12},{9,13},{10,... | collective-permute-start | bytes 700424 | tf_op jit(solution)/shard_map/ppermute | solution.py:23
  36.1 11.3 %collective-permute-start.20 = (bf16[1,16,4608]{2,1,0:T(8,128)(2,1)S(1)}, bf16[1,16,4608]{2,1,0:T(8,128)(2,1)S(1)}, u32[]{:S(2)}, u32[]{:S(2)}) collective-permute-start(bf16[1,16,4608]{2,1,0:T(8,128)(2,1)S(1)} %collective-permute-done.18), channel_id=1, source_target_pairs={{0,1},{1,0},{2,3},{3,2},{4,5},{5,4},{6,7},{7,6},{8,9},{9,8},{10,11... | collective-permute-start | bytes 442376 | tf_op jit(solution)/shard_map/ppermute | solution.py:23
  44.7 23.9 %copy-start.7 = (f32[512]{0:T(512)S(1)}, f32[512]{0:T(512)}, u32[]{:S(2)}) copy-start(f32[512]{0:T(512)} %param.11) | copy-start | bytes 6148
  44.7 4.9 %collective-permute-start.14 = (bf16[80,512]{1,0:T(8,128)(2,1)S(1)}, bf16[80,512]{1,0:T(8,128)(2,1)S(1)}, u32[]{:S(2)}, u32[]{:S(2)}) collective-permute-start(bf16[80,512]{1,0:T(8,128)(2,1)S(1)} %get-tuple-element.15), channel_id=1, source_target_pairs={{0,4},{1,5},{2,6},{3,7},{4,8},{5,9},{6,10},{7,11},{8,12},{9,13},{1... | collective-permute-start | bytes 245768 | tf_op jit(solution)/shard_map/ppermute | solution.py:23
  44.8 5.5 %collective-permute-start.15 = (bf16[80,512]{1,0:T(8,128)(2,1)S(1)}, bf16[80,512]{1,0:T(8,128)(2,1)S(1)}, u32[]{:S(2)}, u32[]{:S(2)}) collective-permute-start(bf16[80,512]{1,0:T(8,128)(2,1)S(1)} %get-tuple-element.17), channel_id=1, source_target_pairs={{0,28},{1,29},{2,30},{3,31},{4,0},{5,1},{6,2},{7,3},{8,4},{9,5},{1... | collective-permute-start | bytes 245768 | tf_op jit(solution)/shard_map/ppermute | solution.py:23
  47.4 11.6 %collective-permute-start.22 = (bf16[3,16,4608]{2,1,0:T(8,128)(2,1)S(1)}, bf16[3,16,4608]{2,1,0:T(8,128)(2,1)S(1)}, u32[]{:S(2)}, u32[]{:S(2)}) collective-permute-start(bf16[3,16,4608]{2,1,0:T(8,128)(2,1)S(1)} %constant_dynamic-update-slice_fusion.3.refs_10_), channel_id=1, source_target_pairs={{0,16},{1,17},{2,18},{3,19},{4,20},{5,21},{6,22},{7,23},{8,24},{9,... | collective-permute-start | bytes 1327112 | tf_op jit(solution)/shard_map/ppermute | solution.py:23
  49.0 12.0 %collective-permute-start.21 = (bf16[3,16,4608]{2,1,0:T(8,128)(2,1)S(1)}, bf16[3,16,4608]{2,1,0:T(8,128)(2,1)S(1)}, u32[]{:S(2)}, u32[]{:S(2)}) collective-permute-start(bf16[3,16,4608]{2,1,0:T(8,128)(2,1)S(1)} %constant_dynamic-update-slice_fusion.3.refs_10_), channel_id=1, source_target_pairs={{0,8},{1,9},{2,10},{3,11},{4,12},{5,13},{6,14},{7,15},{8,0},{9,1},... | collective-permute-start | bytes 1327112 | tf_op jit(solution)/shard_map/ppermute | solution.py:23
  50.3 11.3 %collective-permute-start.17 = (bf16[80,512]{1,0:T(8,128)(2,1)S(1)}, bf16[80,512]{1,0:T(8,128)(2,1)S(1)}, u32[]{:S(2)}, u32[]{:S(2)}) collective-permute-start(bf16[80,512]{1,0:T(8,128)(2,1)S(1)} %get-tuple-element.19), channel_id=1, source_target_pairs={{0,1},{1,2},{2,3},{3,0},{4,5},{5,6},{6,7},{7,4},{8,9},{9,10},{10,1... | collective-permute-start | bytes 245768 | tf_op jit(solution)/shard_map/ppermute | solution.py:23
  52.3 9.3 %collective-permute-start.16 = (bf16[80,512]{1,0:T(8,128)(2,1)S(1)}, bf16[80,512]{1,0:T(8,128)(2,1)S(1)}, u32[]{:S(2)}, u32[]{:S(2)}) collective-permute-start(bf16[80,512]{1,0:T(8,128)(2,1)S(1)} %get-tuple-element.20), channel_id=1, source_target_pairs={{0,3},{1,0},{2,1},{3,2},{4,7},{5,4},{6,5},{7,6},{8,11},{9,8},{10,9... | collective-permute-start | bytes 245768 | tf_op jit(solution)/shard_map/ppermute | solution.py:23
  54.1 13.0 %collective-permute-start.25 = (bf16[3,16,4608]{2,1,0:T(8,128)(2,1)S(1)}, bf16[3,16,4608]{2,1,0:T(8,128)(2,1)S(1)}, u32[]{:S(2)}, u32[]{:S(2)}) collective-permute-start(bf16[3,16,4608]{2,1,0:T(8,128)(2,1)S(1)} %constant_dynamic-update-slice_fusion.3.refs_10_), channel_id=1, source_target_pairs={{0,4},{1,5},{2,6},{3,7},{4,0},{5,1},{6,2},{7,3},{8,12},{9,13},{10,... | collective-permute-start | bytes 1327112 | tf_op jit(solution)/shard_map/ppermute | solution.py:23
  59.0 6.5 %collective-permute-start.24 = (bf16[3,16,2304]{2,1,0:T(8,128)(2,1)S(1)}, bf16[3,16,2304]{2,1,0:T(8,128)(2,1)S(1)}, u32[]{:S(2)}, u32[]{:S(2)}) collective-permute-start(bf16[3,16,2304]{2,1,0:T(8,128)(2,1)S(1)} %slice.31), channel_id=1, source_target_pairs={{0,8},{1,9},{2,10},{3,11},{4,12},{5,13},{6,14},{7,15},{8,0},{9,1},... | collective-permute-start | bytes 663560 | tf_op jit(solution)/shard_map/ppermute | solution.py:23
  61.0 6.1 %collective-permute-start.23 = (bf16[3,16,2304]{2,1,0:T(8,128)(2,1)S(1)}, bf16[3,16,2304]{2,1,0:T(8,128)(2,1)S(1)}, u32[]{:S(2)}, u32[]{:S(2)}) collective-permute-start(bf16[3,16,2304]{2,1,0:T(8,128)(2,1)S(1)} %slice.30), channel_id=1, source_target_pairs={{0,16},{1,17},{2,18},{3,19},{4,20},{5,21},{6,22},{7,23},{8,24},{9,... | collective-permute-start | bytes 663560 | tf_op jit(solution)/shard_map/ppermute | solution.py:23
  61.6 5.6 %collective-permute-start.27 = (bf16[3,16,4608]{2,1,0:T(8,128)(2,1)S(1)}, bf16[3,16,4608]{2,1,0:T(8,128)(2,1)S(1)}, u32[]{:S(2)}, u32[]{:S(2)}) collective-permute-start(bf16[3,16,4608]{2,1,0:T(8,128)(2,1)S(1)} %collective-permute-done.22.refs_12_), channel_id=1, source_target_pairs={{0,4},{1,5},{2,6},{3,7},{4,0},{5,1},{6,2},{7,3},{8,12},{9,13},{10,... | collective-permute-start | bytes 1327112 | tf_op jit(solution)/shard_map/ppermute | solution.py:23
  61.6 7.0 %collective-permute-start.26 = (bf16[3,16,4608]{2,1,0:T(8,128)(2,1)S(1)}, bf16[3,16,4608]{2,1,0:T(8,128)(2,1)S(1)}, u32[]{:S(2)}, u32[]{:S(2)}) collective-permute-start(bf16[3,16,4608]{2,1,0:T(8,128)(2,1)S(1)} %collective-permute-done.21.refs_11_), channel_id=1, source_target_pairs={{0,4},{1,5},{2,6},{3,7},{4,0},{5,1},{6,2},{7,3},{8,12},{9,13},{10,... | collective-permute-start | bytes 1327112 | tf_op jit(solution)/shard_map/ppermute | solution.py:23
  65.6 1.6 %collective-permute-start.29 = (bf16[3,16,2304]{2,1,0:T(8,128)(2,1)S(1)}, bf16[3,16,2304]{2,1,0:T(8,128)(2,1)S(1)}, u32[]{:S(2)}, u32[]{:S(2)}) collective-permute-start(bf16[3,16,2304]{2,1,0:T(8,128)(2,1)S(1)} %collective-permute-done.24.refs_14_), channel_id=1, source_target_pairs={{0,4},{1,5},{2,6},{3,7},{4,0},{5,1},{6,2},{7,3},{8,12},{9,13},{10,... | collective-permute-start | bytes 663560 | tf_op jit(solution)/shard_map/ppermute | solution.py:23
  67.1 1.5 %collective-permute-start.28 = (bf16[3,16,2304]{2,1,0:T(8,128)(2,1)S(1)}, bf16[3,16,2304]{2,1,0:T(8,128)(2,1)S(1)}, u32[]{:S(2)}, u32[]{:S(2)}) collective-permute-start(bf16[3,16,2304]{2,1,0:T(8,128)(2,1)S(1)} %collective-permute-done.23.refs_13_), channel_id=1, source_target_pairs={{0,4},{1,5},{2,6},{3,7},{4,0},{5,1},{6,2},{7,3},{8,12},{9,13},{10,... | collective-permute-start | bytes 663560 | tf_op jit(solution)/shard_map/ppermute | solution.py:23
